TPU v7x, 128 devices: a whole 4x4x4 slice. The times are simulated.
128 devices in a mesh: seg: 4 (over z_lo, core), batch: 32 (over z_hi, y, x).
Axes of the slice: x: 4, y: 4, z: 4 (z_hi: 2, z_lo: 2; z = z_hi * 2 + z_lo), core: 2. Of those that a mesh axis runs over, the one named last changes fastest.
Arguments:
- starts: float32 [4, 4096, 1024], P('seg', 'batch'), may hold values from -6 to 6
- targets: float32 [4, 4096, 1024], P('seg', 'batch'), may hold values from -6 to 6
- counts: int32 [4], P('seg'), may hold values from 1 to 3, as said below
- w_in: bfloat16 [1024, 1024], P('batch'), may hold values from -0.1875 to 0.1875
- b_in: float32 [1024], replicated, may hold values from -3 to 3
- w_out: bfloat16 [1024, 1024], P('batch'), may hold values from -0.1875 to 0.1875
Outputs:
- grad_starts: float32 [4, 4096, 1024], P('seg', 'batch')
- grad_w_in: float32 [1024, 1024], P('batch')
- grad_w_out: float32 [1024, 1024], P('batch')
- grad_b_in: float32 [1024], P('batch')
Inputs may be any that keep to these rules, and one draw needn't show every extreme that they name: `counts`: some segment takes 3 steps and some takes 1.
All inputs are finite; a program needn't handle non-finite values.
Results may differ from a plain program's by a relative error of at most 0.00125.
Values may be sent and summed in bfloat16 or wider, within the bound.
No kernel may reach another device: no remote copies, remote signals or barrier semaphores. Data moves between devices by JAX's collectives and lax.ppermute only.
A program may use at most 64 MiB of HBM per device.

v0:
```python
import math

import jax
import jax.numpy as jnp
from jax import lax
from jax.sharding import PartitionSpec as P

D = 1024
MAXSTEP = 3


time_step = 0.25
penalty = 1.0


def shifted(block, axis, distance):
    devices = range(lax.axis_size(axis))
    route = [(i - distance, i) for i in devices if i - distance in devices]
    return lax.ppermute(block, axis, route)


def contract_rows(left, right):
    return lax.dot_general(
        left, right, (((0,), (0,)), ((), ())), preferred_element_type=jnp.float32
    )


def contract_cols(left, right):
    return lax.dot_general(
        left, right, (((1,), (1,)), ((), ())), preferred_element_type=jnp.float32
    )


def vector_field(current, w_in, b_in, w_out):
    inputs = current.astype(jnp.bfloat16)
    hidden = jnp.tanh(jnp.dot(inputs, w_in, preferred_element_type=jnp.float32) + b_in)
    slope = jnp.dot(hidden.astype(jnp.bfloat16), w_out, preferred_element_type=jnp.float32)
    return (slope, inputs, hidden)


def runge_kutta(current, w_in, b_in, w_out):
    slope_one, in_one, hid_one = vector_field(current, w_in, b_in, w_out)
    slope_two, in_two, hid_two = vector_field(
        current + 0.5 * time_step * slope_one, w_in, b_in, w_out
    )
    slope_three, in_three, hid_three = vector_field(
        current + 0.5 * time_step * slope_two, w_in, b_in, w_out
    )
    slope_four, in_four, hid_four = vector_field(
        current + time_step * slope_three, w_in, b_in, w_out
    )
    updated = current + time_step / 6.0 * (
        slope_one + 2.0 * slope_two + 2.0 * slope_three + slope_four
    )
    inputs = jnp.stack([in_one, in_two, in_three, in_four])
    hiddens = jnp.stack([hid_one, hid_two, hid_three, hid_four])
    return (updated, inputs, hiddens)


def field_back(hidden, outer, w_in, w_out):
    outer_low = outer.astype(jnp.bfloat16)
    inner = contract_cols(outer_low, w_out) * (1.0 - hidden * hidden)
    inner_low = inner.astype(jnp.bfloat16)
    return (contract_cols(inner_low, w_in), outer_low, inner_low, jnp.sum(inner, axis=0))


def runge_kutta_back(state_bar, inputs, hiddens, w_in, w_out):
    back_four, outer_four, inner_four, bias_four = field_back(
        hiddens[3], time_step / 6.0 * state_bar, w_in, w_out
    )
    back_three, outer_three, inner_three, bias_three = field_back(
        hiddens[2], time_step / 3.0 * state_bar + time_step * back_four, w_in, w_out
    )
    back_two, outer_two, inner_two, bias_two = field_back(
        hiddens[1], time_step / 3.0 * state_bar + 0.5 * time_step * back_three, w_in, w_out
    )
    back_one, outer_one, inner_one, bias_one = field_back(
        hiddens[0], time_step / 6.0 * state_bar + 0.5 * time_step * back_two, w_in, w_out
    )
    new_bar = state_bar + back_one + back_two + back_three + back_four
    outers = jnp.concatenate([outer_one, outer_two, outer_three, outer_four], axis=0)
    inners = jnp.concatenate([inner_one, inner_two, inner_three, inner_four], axis=0)
    flat_inputs = inputs.reshape(-1, inputs.shape[-1])
    flat_hidden = hiddens.astype(jnp.bfloat16).reshape(-1, hiddens.shape[-1])
    grad_in_step = contract_rows(flat_inputs, inners)
    grad_out_step = contract_rows(flat_hidden, outers)
    grad_bias_step = bias_one + bias_two + bias_three + bias_four
    return (new_bar, grad_in_step, grad_out_step, grad_bias_step)


def body(starts, targets, counts, w_in, b_in, w_out):
    full_in, full_out = (
        lax.all_gather(w_in, "batch", axis=0, tiled=True),
        lax.all_gather(w_out, "batch", axis=0, tiled=True),
    )
    start_now = starts[0]
    target_now = targets[0]
    step_total = counts[0]
    seg_place = lax.axis_index("seg")
    batch_count = lax.axis_size("batch")
    row_count = start_now.shape[0]

    def advance_plain(step_index, carry):
        current, saved = carry
        saved = lax.dynamic_update_index_in_dim(saved, current, step_index, 0)
        updated, inputs, hiddens = runge_kutta(current, full_in, b_in, full_out)
        return (updated, saved)

    saved_empty = jnp.zeros((MAXSTEP, row_count, D), jnp.float32)
    end_state, saved = lax.fori_loop(0, step_total, advance_plain, (start_now, saved_empty))

    def recall(step_index):
        current = lax.dynamic_index_in_dim(saved, step_index, 0, keepdims=False)
        updated, inputs, hiddens = runge_kutta(current, full_in, b_in, full_out)
        return (inputs, hiddens)

    miss = end_state - target_now
    previous = shifted(end_state, "seg", 1)
    has_prev = (seg_place > 0).astype(jnp.float32)
    gap_here = (previous - start_now) * has_prev
    returned = shifted(penalty * gap_here, "seg", -1)
    end_bar = miss + returned

    def retreat(turn, carry):
        state_bar, acc_in, acc_out, acc_bias = carry
        step_index = step_total - 1 - turn
        inputs, hiddens = recall(step_index)
        new_bar, grad_in_step, grad_out_step, grad_bias_step = runge_kutta_back(
            state_bar, inputs, hiddens, full_in, full_out
        )
        return (new_bar, acc_in + grad_in_step, acc_out + grad_out_step, acc_bias + grad_bias_step)

    initial = (
        end_bar,
        jnp.zeros(full_in.shape, jnp.float32),
        jnp.zeros(full_out.shape, jnp.float32),
        jnp.zeros(b_in.shape, jnp.float32),
    )
    start_bar, total_in, total_out, total_bias = lax.fori_loop(0, step_total, retreat, initial)
    start_term = -(penalty * gap_here)
    grad_starts = (start_bar + start_term)[None]
    scale = 1.0 / math.sqrt(row_count * batch_count)
    scaled_in = total_in * scale
    scaled_out = total_out * scale
    scaled_bias = total_bias * scale
    shares = (
        lax.psum_scatter(scaled_in, "batch", scatter_dimension=0, tiled=True),
        lax.psum_scatter(scaled_out, "batch", scatter_dimension=0, tiled=True),
        lax.psum_scatter(scaled_bias, "batch", scatter_dimension=0, tiled=True),
    )
    grad_in, grad_out, grad_bias = lax.psum((shares[0], shares[1], shares[2]), "seg")
    return (grad_starts, grad_in, grad_out, grad_bias)


def solution(mesh):
    return jax.shard_map(
        body,
        mesh=mesh,
        in_specs=(
            P("seg", "batch", None),
            P("seg", "batch", None),
            P("seg"),
            P("batch", None),
            P(),
            P("batch", None),
        ),
        out_specs=(P("seg", "batch", None), P("batch", None), P("batch", None), P("batch")),
        check_vma=False,
    )
```

profile of v0, /device:TPU:1, one launch (start us, length us, event | category | flops | bytes accessed | tf_op | source)
XLA Modules:
  0.0 728.4 jit_solution(12884548266842338025)
XLA Ops:
  8.7 1.9 copy.12
  10.6 73.6 %all-gather.3.cloned.1.call-done = bf16[1024,1024]{1,0:T(8,128)(2,1)} async-done(((bf16[32,1024]{1,0:T(8,128)(2,1)}), bf16[1024,1024]{1,0:T(8,128)(2,1)}) %all-gather.3.cloned.1.call-update) | async-done | bytes 2097168 | tf_op jit(solution)/shard_map/all_gather | solution.py:93
  84.2 71.7 %all-gather.5.cloned.1.call-done = bf16[1024,1024]{1,0:T(8,128)(2,1)} async-done(((bf16[32,1024]{1,0:T(8,128)(2,1)}), bf16[1024,1024]{1,0:T(8,128)(2,1)}) %all-gather.5.cloned.1.call-update) | async-done | bytes 2097168 | tf_op jit(solution)/shard_map/all_gather | solution.py:94
  155.9 1.4 broadcast_in_dim.14
  157.2 16.5 %while.30 = (s32[]{:T(128)}, f32[128,1024]{1,0:T(8,128)}, f32[3,128,1024]{2,1,0:T(8,128)}, s32[]{:T(128)}, bf16[1024,1024]{1,0:T(8,128)(2,1)}, /*index=5*/f32[10...) while((s32[]{:T(128)}, f32[128,1024]{1,0:T(8,128)}, f32[3,128,1024]{2,1,0:T(8,128)}, ...), condition=%wide.region_1.2_spmd, body=%wide.region_0.1_spmd.sunk | while | flops 2150760448 | bytes 34095276 | solution.py:110
  158.9 3.1 fusion.174
  162.1 3.2 fusion.175
  165.2 3.3 fusion.176
  169.4 3.6 fusion.177
  173.7 36.4 %collective-permute-start = (f32[128,1024]{1,0:T(8,128)}, f32[128,1024]{1,0:T(8,128)S(1)}, u32[]{:S(2)}, u32[]{:S(2)}) collective-permute-start(f32[128,1024]{1,0:T(8,128)} %get-tuple-element.170), channel_id=1, source_target_pairs={{0,32},{32,64},{64,96},{1,33},{33,65},{65,97},{2,34},{34,66},{66,9... | collective-permute-start | bytes 1572872 | tf_op jit(solution)/shard_map/ppermute | solution.py:19
  210.2 6.4 collective-permute-done
  217.7 1.9 collective-permute-start.1
  220.3 8.6 %collective-permute-done.1 = f32[128,1024]{1,0:T(8,128)S(1)} collective-permute-done((f32[128,1024]{1,0:T(8,128)S(1)}, f32[128,1024]{1,0:T(8,128)S(1)}, u32[]{:S(2)}, u32[]{:S(2)}) %collective-permute-start.1) | collective-permute-done | bytes 524320 | tf_op jit(solution)/shard_map/ppermute | solution.py:19
  228.8 1.3 fusion.66
  230.1 2.5 broadcast.45.clone
  232.6 2.5 broadcast.45
  235.1 21.9 %while.31 = (s32[]{:T(128)}, f32[128,1024]{1,0:T(8,128)S(1)}, f32[1024,1024]{1,0:T(8,128)}, f32[1024,1024]{1,0:T(8,128)}, f32[1024]{0:T(1024)S(1)}, /*index=5*/s...) while((s32[]{:T(128)}, f32[128,1024]{1,0:T(8,128)S(1)}, ...), condition=%wide.region_7.8_spmd, body=%wide.region_2.7_spmd.sunk | while | flops 6195249152 | bytes 161800576 | solution.py:139
  236.1 1.2 dynamic-slice_convert_fusion.2
  237.3 1.5 fusion.211
  249.1 1.2 copy-done.5
  250.3 1.4 convolution_add_fusion.14
  252.5 1.4 convolution_add_fusion.15
  254.4 2.0 copy-done.4
  257.1 5.0 broadcast_multiply_fusion.1
  262.1 5.0 broadcast_multiply_fusion
  269.0 79.9 %all-reduce = f32[1024]{0:T(1024)S(1)} all-reduce(f32[1024]{0:T(1024)S(1)} %broadcast_multiply_fusion.2), channel_id=4, replica_groups=mesh['seg'=4,'batch'=32] {'batch'}, use_global_device_ids=true, to_apply=%region_12.13.clone | all-reduce | flops 1024 | bytes 8192
  349.0 58.6 %psum.23 = f32[32]{0:T(128)} all-reduce(f32[32]{0:T(128)S(1)} %dynamic-slice.1), channel_id=1, replica_groups=mesh['seg'=4,'batch'=32] {'seg'}, use_global_device_ids=true, to_apply=%region_13.14 | all-reduce | flops 32 | bytes 256 | tf_op jit(solution)/shard_map/psum | solution.py:151
  407.6 63.2 %reduce-scatter.3.cloned.1.call-done = f32[32,1024]{1,0:T(8,128)} async-done(((f32[1024,1024]{1,0:T(8,128)}), f32[32,1024]{1,0:T(8,128)}) %reduce-scatter.3.cloned.1.call-update) | async-done | bytes 131088 | tf_op jit(solution)/shard_map/reduce_scatter | solution.py:147
  470.9 190.8 %reduce-scatter.5.cloned.1.call-done = f32[32,1024]{1,0:T(8,128)} async-done(((f32[1024,1024]{1,0:T(8,128)}), f32[32,1024]{1,0:T(8,128)}) %reduce-scatter.5.cloned.1.call-update) | async-done | bytes 131088 | tf_op jit(solution)/shard_map/reduce_scatter | solution.py:148
  662.6 56.1 %all-reduce.4.cloned.1.call-done = (f32[32,1024]{1,0:T(8,128)}, f32[32,1024]{1,0:T(8,128)}) async-done(((f32[32,1024]{1,0:T(8,128)}, f32[32,1024]{1,0:T(8,128)}), (f32[32,1024]{1,0:T(8,128)}, f32[32,1024]{1,0:T(8,128)})) %all-reduce.4.cloned.1.call-update) | async-done | bytes 262160 | tf_op jit(solution)/shard_map/psum | solution.py:151
  718.7 1.6 copy.40
  720.3 1.6 copy.41
  (56 shorter events, 18.1 us)
Async XLA Ops:
  7.2 150.0 %copy-start.8 = (f32[1024]{0:T(1024)S(1)}, f32[1024]{0:T(1024)}, u32[]{:S(2)}) copy-start(f32[1024]{0:T(1024)} %param.14) | copy-start | bytes 12292
  7.2 77.0 %all-gather.3.cloned.1.call-start = ((), (), s32[]{:S(2)}) async-start(), calls=%async_computation.2 | async-start | bytes 2162688 | tf_op jit(solution)/shard_map/all_gather | solution.py:93
  7.9 147.9 %all-gather.5.cloned.1.call-start = ((), (), s32[]{:S(2)}) async-start(), calls=%async_computation.3 | async-start | bytes 2162688 | tf_op jit(solution)/shard_map/all_gather | solution.py:94
  8.7 462.2 %reduce-scatter.3.cloned.1.call-start = ((), (), s32[]{:S(2)}) async-start(), calls=%async_computation.4 | async-start | bytes 4325376 | tf_op jit(solution)/shard_map/reduce_scatter | solution.py:147
  158.9 3.1 copy-start
  173.7 42.9 %collective-permute-start = (f32[128,1024]{1,0:T(8,128)}, f32[128,1024]{1,0:T(8,128)S(1)}, u32[]{:S(2)}, u32[]{:S(2)}) collective-permute-start(f32[128,1024]{1,0:T(8,128)} %get-tuple-element.170), channel_id=1, source_target_pairs={{0,32},{32,64},{64,96},{1,33},{33,65},{65,97},{2,34},{34,66},{66,9... | collective-permute-start | bytes 1572872 | tf_op jit(solution)/shard_map/ppermute | solution.py:19
  217.7 11.1 %collective-permute-start.1 = (f32[128,1024]{1,0:T(8,128)S(1)}, f32[128,1024]{1,0:T(8,128)S(1)}, u32[]{:S(2)}, u32[]{:S(2)}) collective-permute-start(f32[128,1024]{1,0:T(8,128)S(1)} %subtract_multiply_fusion), channel_id=1, source_target_pairs={{32,0},{64,32},{96,64},{33,1},{65,33},{97,65},{34,2},{66,34},{98,6... | collective-permute-start | bytes 1572872 | tf_op jit(solution)/shard_map/ppermute | solution.py:19
  232.6 2.5 copy-start.1
  236.0 2.8 copy-start.2
  236.0 2.8 copy-start.7
  248.1 2.2 copy-start.5
  250.3 2.2 copy-start.3
  252.5 2.0 copy-start.6
  254.4 2.0 copy-start.4
  262.1 399.7 %reduce-scatter.5.cloned.1.call-start = ((), (), s32[]{:S(2)}) async-start(), calls=%async_computation.5 | async-start | bytes 4325376 | tf_op jit(solution)/shard_map/reduce_scatter | solution.py:148
  267.1 0.7 copy-start.9
  267.1 451.6 %all-reduce.4.cloned.1.call-start = ((), (), s32[]{:S(2)}) async-start(), calls=%async_computation.6 | async-start | bytes 524288 | tf_op jit(solution)/shard_map/psum | solution.py:151
Sparse Core Ops, SparseCore 0:
  11.1 73.0 all-gather.2
  87.3 68.5 all-gather.4
  262.2 208.6 reduce-scatter.2
  473.1 188.5 reduce-scatter.4
  664.1 54.5 all-reduce.3
where the time goes:
time: 729 us; the launch traced here: 728 us
  waiting for transfers between devices  472 us (65%)
  blocking collectives  139 us (19%)
  starting transfers between devices  38.6 us (5%)
  matrix products  27.3 us (4%)
  local copies, waits for them, and re-layouts  20.2 us (3%)
  between operations  15.2 us (2%)
  other arithmetic  13.7 us (2%)
    reduce_scatter x1, waiting for transfers between devices, body(): lax.psum_scatter(scaled_out, 'batch', scatter_dimension=0, tiled=True)  191 us
    unnamed x1, blocking collectives  79.9 us
    all_gather x1, waiting for transfers between devices, body(): lax.all_gather(w_in, 'batch', axis=0, tiled=True)  73.6 us
    all_gather x1, waiting for transfers between devices, body(): lax.all_gather(w_out, 'batch', axis=0, tiled=True)  71.7 us
    reduce_scatter x1, waiting for transfers between devices, body(): lax.psum_scatter(scaled_in, 'batch', scatter_dimension=0, tiled=True)  63.2 us
    psum x1, blocking collectives, body(): lax.psum((shares[0], shares[1], shares[2]), 'seg')  58.6 us
    psum x1, waiting for transfers between devices, body(): lax.psum((shares[0], shares[1], shares[2]), 'seg')  56.1 us
    ppermute x2, starting transfers between devices, shifted(): return lax.ppermute(block, axis, route)  38.4 us
  transfers between devices with their start and end apart: 7, of which 7 were waited for; matrix products, arithmetic and copies ran while one was open for 1% of the time, Pallas kernels for 0%

commit v1 on v0

--- a/solution.py
+++ b/solution.py
@@ -3,20 +3,14 @@
 import jax
 import jax.numpy as jnp
 from jax import lax
-from jax.sharding import PartitionSpec as P
+from jax.sharding import Mesh, PartitionSpec as P
 
 D = 1024
 MAXSTEP = 3
-
-
 time_step = 0.25
 penalty = 1.0
-
-
-def shifted(block, axis, distance):
-    devices = range(lax.axis_size(axis))
-    route = [(i - distance, i) for i in devices if i - distance in devices]
-    return lax.ppermute(block, axis, route)
+SEG = ("zlo", "core")
+GROUP = ("zlo", "batch")
 
 
 def contract_rows(left, right):
@@ -88,17 +82,41 @@
     return (new_bar, grad_in_step, grad_out_step, grad_bias_step)
 
 
+def level_of(peak):
+    return jnp.ceil(256.0 * jnp.log2(jnp.maximum(peak, 1e-36))) + 2.0
+
+
+def coded(values, level):
+    scaled = values * (32767.0 * jnp.exp2(level * (-1.0 / 256.0)))
+    return scaled
+
+
+def low(values):
+    return jnp.round(values).astype(jnp.int32).astype(jnp.int16)
+
+
+def shift_seg(block, distance):
+    route = [(i - distance, i) for i in range(4) if 0 <= i - distance < 4]
+    return lax.ppermute(block, SEG, route)
+
+
 def body(starts, targets, counts, w_in, b_in, w_out):
-    full_in, full_out = (
-        lax.all_gather(w_in, "batch", axis=0, tiled=True),
-        lax.all_gather(w_out, "batch", axis=0, tiled=True),
-    )
     start_now = starts[0]
     target_now = targets[0]
     step_total = counts[0]
-    seg_place = lax.axis_index("seg")
+    core = lax.axis_index("core")
+    seg_place = lax.axis_index(SEG)
     batch_count = lax.axis_size("batch")
     row_count = start_now.shape[0]
+    own = w_in.shape[0]
+
+    next_start = shift_seg(start_now, -1)
+    shard = jnp.where(core == 0, w_in, w_out)
+    gathered = lax.all_to_all(
+        jnp.broadcast_to(shard[None], (batch_count, own, D)), "batch", 0, 0
+    ).reshape(D, D)
+    both = lax.all_to_all(jnp.broadcast_to(gathered[None], (2, D, D)), "core", 0, 0)
+    full_in, full_out = both[0], both[1]
 
     def advance_plain(step_index, carry):
         current, saved = carry
@@ -114,12 +132,10 @@
         updated, inputs, hiddens = runge_kutta(current, full_in, b_in, full_out)
         return (inputs, hiddens)
 
-    miss = end_state - target_now
-    previous = shifted(end_state, "seg", 1)
+    previous = shift_seg(end_state, 1)
+    has_next = (seg_place < 3).astype(jnp.float32)
     has_prev = (seg_place > 0).astype(jnp.float32)
-    gap_here = (previous - start_now) * has_prev
-    returned = shifted(penalty * gap_here, "seg", -1)
-    end_bar = miss + returned
+    end_bar = (end_state - target_now) + penalty * ((end_state - next_start) * has_next)
 
     def retreat(turn, carry):
         state_bar, acc_in, acc_out, acc_bias = carry
@@ -137,33 +153,65 @@
         jnp.zeros(b_in.shape, jnp.float32),
     )
     start_bar, total_in, total_out, total_bias = lax.fori_loop(0, step_total, retreat, initial)
-    start_term = -(penalty * gap_here)
-    grad_starts = (start_bar + start_term)[None]
+    gap_before = (previous - start_now) * has_prev
+    grad_starts = (start_bar - penalty * gap_before)[None]
+
+    keep = jnp.where(core == 0, total_in, total_out)
+    send = jnp.where(core == 0, total_out, total_in)
+    total = keep + lax.ppermute(send, "core", [(0, 1), (1, 0)])
+    group = lax.axis_size(GROUP)
+    piece = D // group
+    level = level_of(jnp.max(jnp.abs(total), axis=0, keepdims=True))
+    data = low(coded(total, level)).reshape(group, piece, D)
+    bias_level = level_of(jnp.max(jnp.abs(total_bias)))
+    bias_scaled = coded(total_bias, bias_level)
+    bias_high = jnp.round(bias_scaled)
+    bias_rows = jnp.stack([bias_high, (bias_scaled - bias_high) * 32767.0]).reshape(2, batch_count, own)
+    bias_rows = jnp.pad(jnp.swapaxes(bias_rows, 0, 1), ((0, 0), (0, 0), (0, D - own)))
+    head = jnp.concatenate(
+        [
+            jnp.broadcast_to(level[None], (batch_count, 1, D)),
+            jnp.broadcast_to(bias_level, (batch_count, 1, D)),
+            bias_rows,
+            jnp.zeros((batch_count, 4, D), jnp.float32),
+        ],
+        axis=1,
+    )
+    head = jnp.repeat(low(head), group // batch_count, axis=0)
+    data = jnp.swapaxes(data.reshape(batch_count, 2, piece, D), 0, 1).reshape(group, piece, D)
+    head = jnp.swapaxes(head.reshape(batch_count, 2, 8, D), 0, 1).reshape(group, 8, D)
+    got = lax.all_to_all(jnp.concatenate([data, head], axis=1), GROUP, 0, 0)
+    got = got.astype(jnp.float32)
+    back = jnp.exp2(got[:, piece : piece + 1] * (1.0 / 256.0)) * (1.0 / 32767.0)
+    part = jnp.sum(got[:, :piece] * back, axis=0)
+    bias_back = jnp.exp2(got[:, piece + 1] * (1.0 / 256.0)) * (1.0 / 32767.0)
+    bias_part = jnp.sum(
+        (got[:, piece + 2] + got[:, piece + 3] * (1.0 / 32767.0)) * bias_back, axis=0
+    )
+    mine = jnp.concatenate([part, jnp.broadcast_to(bias_part[None], (8, D))], axis=0)
+    four = lax.all_to_all(jnp.broadcast_to(mine[None], (4, piece + 8, D)), SEG, 0, 0)
     scale = 1.0 / math.sqrt(row_count * batch_count)
-    scaled_in = total_in * scale
-    scaled_out = total_out * scale
-    scaled_bias = total_bias * scale
-    shares = (
-        lax.psum_scatter(scaled_in, "batch", scatter_dimension=0, tiled=True),
-        lax.psum_scatter(scaled_out, "batch", scatter_dimension=0, tiled=True),
-        lax.psum_scatter(scaled_bias, "batch", scatter_dimension=0, tiled=True),
-    )
-    grad_in, grad_out, grad_bias = lax.psum((shares[0], shares[1], shares[2]), "seg")
+    four = four * scale
+    grad_in = jnp.concatenate([four[0, :piece], four[2, :piece]], axis=0)
+    grad_out = jnp.concatenate([four[1, :piece], four[3, :piece]], axis=0)
+    grad_bias = four[0, piece, :own] + four[1, piece, :own]
     return (grad_starts, grad_in, grad_out, grad_bias)
 
 
 def solution(mesh):
+    segs, batches = mesh.devices.shape
+    finer = Mesh(mesh.devices.reshape(2, segs // 2, batches), ("zlo", "core", "batch"))
     return jax.shard_map(
         body,
-        mesh=mesh,
+        mesh=finer,
         in_specs=(
-            P("seg", "batch", None),
-            P("seg", "batch", None),
-            P("seg"),
+            P(SEG, "batch", None),
+            P(SEG, "batch", None),
+            P(SEG),
             P("batch", None),
             P(),
             P("batch", None),
         ),
-        out_specs=(P("seg", "batch", None), P("batch", None), P("batch", None), P("batch")),
+        out_specs=(P(SEG, "batch", None), P("batch", None), P("batch", None), P("batch")),
         check_vma=False,
     )

time: 729 us -> 259 us (0.36)
  waiting for transfers between devices: 472 us -> 68.7 us
  blocking collectives: 139 us -> 8.74 us
  starting transfers between devices: 38.6 us -> 103 us
  between operations: 15.2 us -> 2.22 us
  other arithmetic: 13.7 us -> 24.2 us
    reduce_scatter x2 -> x0, waiting for transfers between devices: 254 us -> none  [the longest x1 191 us: body(): lax.psum_scatter(scaled_out, 'batch', scatter_dimension=0, tiled=True)]
    all_gather x2 -> x0, waiting for transfers between devices: 145 us -> none  [the longest x1 73.6 us: body(): lax.all_gather(w_in, 'batch', axis=0, tiled=True)]
    all_to_all x0 -> x3, starting transfers between devices: none -> 95.7 us  [the longest x1 78.3 us: body(): got = lax.all_to_all(jnp.concatenate([data, head], axis=1), GROUP, 0, 0)]
    unnamed x1 -> x0, blocking collectives: 79.9 us -> none
    all_to_all x0 -> x3, waiting for transfers between devices: none -> 63.3 us  [the longest x1 35.8 us: body(): got = lax.all_to_all(jnp.concatenate([data, head], axis=1), GROUP, 0, 0)]
    psum x1 -> x0, blocking collectives: 58.6 us -> none  [body(): lax.psum((shares[0], shares[1], shares[2]), 'seg')]
    psum x1 -> x0, waiting for transfers between devices: 56.1 us -> none  [body(): lax.psum((shares[0], shares[1], shares[2]), 'seg')]
    ppermute x2 -> x3, starting transfers between devices: 38.4 us -> 7 us  [the longest x2 6.64 us: shift_seg(): return lax.ppermute(block, SEG, route)]
  transfers between devices with their start and end apart: 7 -> 6, of which waited for: 7 -> 4; matrix products, arithmetic and copies ran while one was open for 1% -> 11% of each run, Pallas kernels for 0% -> 0%
where the time goes in v1:
time: 259 us; the launch traced here: 258 us
  starting transfers between devices  103 us (40%)
  waiting for transfers between devices  68.7 us (27%)
  matrix products  26.6 us (10%)
  other arithmetic  24.2 us (9%)
  local copies, waits for them, and re-layouts  21.3 us (8%)
  blocking collectives  8.74 us (3%)
  loops' own time  3.04 us (1%)
    all_to_all x1, starting transfers between devices, body(): got = lax.all_to_all(jnp.concatenate([data, head], axis=1), GROUP, 0, 0)  78.3 us
    all_to_all x1, waiting for transfers between devices, body(): got = lax.all_to_all(jnp.concatenate([data, head], axis=1), GROUP, 0, 0)  35.8 us
    all_to_all x1, waiting for transfers between devices, body(): lax.all_to_all(jnp.broadcast_to(shard[None], (batch_count, own, D)), 'bat...  23 us
    dot_general x7, matrix products, vector_field(): jnp.dot(hidden.astype(jnp.bfloat16), w_out, preferred_element_type=jnp.fl...  13.8 us
    all_to_all x1, starting transfers between devices, body(): lax.all_to_all(jnp.broadcast_to(shard[None], (batch_count, own, D)), 'bat...  11.2 us
    all_to_all x1, blocking collectives, body(): lax.all_to_all(jnp.broadcast_to(gathered[None], (2, D, D)), 'core', 0, 0)  8.74 us
    dot_general x8, matrix products, contract_cols(): lax.dot_general(left, right, (((1,), (1,)), ((), ())), preferred_element_...  6.95 us
    ppermute x2, starting transfers between devices, shift_seg(): return lax.ppermute(block, SEG, route)  6.64 us
  transfers between devices with their start and end apart: 6, of which 4 were waited for; matrix products, arithmetic and copies ran while one was open for 11% of the time, Pallas kernels for 0%

profile of v1, /device:TPU:1, one launch (start us, length us, event | category | flops | bytes accessed | tf_op | source)
XLA Modules:
  0.0 257.5 jit_solution(9741585967559970131)
XLA Ops:
  1.5 1.6 broadcast_in_dim.35
  3.1 11.2 %all-to-all-start = ((bf16[32,32,1024]{2,1,0:T(8,128)(2,1)}), bf16[32,32,1024]{2,1,0:T(8,128)(2,1)S(1)}, u32[]{:S(2)}, u32[]{:S(2)}) async-start(bf16[32,32,1024]{2,1,0:T(8,128)(2,1)} %broadcast_in_dim.35), calls=%async_computation | async-start | bytes 4194304 | tf_op jit(solution)/shard_map/all_to_all | solution.py:115
  14.3 2.9 %collective-permute-start = (f32[128,1024]{1,0:T(8,128)}, f32[128,1024]{1,0:T(8,128)}, u32[]{:S(2)}, u32[]{:S(2)}) collective-permute-start(f32[128,1024]{1,0:T(8,128)} %bitcast.11), channel_id=1, source_target_pairs={{32,0},{64,32},{96,64},{33,1},{65,33},{97,65},{34,2},{66,34},{98,6... | collective-permute-start | bytes 1572872 | tf_op jit(solution)/shard_map/ppermute | solution.py:100
  17.1 1.9 copy.16
  19.7 23.0 %all-to-all-done = bf16[32,32,1024]{2,1,0:T(8,128)(2,1)S(1)} async-done(((bf16[32,32,1024]{2,1,0:T(8,128)(2,1)}), bf16[32,32,1024]{2,1,0:T(8,128)(2,1)S(1)}, u32[]{:S(2)}, u32[]{:S(2)}) %all-to-all-start) | async-done | bytes 2097184 | tf_op jit(solution)/shard_map/all_to_all | solution.py:115
  43.2 8.7 %all_to_all.20 = bf16[2,1024,1024]{2,1,0:T(8,128)(2,1)S(1)} all-to-all(bf16[2,1024,1024]{2,1,0:T(8,128)(2,1)S(1)} %broadcast_in_dim.37), channel_id=1, replica_groups=mesh['zlo'=2,'core'=2,'batch'=32] {'core'}, dimensions={0} | all-to-all | bytes 8388608 | tf_op jit(solution)/shard_map/all_to_all | solution.py:118
  52.0 1.8 slice_bitcast_fusion
  53.8 1.3 broadcast_in_dim.34
  55.1 15.7 %while.30 = (s32[]{:T(128)}, f32[128,1024]{1,0:T(8,128)}, f32[3,128,1024]{2,1,0:T(8,128)}, s32[]{:T(128)}, bf16[1024,1024]{1,0:T(8,128)(2,1)S(1)}, /*index=5*/f3...) while((s32[]{:T(128)}, f32[128,1024]{1,0:T(8,128)}, ...), condition=%wide.region_1.2_spmd, body=%wide.region_0.1_spmd.sunk | while | flops 2150760448 | bytes 25706640 | solution.py:128
  56.8 2.4 fusion.188
  59.2 3.2 %fusion.189 = f32[128,1024]{1,0:T(8,128)} fusion(bf16[1024,1024]{1,0:T(8,128)(2,1)} %get-tuple-element.424, bf16[1024,1024]{1,0:T(8,128)(2,1)S(1)} %get-tuple-element.422, f32[128,1024]{1,0:T(8,128)S(1)} %copy.41, f32[128,1024]{1,0:T(8,128)S(1)} %fusion.188, f32[1024]{0:T(1024)S(1)} %get-tuple-element.423), kind=kOutput, calls=%fused_computation.16.clone.1 | convolution fusion | flops 537526272 | bytes 5771264 | tf_op jit(solution)/shard_map/while/body/dot_general | solution.py:31
  62.3 3.3 %fusion.190 = f32[128,1024]{1,0:T(8,128)} fusion(bf16[1024,1024]{1,0:T(8,128)(2,1)} %get-tuple-element.424, bf16[1024,1024]{1,0:T(8,128)(2,1)S(1)} %get-tuple-element.422, f32[128,1024]{1,0:T(8,128)S(1)} %copy.41, f32[128,1024]{1,0:T(8,128)} %fusion.189, f32[1024]{0:T(1024)S(1)} %get-tuple-element.423), kind=kOutput, calls=%fused_computation.15.clone.1 | convolution fusion | flops 537526272 | bytes 5771264 | tf_op jit(solution)/shard_map/while/body/dot_general | solution.py:31
  66.5 3.6 %fusion.191 = f32[128,1024]{1,0:T(8,128)} fusion(f32[128,1024]{1,0:T(8,128)S(1)} %copy.41, bf16[1024,1024]{1,0:T(8,128)(2,1)} %get-tuple-element.424, bf16[1024,1024]{1,0:T(8,128)(2,1)S(1)} %get-tuple-element.422, f32[128,1024]{1,0:T(8,128)} %fusion.190, f32[128,1024]{1,0:T(8,128)S(1)} %fusion.188, f32[128,1024]{1,0:T(8,128)} %fusion.189, ...), kind=kOutput, calls=%fused_computation.2.clone.1 | convolution fusion | flops 538443776 | bytes 6819840 | tf_op jit(solution)/shard_map/while/body/dot_general | solution.py:31
  70.8 1.5 fusion.72
  72.3 2.5 broadcast.100.clone
  74.8 2.5 broadcast.100
  77.3 21.9 %while.31 = (s32[]{:T(128)}, f32[128,1024]{1,0:T(8,128)S(1)}, f32[1024,1024]{1,0:T(8,128)}, f32[1024,1024]{1,0:T(8,128)}, f32[1024]{0:T(1024)S(1)}, /*index=5*/s...) while((s32[]{:T(128)}, f32[128,1024]{1,0:T(8,128)S(1)}, ...), condition=%wide.region_7.8_spmd, body=%wide.region_2.7_spmd.sunk | while | flops 6195249152 | bytes 161800576 | solution.py:155
  79.5 1.5 fusion.225
  92.5 1.4 convolution_add_fusion.14
  94.6 1.4 convolution_add_fusion.15
  96.6 2.0 copy-done.2
  99.2 5.5 %broadcast_select_fusion = f32[1024,1024]{1,0:T(8,128)} fusion(f32[1024,1024]{1,0:T(8,128)} %get-tuple-element.174, f32[1024,1024]{1,0:T(8,128)} %get-tuple-element.173, pred[]{:T(512)S(6)} %eq.2), kind=kLoop, calls=%fused_computation.102 | loop fusion | flops 1048576 | bytes 12582913 | tf_op jit(solution)/shard_map/jit(_where)/select_n | solution.py:160
  106.8 5.4 %collective-permute-done.2 = f32[1024,1024]{1,0:T(8,128)} collective-permute-done((f32[1024,1024]{1,0:T(8,128)}, f32[1024,1024]{1,0:T(8,128)}, u32[]{:S(2)}, u32[]{:S(2)}) %collective-permute-start.2) | collective-permute-done | bytes 4194336 | tf_op jit(solution)/shard_map/ppermute | solution.py:161
  112.2 4.0 %abs_reduce_fusion = (f32[1024]{0:T(1024)S(1)}, f32[1024,1024]{1,0:T(8,128)S(1)}) fusion(f32[1024,1024]{1,0:T(8,128)} %collective-permute-done.2, f32[1024,1024]{1,0:T(8,128)} %get-tuple-element.173, f32[1024,1024]{1,0:T(8,128)} %get-tuple-element.174, pred[]{:T(512)S(6)} %eq.2), kind=kLoop, calls=%fused_computation.97 | loop fusion | flops 4193280 | bytes 16781312 | tf_op jit(solution)/shard_map/reduce_max | solution.py:164
  117.7 2.1 pad_add_fusion
  119.8 78.3 %all-to-all-start.2 = ((s16[64,24,1024]{2,1,0:T(8,128)(2,1)}), s16[64,24,1024]{2,1,0:T(8,128)(2,1)}, u32[]{:S(2)}, u32[]{:S(2)}) async-start(s16[64,24,1024]{2,1,0:T(8,128)(2,1)} %pad_add_fusion), calls=%async_computation.2 | async-start | bytes 6291456 | tf_op jit(solution)/shard_map/all_to_all | solution.py:183
  198.1 3.8 %collective-permute-start.1 = (f32[128,1024]{1,0:T(8,128)}, f32[128,1024]{1,0:T(8,128)S(1)}, u32[]{:S(2)}, u32[]{:S(2)}) collective-permute-start(f32[128,1024]{1,0:T(8,128)} %get-tuple-element.170), channel_id=1, source_target_pairs={{0,32},{32,64},{64,96},{1,33},{33,65},{65,97},{2,34},{34,66},{66,9... | collective-permute-start | bytes 1572872 | tf_op jit(solution)/shard_map/ppermute | solution.py:100
  201.9 35.8 %all-to-all-done.2 = s16[64,24,1024]{2,1,0:T(8,128)(2,1)} async-done(((s16[64,24,1024]{2,1,0:T(8,128)(2,1)}), s16[64,24,1024]{2,1,0:T(8,128)(2,1)}, u32[]{:S(2)}, u32[]{:S(2)}) %all-to-all-start.2) | async-done | bytes 3145760 | tf_op jit(solution)/shard_map/all_to_all | solution.py:183
  237.7 2.9 %convert_element_type.140 = f32[64,24,1024]{2,1,0:T(8,128)S(1)} convert(s16[64,24,1024]{2,1,0:T(8,128)(2,1)} %all-to-all-done.2) | non-fusion elementwise | flops 1572864 | bytes 9437184 | tf_op jit(solution)/shard_map/convert_element_type | solution.py:184
  243.6 6.2 %all-to-all-start.3 = ((f32[4,24,1024]{2,1,0:T(8,128)}), f32[4,24,1024]{2,1,0:T(8,128)S(1)}, u32[]{:S(2)}, u32[]{:S(2)}) async-start(f32[4,24,1024]{2,1,0:T(8,128)} %broadcast_in_dim.70), calls=%async_computation.3 | async-start | bytes 786432 | tf_op jit(solution)/shard_map/all_to_all | solution.py:192
  249.8 1.9 subtract_bitcast_fusion
  251.7 4.5 %all-to-all-done.3 = f32[4,24,1024]{2,1,0:T(8,128)S(1)} async-done(((f32[4,24,1024]{2,1,0:T(8,128)}), f32[4,24,1024]{2,1,0:T(8,128)S(1)}, u32[]{:S(2)}, u32[]{:S(2)}) %all-to-all-start.3) | async-done | bytes 393248 | tf_op jit(solution)/shard_map/all_to_all | solution.py:192
  (66 shorter events, 24.1 us)
Async XLA Ops:
  3.1 39.6 %all-to-all-start = ((bf16[32,32,1024]{2,1,0:T(8,128)(2,1)}), bf16[32,32,1024]{2,1,0:T(8,128)(2,1)S(1)}, u32[]{:S(2)}, u32[]{:S(2)}) async-start(bf16[32,32,1024]{2,1,0:T(8,128)(2,1)} %broadcast_in_dim.35), calls=%async_computation | async-start | bytes 4194304 | tf_op jit(solution)/shard_map/all_to_all | solution.py:115
  14.3 56.6 %collective-permute-start = (f32[128,1024]{1,0:T(8,128)}, f32[128,1024]{1,0:T(8,128)}, u32[]{:S(2)}, u32[]{:S(2)}) collective-permute-start(f32[128,1024]{1,0:T(8,128)} %bitcast.11), channel_id=1, source_target_pairs={{32,0},{64,32},{96,64},{33,1},{65,33},{97,65},{34,2},{66,34},{98,6... | collective-permute-start | bytes 1572872 | tf_op jit(solution)/shard_map/ppermute | solution.py:100
  52.0 3.1 %copy-start.6 = (f32[1024]{0:T(1024)S(1)}, f32[1024]{0:T(1024)}, u32[]{:S(2)}) copy-start(f32[1024]{0:T(1024)} %param.14) | copy-start | bytes 12292
  78.2 2.8 %copy-start = (bf16[1024,1024]{1,0:T(8,128)(2,1)S(1)}, bf16[1024,1024]{1,0:T(8,128)(2,1)}, u32[]{:S(2)}) copy-start(bf16[1024,1024]{1,0:T(8,128)(2,1)} %get-tuple-element.462) | copy-start | bytes 6291460 | tf_op jit(solution)/shard_map/while
  78.2 2.8 %copy-start.5 = (f32[3,128,1024]{2,1,0:T(8,128)S(1)}, f32[3,128,1024]{2,1,0:T(8,128)}, u32[]{:S(2)}) copy-start(f32[3,128,1024]{2,1,0:T(8,128)} %get-tuple-element.464) | copy-start | bytes 4718596 | tf_op jit(solution)/shard_map/while
  90.3 2.2 copy-start.3
  92.5 2.2 copy-start.1
  94.6 1.9 copy-start.4
  96.6 2.0 copy-start.2
  104.7 7.5 %collective-permute-start.2 = (f32[1024,1024]{1,0:T(8,128)}, f32[1024,1024]{1,0:T(8,128)}, u32[]{:S(2)}, u32[]{:S(2)}) collective-permute-start(f32[1024,1024]{1,0:T(8,128)} %broadcast_select_fusion), channel_id=1, source_target_pairs={{0,32},{32,0},{1,33},{33,1},{2,34},{34,2},{3,35},{35,3},{4,36},{36... | collective-permute-start | bytes 12582920 | tf_op jit(solution)/shard_map/ppermute | solution.py:161
  119.8 117.9 %all-to-all-start.2 = ((s16[64,24,1024]{2,1,0:T(8,128)(2,1)}), s16[64,24,1024]{2,1,0:T(8,128)(2,1)}, u32[]{:S(2)}, u32[]{:S(2)}) async-start(s16[64,24,1024]{2,1,0:T(8,128)(2,1)} %pad_add_fusion), calls=%async_computation.2 | async-start | bytes 6291456 | tf_op jit(solution)/shard_map/all_to_all | solution.py:183
  198.1 51.7 %collective-permute-start.1 = (f32[128,1024]{1,0:T(8,128)}, f32[128,1024]{1,0:T(8,128)S(1)}, u32[]{:S(2)}, u32[]{:S(2)}) collective-permute-start(f32[128,1024]{1,0:T(8,128)} %get-tuple-element.170), channel_id=1, source_target_pairs={{0,32},{32,64},{64,96},{1,33},{33,65},{65,97},{2,34},{34,66},{66,9... | collective-permute-start | bytes 1572872 | tf_op jit(solution)/shard_map/ppermute | solution.py:100
  243.6 12.6 %all-to-all-start.3 = ((f32[4,24,1024]{2,1,0:T(8,128)}), f32[4,24,1024]{2,1,0:T(8,128)S(1)}, u32[]{:S(2)}, u32[]{:S(2)}) async-start(f32[4,24,1024]{2,1,0:T(8,128)} %broadcast_in_dim.70), calls=%async_computation.3 | async-start | bytes 786432 | tf_op jit(solution)/shard_map/all_to_all | solution.py:192

commit v2 on v0

v2 whole, which is shorter than its diff:
```python
import math

import jax
import jax.numpy as jnp
from jax import lax
from jax.experimental import pallas as pl
from jax.experimental.pallas import tpu as pltpu
from jax.sharding import Mesh, PartitionSpec as P

MAXSTEP = 3
STAGES = 4
step_size = 0.25
penalty = 1.0
SEG = ("zlo", "core")
GROUP = ("zlo", "batch")
f32 = jnp.float32
bf16 = jnp.bfloat16
LANES = 128
HEAD = 16
TOP = 32767.0
VMEM = pl.BlockSpec(memory_space=pltpu.VMEM)
ANY = pl.BlockSpec(memory_space=pl.ANY)
SMEM = pl.BlockSpec(memory_space=pltpu.SMEM)


def product(left, right):
    return jnp.dot(left, right, preferred_element_type=f32)


def integrate_kernel(
    info, start, target, following, bias_in, own_w, other_w,
    ends, bar, bias, left, right,
    w, w_turned, state, tanhs, total, sems,
):
    count, core, has_next = info[0], info[1], info[2].astype(f32)
    slot_in = 1 - core
    slot_out = core
    rows = start.shape[0]
    first = pltpu.make_async_copy(own_w, w.at[core], sems.at[0])
    second = pltpu.make_async_copy(other_w, w.at[1 - core], sems.at[1])
    first.start()
    second.start()
    state[...] = start[...]
    bias[...] = jnp.zeros_like(bias)
    offset = bias_in[...]
    first.wait()
    second.wait()
    w_turned[0] = w[0].T
    w_turned[1] = w[1].T

    def place(at):
        return pl.ds(pl.multiple_of(at * rows, rows), rows)

    def field(u, at):
        inputs = u.astype(bf16)
        left[slot_in, place(at), :] = inputs
        hidden = jnp.tanh(product(inputs, w[0]) + offset)
        tanhs[at] = hidden
        low = hidden.astype(bf16)
        left[slot_out, place(at), :] = low
        return product(low, w[1])

    def field_back(q, at):
        outer = q.astype(bf16)
        right[slot_out, place(at), :] = outer
        hidden = tanhs[at]
        inner = product(outer, w_turned[1]) * (1.0 - hidden * hidden)
        bias[...] += jnp.sum(inner, axis=0, keepdims=True)
        low = inner.astype(bf16)
        right[slot_in, place(at), :] = low
        return product(low, w_turned[0])

    def forward(s, carry):
        at = STAGES * s
        k = field(state[...], at)
        total[...] = k
        k = field(state[...] + 0.5 * step_size * k, at + 1)
        total[...] += 2.0 * k
        k = field(state[...] + 0.5 * step_size * k, at + 2)
        total[...] += 2.0 * k
        k = field(state[...] + step_size * k, at + 3)
        state[...] = state[...] + step_size / 6.0 * (total[...] + k)
        return carry

    lax.fori_loop(0, count, forward, 0)
    end = state[...]
    ends[...] = end
    state[...] = (end - target[...]) + penalty * ((end - following[...]) * has_next)

    def backward(turn, carry):
        at = STAGES * (count - 1 - turn)
        g = field_back(step_size / 6.0 * state[...], at + 3)
        total[...] = state[...] + g
        g = field_back(step_size / 3.0 * state[...] + step_size * g, at + 2)
        total[...] += g
        g = field_back(step_size / 3.0 * state[...] + 0.5 * step_size * g, at + 1)
        total[...] += g
        g = field_back(step_size / 6.0 * state[...] + 0.5 * step_size * g, at)
        state[...] = total[...] + g
        return carry

    lax.fori_loop(0, count, backward, 0)
    bar[...] = state[...]

    def clear(s, carry):
        block = pl.ds(pl.multiple_of(s * STAGES * rows, STAGES * rows), STAGES * rows)
        for slot in range(2):
            left[slot, block, :] = jnp.zeros((STAGES * rows, left.shape[2]), bf16)
            right[slot, block, :] = jnp.zeros((STAGES * rows, right.shape[2]), bf16)
        return carry

    lax.fori_loop(count, MAXSTEP, clear, 0)


def integrate(info, start, target, following, bias_in, own_w, other_w):
    rows, width = start.shape
    depth = own_w.shape[1]
    factors = jax.ShapeDtypeStruct((2, MAXSTEP * STAGES * rows, width), bf16)
    states = jax.ShapeDtypeStruct((rows, width), f32)
    return pl.pallas_call(
        integrate_kernel,
        out_shape=(states, states, jax.ShapeDtypeStruct((1, depth), f32), factors, factors),
        in_specs=[SMEM] + [VMEM] * 4 + [ANY] * 2,
        out_specs=(VMEM,) * 5,
        scratch_shapes=[
            pltpu.VMEM((2, width, depth), bf16),
            pltpu.VMEM((2, depth, width), bf16),
            pltpu.VMEM((rows, width), f32),
            pltpu.VMEM((MAXSTEP * STAGES, rows, depth), f32),
            pltpu.VMEM((rows, width), f32),
            pltpu.SemaphoreType.DMA((2,)),
        ],
        compiler_params=pltpu.CompilerParams(vmem_limit_bytes=40 * 1024 * 1024),
        name="integrate",
    )(info, start, target, following, bias_in, own_w, other_w)


def level_of(peak):
    return jnp.ceil(256.0 * jnp.log2(jnp.maximum(peak, 1e-30))) + 1.0


def scale_of(level):
    return jnp.exp2(level * (1.0 / 256.0) - 15.0)


def steps_of(level):
    return jnp.exp2(15.0 - level * (1.0 / 256.0))


def whole(values):
    return jnp.round(values).astype(jnp.int32).astype(jnp.int16)


def code_kernel(keep, received, bias, message):
    halves, owners, height, _ = message.shape
    piece = keep.shape[0] // (halves * owners)
    blocks = keep.shape[1] // LANES
    row = lax.broadcasted_iota(jnp.int32, (HEAD, LANES), 0)
    bias_now = bias[...]
    bias_level = level_of(jnp.abs(bias_now))
    bias_steps = bias_now * steps_of(bias_level)
    bias_high = jnp.round(bias_steps)
    bias_low = (bias_steps - bias_high) * TOP
    base = jnp.where(row == 8, bias_level, 0.0)
    base = jnp.where(row == 9, bias_high, base)
    base = jnp.where(row == 10, bias_low, base)
    for owner in range(owners):
        for half in range(halves):
            at = (owner * halves + half) * piece
            head = base
            for block in range(blocks):
                columns = pl.ds(block * LANES, LANES)
                values = keep[pl.ds(at, piece), columns] + received[pl.ds(at, piece), columns]
                level = level_of(jnp.max(jnp.abs(values), axis=0, keepdims=True))
                head = jnp.where(row == block, level, head)
                message[half, owner, pl.ds(block * piece, piece), :] = whole(
                    values * steps_of(level)
                )
            message[half, owner, pl.ds(blocks * piece, HEAD), :] = whole(head)


def code(keep, received, bias, halves, batches):
    depth, width = keep.shape
    steps = width // LANES
    owners = batches // steps
    piece = depth // (halves * batches)
    height = piece * steps + HEAD
    block = pl.BlockSpec((depth // steps, width), lambda i: (i, 0))
    return pl.pallas_call(
        code_kernel,
        grid=(steps,),
        out_shape=jax.ShapeDtypeStruct((halves, batches, height, LANES), jnp.int16),
        in_specs=[block, block, pl.BlockSpec((1, LANES), lambda i: (0, i))],
        out_specs=pl.BlockSpec((halves, owners, height, LANES), lambda i: (0, i, 0, 0)),
        compiler_params=pltpu.CompilerParams(vmem_limit_bytes=16 * 1024 * 1024),
        name="code",
    )(keep, received, bias)


def decode_kernel(message, out):
    senders, height, _ = message.shape
    blocks = out.shape[1] // LANES
    piece = (height - HEAD) // blocks

    @pl.when(pl.program_id(0) == 0)
    def _():
        out[...] = jnp.zeros_like(out)

    sums = [jnp.zeros((piece, LANES), f32) for _ in range(blocks)]
    bias = jnp.zeros((1, LANES), f32)
    for sender in range(senders):
        head = message[sender, pl.ds(blocks * piece, HEAD), :].astype(jnp.int32).astype(f32)
        scale = scale_of(head)
        bias += (head[9:10] + head[10:11] * (1.0 / TOP)) * scale[8:9]
        for block in range(blocks):
            data = message[sender, pl.ds(block * piece, piece), :].astype(jnp.int32).astype(f32)
            sums[block] += data * scale[block : block + 1]
    for block in range(blocks):
        out[pl.ds(0, piece), pl.ds(block * LANES, LANES)] += sums[block]
    out[pl.ds(piece, 8), pl.ds(0, LANES)] += jnp.broadcast_to(bias, (8, LANES))


def decode(message, width):
    senders, height, _ = message.shape
    steps = 8
    piece = (height - HEAD) * LANES // width
    return pl.pallas_call(
        decode_kernel,
        grid=(steps,),
        out_shape=jax.ShapeDtypeStruct((piece + 8, width), f32),
        in_specs=[pl.BlockSpec((senders // steps, height, LANES), lambda i: (i, 0, 0))],
        out_specs=pl.BlockSpec((piece + 8, width), lambda i: (0, 0)),
        compiler_params=pltpu.CompilerParams(vmem_limit_bytes=16 * 1024 * 1024),
        name="decode",
    )(message)


def contract_rows(left, right):
    return lax.dot_general(left, right, (((0,), (0,)), ((), ())), preferred_element_type=f32)


def shift_seg(block, distance):
    count = lax.axis_size(SEG)
    route = [(i - distance, i) for i in range(count) if 0 <= i - distance < count]
    return lax.ppermute(block, SEG, route)


def swap(block):
    return lax.ppermute(block, "core", [(0, 1), (1, 0)])


def body(starts, targets, counts, w_in, b_in, w_out):
    start = starts[0]
    core = lax.axis_index("core")
    place = lax.axis_index(SEG)
    batches = lax.axis_size("batch")
    halves = lax.axis_size("zlo")
    rows, width = start.shape
    own = w_in.shape[0]

    following = shift_seg(start, -1)
    shard = jnp.where(core == 0, w_in, w_out)
    own_w = lax.all_to_all(jnp.broadcast_to(shard[None], (batches, own, width)), "batch", 0, 0)
    own_w = own_w.reshape(batches * own, width)
    other_w = swap(own_w)

    has_next = (place < lax.axis_size(SEG) - 1).astype(jnp.int32)
    info = jnp.stack([counts[0], core, has_next])
    ends, bar, bias, left, right = integrate(
        info, start, targets[0], following, b_in[None], own_w, other_w
    )
    previous = shift_seg(ends, 1)
    has_prev = (place > 0).astype(f32)
    grad_starts = (bar - penalty * ((previous - start) * has_prev))[None]

    received = swap(contract_rows(left[0], right[0]))
    keep = contract_rows(left[1], right[1])
    message = code(keep, received, bias, halves, batches)
    message = lax.all_to_all(message.reshape((halves * batches,) + message.shape[2:]), GROUP, 0, 0)
    mine = decode(message, width)
    four = lax.all_to_all(jnp.broadcast_to(mine[None], (4,) + mine.shape), SEG, 0, 0)
    piece = mine.shape[0] - 8
    four = four * (1.0 / math.sqrt(rows * batches))
    grad_in = jnp.concatenate([four[0, :piece], four[2, :piece]], axis=0)
    grad_out = jnp.concatenate([four[1, :piece], four[3, :piece]], axis=0)
    bias_rows = four[0, piece, :LANES] + four[1, piece, :LANES]
    offset = lax.axis_index("batch") % (LANES // own) * own
    grad_bias = lax.dynamic_slice(bias_rows, (offset,), (own,))
    return (grad_starts, grad_in, grad_out, grad_bias)


def solution(mesh):
    segs, batches = mesh.devices.shape
    finer = Mesh(mesh.devices.reshape(2, segs // 2, batches), ("zlo", "core", "batch"))
    return jax.shard_map(
        body,
        mesh=finer,
        in_specs=(
            P(SEG, "batch", None),
            P(SEG, "batch", None),
            P(SEG),
            P("batch", None),
            P(),
            P("batch", None),
        ),
        out_specs=(P(SEG, "batch", None), P("batch", None), P("batch", None), P("batch")),
        check_vma=False,
    )
```

time: 729 us -> 146 us (0.20)
  waiting for transfers between devices: 472 us -> 44.5 us
  blocking collectives: 139 us -> 39.2 us
  Pallas kernels: 0 us -> 28.2 us
  starting transfers between devices: 38.6 us -> 17.7 us
  matrix products: 27.3 us -> 9.38 us
  local copies, waits for them, and re-layouts: 20.2 us -> 4.54 us
  between operations: 15.2 us -> 1.45 us
  other arithmetic: 13.7 us -> 3.68 us
    reduce_scatter x2 -> x0, waiting for transfers between devices: 254 us -> none  [the longest x1 191 us: body(): lax.psum_scatter(scaled_out, 'batch', scatter_dimension=0, tiled=True)]
    all_gather x2 -> x0, waiting for transfers between devices: 145 us -> none  [the longest x1 73.6 us: body(): lax.all_gather(w_in, 'batch', axis=0, tiled=True)]
    unnamed x1 -> x0, blocking collectives: 79.9 us -> none
    psum x1 -> x0, blocking collectives: 58.6 us -> none  [body(): lax.psum((shares[0], shares[1], shares[2]), 'seg')]
    psum x1 -> x0, waiting for transfers between devices: 56.1 us -> none  [body(): lax.psum((shares[0], shares[1], shares[2]), 'seg')]
    all_to_all x0 -> x1, blocking collectives: none -> 39.2 us  [body(): lax.all_to_all(jnp.broadcast_to(shard[None], (batches, own, width)), 'bat...]
    all_to_all x0 -> x2, waiting for transfers between devices: none -> 33.1 us  [the longest x1 28.6 us: body(): lax.all_to_all(message.reshape((halves * batches,) + message.shape[2:]),...]
    ppermute x2 -> x4, starting transfers between devices: 38.4 us -> 8.05 us  [the longest x2 5.5 us: shift_seg(): return lax.ppermute(block, SEG, route)]
  transfers between devices with their start and end apart: 7 -> 6, of which waited for: 7 -> 4; matrix products, arithmetic and copies ran while one was open for 1% -> 4% of each run, Pallas kernels for 0% -> 1%
where the time goes in v2:
time: 146 us; the launch traced here: 149 us
  waiting for transfers between devices  44.5 us (30%)
  blocking collectives  39.2 us (27%)
  Pallas kernels  28.2 us (19%)
  starting transfers between devices  17.7 us (12%)
  matrix products  9.38 us (6%)
  local copies, waits for them, and re-layouts  4.54 us (3%)
  other arithmetic  3.68 us (3%)
    all_to_all x1, blocking collectives, body(): lax.all_to_all(jnp.broadcast_to(shard[None], (batches, own, width)), 'bat...  39.2 us
    all_to_all x1, waiting for transfers between devices, body(): lax.all_to_all(message.reshape((halves * batches,) + message.shape[2:]),...  28.6 us
    pallas_call x1, Pallas kernels, integrate(): pl.pallas_call(integrate_kernel, out_shape=(states, states, jax.ShapeDtyp...  23.3 us
    dot_general x2, matrix products, contract_rows(): lax.dot_general(left, right, (((0,), (0,)), ((), ())), preferred_element_...  9.38 us
    ppermute x2, waiting for transfers between devices, shift_seg(): return lax.ppermute(block, SEG, route)  7.84 us
    ppermute x2, starting transfers between devices, shift_seg(): return lax.ppermute(block, SEG, route)  5.5 us
    all_to_all x1, starting transfers between devices, body(): lax.all_to_all(jnp.broadcast_to(mine[None], (4,) + mine.shape), SEG, 0, 0)  4.98 us
    all_to_all x1, starting transfers between devices, body(): lax.all_to_all(message.reshape((halves * batches,) + message.shape[2:]),...  4.71 us
  transfers between devices with their start and end apart: 6, of which 4 were waited for; matrix products, arithmetic and copies ran while one was open for 4% of the time, Pallas kernels for 1%

profile of v2, /device:TPU:1, one launch (start us, length us, event | category | flops | bytes accessed | tf_op | source)
XLA Modules:
  0.0 148.7 jit_solution(6313557934409821296)
XLA Ops:
  0.6 0.0 copy-start
  0.6 0.0 copy-start.4
  0.7 0.9 broadcast_select_fusion
  1.6 0.2 broadcast_in_dim.9
  1.8 39.2 %all_to_all.15 = bf16[32,32,1024]{2,1,0:T(8,128)(2,1)S(1)} all-to-all(bf16[32,32,1024]{2,1,0:T(8,128)(2,1)S(1)} %broadcast_in_dim.9), channel_id=1, replica_groups=mesh['zlo'=2,'core'=2,'batch'=32] {'batch'}, dimensions={0} | all-to-all | bytes 4194304 | tf_op jit(solution)/shard_map/all_to_all | solution.py:263
  41.0 2.3 %collective-permute-start.1 = (bf16[1024,1024]{1,0:T(8,128)(2,1)S(1)}, bf16[1024,1024]{1,0:T(8,128)(2,1)}, u32[]{:S(2)}, u32[]{:S(2)}) collective-permute-start(bf16[1024,1024]{1,0:T(8,128)(2,1)S(1)} %bitcast.32), channel_id=1, source_target_pairs={{0,32},{32,0},{1,33},{33,1},{2,34},{34,2},{3,35},{35,3},{4,36},{36... | collective-permute-start | bytes 6291464 | tf_op jit(solution)/shard_map/ppermute | solution.py:249
  43.3 0.0 copy-done
  43.3 1.9 %collective-permute-start = (f32[128,1024]{1,0:T(8,128)S(1)}, f32[128,1024]{1,0:T(8,128)S(1)}, u32[]{:S(2)}, u32[]{:S(2)}) collective-permute-start(f32[128,1024]{1,0:T(8,128)S(1)} %bitcast.34), channel_id=1, source_target_pairs={{32,0},{64,32},{96,64},{33,1},{65,33},{97,65},{34,2},{66,34},{98,6... | collective-permute-start | bytes 1572872 | tf_op jit(solution)/shard_map/ppermute | solution.py:245
  45.9 0.1 pad_add_fusion.info
  46.0 7.8 %collective-permute-done.following = f32[128,1024]{1,0:T(8,128)S(1)} collective-permute-done((f32[128,1024]{1,0:T(8,128)S(1)}, f32[128,1024]{1,0:T(8,128)S(1)}, u32[]{:S(2)}, u32[]{:S(2)}) %collective-permute-start) | collective-permute-done | bytes 524320 | tf_op jit(solution)/shard_map/ppermute | solution.py:245
  53.8 0.8 copy-done.2
  54.6 0.0 collective-permute-done.1.other_w
  54.6 1.0 copy-done.1
  55.6 1.0 copy-done.3
  56.7 23.3 %integrate.1 = (f32[128,1024]{1,0:T(8,128)S(1)}, f32[128,1024]{1,0:T(8,128)S(1)}, f32[1,1024]{1,0:T(1,128)S(1)}, bf16[2,1536,1024]{2,1,0:T(8,128)(2,1)S(1)}, bf16[2,1536,1024]{2,1,0:T(8,128)(2,1)}) custom-call(s32[3]{0:T(128)S(1)} %pad_add_fusion.info, f32[128,1024]{1,0:T(8,128)S(1)} %bitcast.35, f32[128,1024]{1,0:T(8,128)S(1)} %bitcast.36, ...), custom_call_target="tpu_custom_call" | custom-call | tf_op jit(solution)/shard_map/integrate/pallas_call | solution.py:120
  79.9 0.0 copy-start.5
  80.0 5.8 %fusion = f32[1024,1024]{1,0:T(8,128)S(1)} fusion(bf16[2,1536,1024]{2,1,0:T(8,128)(2,1)} %get-tuple-element.12, bf16[2,1536,1024]{2,1,0:T(8,128)(2,1)S(1)} %get-tuple-element.11), kind=kOutput, calls=%fused_computation | convolution fusion | flops 3221225472 | bytes 10485760 | tf_op jit(solution)/shard_map/dot_general | solution.py:239
  85.8 0.3 collective-permute-start.3
  86.0 3.6 %fusion.3.keep = f32[1024,1024]{1,0:T(8,128)S(1)} fusion(bf16[2,1536,1024]{2,1,0:T(8,128)(2,1)S(1)} %copy-done.6, bf16[2,1536,1024]{2,1,0:T(8,128)(2,1)S(1)} %get-tuple-element.11), kind=kOutput, calls=%fused_computation.3 | convolution fusion | flops 3221225472 | bytes 10485760 | tf_op jit(solution)/shard_map/dot_general | solution.py:239
  89.6 3.5 %collective-permute-done.3.received = f32[1024,1024]{1,0:T(8,128)S(1)} collective-permute-done((f32[1024,1024]{1,0:T(8,128)S(1)}, f32[1024,1024]{1,0:T(8,128)S(1)}, u32[]{:S(2)}, u32[]{:S(2)}) %collective-permute-start.3) | collective-permute-done | bytes 4194336 | tf_op jit(solution)/shard_map/ppermute | solution.py:249
  93.2 4.1 %code.1 = s16[2,32,144,128]{3,2,1,0:T(8,128)(2,1)} custom-call(f32[1024,1024]{1,0:T(8,128)S(1)} %fusion.3.keep, f32[1024,1024]{1,0:T(8,128)S(1)} %collective-permute-done.3.received, f32[1,1024]{1,0:T(1,128)S(1)} %get-tuple-element.13.bias), custom_call_target="tpu_custom_call" | custom-call | tf_op jit(solution)/shard_map/code/pallas_call | solution.py:189
  97.2 4.7 %all-to-all-start.1 = ((s16[64,144,128]{2,1,0:T(8,128)(2,1)}), s16[64,144,128]{2,1,0:T(8,128)(2,1)S(1)}, u32[]{:S(2)}, u32[]{:S(2)}) async-start(s16[64,144,128]{2,1,0:T(8,128)(2,1)} %bitcast.11), calls=%async_computation.1 | async-start | bytes 4718592 | tf_op jit(solution)/shard_map/all_to_all | solution.py:279
  102.0 3.6 %collective-permute-start.2 = (f32[128,1024]{1,0:T(8,128)}, f32[128,1024]{1,0:T(8,128)}, u32[]{:S(2)}, u32[]{:S(2)}) collective-permute-start(f32[128,1024]{1,0:T(8,128)} %copy-done.5), channel_id=1, source_target_pairs={{0,32},{32,64},{64,96},{1,33},{33,65},{65,97},{2,34},{34,66},{66,9... | collective-permute-start | bytes 1572872 | tf_op jit(solution)/shard_map/ppermute | solution.py:245
  105.6 28.6 %all-to-all-done.1.message = s16[64,144,128]{2,1,0:T(8,128)(2,1)S(1)} async-done(((s16[64,144,128]{2,1,0:T(8,128)(2,1)}), s16[64,144,128]{2,1,0:T(8,128)(2,1)S(1)}, u32[]{:S(2)}, u32[]{:S(2)}) %all-to-all-start.1) | async-done | bytes 2359328 | tf_op jit(solution)/shard_map/all_to_all | solution.py:279
  134.2 0.9 decode.1
  135.1 0.8 broadcast_in_dim.21
  135.9 5.0 %all-to-all-start.2 = ((f32[4,24,1024]{2,1,0:T(8,128)}), f32[4,24,1024]{2,1,0:T(8,128)S(1)}, u32[]{:S(2)}, u32[]{:S(2)}) async-start(f32[4,24,1024]{2,1,0:T(8,128)} %broadcast_in_dim.21), calls=%async_computation.2 | async-start | bytes 786432 | tf_op jit(solution)/shard_map/all_to_all | solution.py:281
  140.9 0.0 collective-permute-done.2
  140.9 1.9 %subtract_bitcast_fusion = f32[1,128,1024]{2,1,0:T(8,128)} fusion(f32[128,1024]{1,0:T(8,128)S(1)} %get-tuple-element.9, f32[128,1024]{1,0:T(8,128)} %collective-permute-done.2, f32[]{:T(128)S(6)} %convert_element_type.4, f32[1,128,1024]{2,1,0:T(8,128)S(1)} %copy-done), kind=kLoop, calls=%fused_computation.10 | loop fusion | flops 393216 | bytes 2097156 | tf_op jit(solution)/shard_map/broadcast_in_dim | solution.py:274
  142.8 4.5 %all-to-all-done.2 = f32[4,24,1024]{2,1,0:T(8,128)S(1)} async-done(((f32[4,24,1024]{2,1,0:T(8,128)}), f32[4,24,1024]{2,1,0:T(8,128)S(1)}, u32[]{:S(2)}, u32[]{:S(2)}) %all-to-all-start.2) | async-done | bytes 393248 | tf_op jit(solution)/shard_map/all_to_all | solution.py:281
  147.4 0.6 dynamic-slice_bitcast_fusion
  148.0 0.7 pad_maximum_fusion
  (10 shorter events, 0.1 us)
Async XLA Ops:
  0.6 42.7 %copy-start = (f32[1,128,1024]{2,1,0:T(8,128)S(1)}, f32[1,128,1024]{2,1,0:T(8,128)}, u32[]{:S(2)}) copy-start(f32[1,128,1024]{2,1,0:T(8,128)} %param.6) | copy-start | bytes 1572868
  0.6 54.0 %copy-start.4 = (f32[1024]{0:T(1024)S(1)}, f32[1024]{0:T(1024)}, u32[]{:S(2)}) copy-start(f32[1024]{0:T(1024)} %param.10) | copy-start | bytes 12292
  41.0 13.6 %collective-permute-start.1 = (bf16[1024,1024]{1,0:T(8,128)(2,1)S(1)}, bf16[1024,1024]{1,0:T(8,128)(2,1)}, u32[]{:S(2)}, u32[]{:S(2)}) collective-permute-start(bf16[1024,1024]{1,0:T(8,128)(2,1)S(1)} %bitcast.32), channel_id=1, source_target_pairs={{0,32},{32,0},{1,33},{33,1},{2,34},{34,2},{3,35},{35,3},{4,36},{36... | collective-permute-start | bytes 6291464 | tf_op jit(solution)/shard_map/ppermute | solution.py:249
  43.3 10.5 %collective-permute-start = (f32[128,1024]{1,0:T(8,128)S(1)}, f32[128,1024]{1,0:T(8,128)S(1)}, u32[]{:S(2)}, u32[]{:S(2)}) collective-permute-start(f32[128,1024]{1,0:T(8,128)S(1)} %bitcast.34), channel_id=1, source_target_pairs={{32,0},{64,32},{96,64},{33,1},{65,33},{97,65},{34,2},{66,34},{98,6... | collective-permute-start | bytes 1572872 | tf_op jit(solution)/shard_map/ppermute | solution.py:245
  53.8 0.8 copy-start.2
  54.6 1.0 copy-start.1
  55.6 1.0 copy-start.3
  79.9 5.8 %copy-start.5 = (f32[128,1024]{1,0:T(8,128)}, f32[128,1024]{1,0:T(8,128)S(1)}, u32[]{:S(2)}) copy-start(f32[128,1024]{1,0:T(8,128)S(1)} %get-tuple-element.10) | copy-start | bytes 1572868
  80.0 6.1 %copy-start.6 = (bf16[2,1536,1024]{2,1,0:T(8,128)(2,1)S(1)}, bf16[2,1536,1024]{2,1,0:T(8,128)(2,1)}, u32[]{:S(2)}) copy-start(bf16[2,1536,1024]{2,1,0:T(8,128)(2,1)} %get-tuple-element.12) | copy-start | bytes 18874372
  85.8 7.4 %collective-permute-start.3 = (f32[1024,1024]{1,0:T(8,128)S(1)}, f32[1024,1024]{1,0:T(8,128)S(1)}, u32[]{:S(2)}, u32[]{:S(2)}) collective-permute-start(f32[1024,1024]{1,0:T(8,128)S(1)} %fusion), channel_id=1, source_target_pairs={{0,32},{32,0},{1,33},{33,1},{2,34},{34,2},{3,35},{35,3},{4,36},{36... | collective-permute-start | bytes 12582920 | tf_op jit(solution)/shard_map/ppermute | solution.py:249
  97.2 36.9 %all-to-all-start.1 = ((s16[64,144,128]{2,1,0:T(8,128)(2,1)}), s16[64,144,128]{2,1,0:T(8,128)(2,1)S(1)}, u32[]{:S(2)}, u32[]{:S(2)}) async-start(s16[64,144,128]{2,1,0:T(8,128)(2,1)} %bitcast.11), calls=%async_computation.1 | async-start | bytes 4718592 | tf_op jit(solution)/shard_map/all_to_all | solution.py:279
  102.0 38.9 %collective-permute-start.2 = (f32[128,1024]{1,0:T(8,128)}, f32[128,1024]{1,0:T(8,128)}, u32[]{:S(2)}, u32[]{:S(2)}) collective-permute-start(f32[128,1024]{1,0:T(8,128)} %copy-done.5), channel_id=1, source_target_pairs={{0,32},{32,64},{64,96},{1,33},{33,65},{65,97},{2,34},{34,66},{66,9... | collective-permute-start | bytes 1572872 | tf_op jit(solution)/shard_map/ppermute | solution.py:245
  135.9 11.4 %all-to-all-start.2 = ((f32[4,24,1024]{2,1,0:T(8,128)}), f32[4,24,1024]{2,1,0:T(8,128)S(1)}, u32[]{:S(2)}, u32[]{:S(2)}) async-start(f32[4,24,1024]{2,1,0:T(8,128)} %broadcast_in_dim.21), calls=%async_computation.2 | async-start | bytes 786432 | tf_op jit(solution)/shard_map/all_to_all | solution.py:281

commit v3 on v2

--- a/solution.py
+++ b/solution.py
@@ -1,3 +1,4 @@
+import functools
 import math
 
 import jax
@@ -6,6 +7,7 @@
 from jax.experimental import pallas as pl
 from jax.experimental.pallas import tpu as pltpu
 from jax.sharding import Mesh, PartitionSpec as P
+
 
 MAXSTEP = 3
 STAGES = 4
@@ -16,7 +18,7 @@
 f32 = jnp.float32
 bf16 = jnp.bfloat16
 LANES = 128
-HEAD = 16
+HEAD = 8
 TOP = 32767.0
 VMEM = pl.BlockSpec(memory_space=pltpu.VMEM)
 ANY = pl.BlockSpec(memory_space=pl.ANY)
@@ -28,19 +30,20 @@
 
 
 def integrate_kernel(
-    info, start, target, following, bias_in, own_w, other_w,
+    info, given, bias_in, own_w, other_w,
     ends, bar, bias, left, right,
     w, w_turned, state, tanhs, total, sems,
 ):
     count, core, has_next = info[0], info[1], info[2].astype(f32)
     slot_in = 1 - core
     slot_out = core
-    rows = start.shape[0]
+    rows = state.shape[0]
+    middle = right.shape[3]
     first = pltpu.make_async_copy(own_w, w.at[core], sems.at[0])
     second = pltpu.make_async_copy(other_w, w.at[1 - core], sems.at[1])
     first.start()
     second.start()
-    state[...] = start[...]
+    state[...] = given[0]
     bias[...] = jnp.zeros_like(bias)
     offset = bias_in[...]
     first.wait()
@@ -62,12 +65,14 @@
 
     def field_back(q, at):
         outer = q.astype(bf16)
-        right[slot_out, place(at), :] = outer
+        right[slot_out, 0, place(at), :] = outer[:, :middle]
+        right[slot_out, 1, place(at), :] = outer[:, middle:]
         hidden = tanhs[at]
         inner = product(outer, w_turned[1]) * (1.0 - hidden * hidden)
         bias[...] += jnp.sum(inner, axis=0, keepdims=True)
         low = inner.astype(bf16)
-        right[slot_in, place(at), :] = low
+        right[slot_in, 0, place(at), :] = low[:, :middle]
+        right[slot_in, 1, place(at), :] = low[:, middle:]
         return product(low, w_turned[0])
 
     def forward(s, carry):
@@ -85,7 +90,7 @@
     lax.fori_loop(0, count, forward, 0)
     end = state[...]
     ends[...] = end
-    state[...] = (end - target[...]) + penalty * ((end - following[...]) * has_next)
+    state[...] = (end - given[1]) + penalty * ((end - given[2]) * has_next)
 
     def backward(turn, carry):
         at = STAGES * (count - 1 - turn)
@@ -106,21 +111,24 @@
         block = pl.ds(pl.multiple_of(s * STAGES * rows, STAGES * rows), STAGES * rows)
         for slot in range(2):
             left[slot, block, :] = jnp.zeros((STAGES * rows, left.shape[2]), bf16)
-            right[slot, block, :] = jnp.zeros((STAGES * rows, right.shape[2]), bf16)
+            for half in range(2):
+                right[slot, half, block, :] = jnp.zeros((STAGES * rows, middle), bf16)
         return carry
 
     lax.fori_loop(count, MAXSTEP, clear, 0)
 
 
-def integrate(info, start, target, following, bias_in, own_w, other_w):
-    rows, width = start.shape
+def integrate(info, given, bias_in, own_w, other_w):
+    _, rows, width = given.shape
     depth = own_w.shape[1]
-    factors = jax.ShapeDtypeStruct((2, MAXSTEP * STAGES * rows, width), bf16)
+    terms = MAXSTEP * STAGES * rows
+    lefts = jax.ShapeDtypeStruct((2, terms, width), bf16)
+    rights = jax.ShapeDtypeStruct((2, 2, terms, width // 2), bf16)
     states = jax.ShapeDtypeStruct((rows, width), f32)
     return pl.pallas_call(
         integrate_kernel,
-        out_shape=(states, states, jax.ShapeDtypeStruct((1, depth), f32), factors, factors),
-        in_specs=[SMEM] + [VMEM] * 4 + [ANY] * 2,
+        out_shape=(states, states, jax.ShapeDtypeStruct((1, depth), f32), lefts, rights),
+        in_specs=[SMEM] + [VMEM] * 2 + [ANY] * 2,
         out_specs=(VMEM,) * 5,
         scratch_shapes=[
             pltpu.VMEM((2, width, depth), bf16),
@@ -130,9 +138,9 @@
             pltpu.VMEM((rows, width), f32),
             pltpu.SemaphoreType.DMA((2,)),
         ],
-        compiler_params=pltpu.CompilerParams(vmem_limit_bytes=40 * 1024 * 1024),
+        compiler_params=pltpu.CompilerParams(vmem_limit_bytes=32 * 1024 * 1024),
         name="integrate",
-    )(info, start, target, following, bias_in, own_w, other_w)
+    )(info, given, bias_in, own_w, other_w)
 
 
 def level_of(peak):
@@ -151,55 +159,64 @@
     return jnp.round(values).astype(jnp.int32).astype(jnp.int16)
 
 
-def code_kernel(keep, received, bias, message):
-    halves, owners, height, _ = message.shape
-    piece = keep.shape[0] // (halves * owners)
-    blocks = keep.shape[1] // LANES
+def code_kernel(keep_low, keep_high, received_low, received_high, bias, message):
+    halves, owners, _, _ = message.shape
+    piece = keep_low.shape[0] // (halves * owners)
+    shared = keep_low.shape[1] // LANES
+    blocks = 2 * shared
     row = lax.broadcasted_iota(jnp.int32, (HEAD, LANES), 0)
     bias_now = bias[...]
     bias_level = level_of(jnp.abs(bias_now))
     bias_steps = bias_now * steps_of(bias_level)
     bias_high = jnp.round(bias_steps)
     bias_low = (bias_steps - bias_high) * TOP
-    base = jnp.where(row == 8, bias_level, 0.0)
-    base = jnp.where(row == 9, bias_high, base)
-    base = jnp.where(row == 10, bias_low, base)
+    head = jnp.where(row == shared, bias_level, 0.0)
+    head = jnp.where(row == shared + 1, bias_high, head)
+    head = jnp.where(row == shared + 2, bias_low, head)
+    for block in range(shared):
+        columns = pl.ds(block * LANES, LANES)
+        pair = (
+            keep_low[:, columns] + received_low[:, columns],
+            keep_high[:, columns] + received_high[:, columns],
+        )
+        peak = jnp.maximum(jnp.abs(pair[0]), jnp.abs(pair[1]))
+        level = level_of(jnp.max(peak, axis=0, keepdims=True))
+        steps = steps_of(level)
+        head = jnp.where(row == block, level, head)
+        for part, values in zip((block, block + shared), pair):
+            numbers = whole(values * steps)
+            for owner in range(owners):
+                for half in range(halves):
+                    at = (owner * halves + half) * piece
+                    message[half, owner, pl.ds(part * piece, piece), :] = numbers[at : at + piece]
+    numbers = whole(head)
     for owner in range(owners):
         for half in range(halves):
-            at = (owner * halves + half) * piece
-            head = base
-            for block in range(blocks):
-                columns = pl.ds(block * LANES, LANES)
-                values = keep[pl.ds(at, piece), columns] + received[pl.ds(at, piece), columns]
-                level = level_of(jnp.max(jnp.abs(values), axis=0, keepdims=True))
-                head = jnp.where(row == block, level, head)
-                message[half, owner, pl.ds(block * piece, piece), :] = whole(
-                    values * steps_of(level)
-                )
-            message[half, owner, pl.ds(blocks * piece, HEAD), :] = whole(head)
+            message[half, owner, pl.ds(blocks * piece, HEAD), :] = numbers
 
 
 def code(keep, received, bias, halves, batches):
-    depth, width = keep.shape
+    depth, width = keep[0].shape[0], 2 * keep[0].shape[1]
     steps = width // LANES
     owners = batches // steps
     piece = depth // (halves * batches)
     height = piece * steps + HEAD
-    block = pl.BlockSpec((depth // steps, width), lambda i: (i, 0))
     return pl.pallas_call(
         code_kernel,
         grid=(steps,),
         out_shape=jax.ShapeDtypeStruct((halves, batches, height, LANES), jnp.int16),
-        in_specs=[block, block, pl.BlockSpec((1, LANES), lambda i: (0, i))],
+        in_specs=[pl.BlockSpec((depth // steps, width // 2), lambda i: (i, 0))] * 4
+        + [pl.BlockSpec((1, LANES), lambda i: (0, i))],
         out_specs=pl.BlockSpec((halves, owners, height, LANES), lambda i: (0, i, 0, 0)),
         compiler_params=pltpu.CompilerParams(vmem_limit_bytes=16 * 1024 * 1024),
         name="code",
-    )(keep, received, bias)
+    )(*keep, *received, bias)
 
 
 def decode_kernel(message, out):
     senders, height, _ = message.shape
     blocks = out.shape[1] // LANES
+    shared = blocks // 2
     piece = (height - HEAD) // blocks
 
     @pl.when(pl.program_id(0) == 0)
@@ -211,10 +228,12 @@
     for sender in range(senders):
         head = message[sender, pl.ds(blocks * piece, HEAD), :].astype(jnp.int32).astype(f32)
         scale = scale_of(head)
-        bias += (head[9:10] + head[10:11] * (1.0 / TOP)) * scale[8:9]
+        high, low = head[shared + 1 : shared + 2], head[shared + 2 : shared + 3]
+        bias += (high + low * (1.0 / TOP)) * scale[shared : shared + 1]
         for block in range(blocks):
             data = message[sender, pl.ds(block * piece, piece), :].astype(jnp.int32).astype(f32)
-            sums[block] += data * scale[block : block + 1]
+            at = block % shared
+            sums[block] += data * scale[at : at + 1]
     for block in range(blocks):
         out[pl.ds(0, piece), pl.ds(block * LANES, LANES)] += sums[block]
     out[pl.ds(piece, 8), pl.ds(0, LANES)] += jnp.broadcast_to(bias, (8, LANES))
@@ -235,6 +254,44 @@
     )(message)
 
 
+def lay_out_kernel(scale, info, mine, by_core, by_zlo, by_both, grad_in, grad_out, grad_bias):
+    core, zlo, offset = info[0], info[1], info[2]
+    piece = mine.shape[0] - 8
+    here = pl.ds(pl.multiple_of(zlo * piece, piece), piece)
+    there = pl.ds(pl.multiple_of((1 - zlo) * piece, piece), piece)
+    rows = pl.ds(0, piece)
+
+    def fill(kept, other):
+        kept[here, :] = mine[rows, :] * scale
+        kept[there, :] = by_zlo[rows, :] * scale
+        other[here, :] = by_core[rows, :] * scale
+        other[there, :] = by_both[rows, :] * scale
+
+    @pl.when(core == 0)
+    def _():
+        fill(grad_in, grad_out)
+
+    @pl.when(core == 1)
+    def _():
+        fill(grad_out, grad_in)
+
+    stretch = (mine[pl.ds(piece, 8), pl.ds(0, LANES)] + by_core[pl.ds(piece, 8), pl.ds(0, LANES)]) * scale
+    grad_bias[...] = pltpu.roll(stretch, LANES - offset, 1)
+
+
+def lay_out(scale, info, *quarters):
+    rows, width = quarters[0].shape
+    gradient = jax.ShapeDtypeStruct((2 * (rows - 8), width), f32)
+    return pl.pallas_call(
+        functools.partial(lay_out_kernel, scale),
+        out_shape=(gradient, gradient, jax.ShapeDtypeStruct((8, LANES), f32)),
+        in_specs=[SMEM] + [VMEM] * 4,
+        out_specs=(VMEM,) * 3,
+        compiler_params=pltpu.CompilerParams(vmem_limit_bytes=8 * 1024 * 1024),
+        name="lay_out",
+    )(info, *quarters)
+
+
 def contract_rows(left, right):
     return lax.dot_general(left, right, (((0,), (0,)), ((), ())), preferred_element_type=f32)
 
@@ -260,33 +317,36 @@
 
     following = shift_seg(start, -1)
     shard = jnp.where(core == 0, w_in, w_out)
-    own_w = lax.all_to_all(jnp.broadcast_to(shard[None], (batches, own, width)), "batch", 0, 0)
+    copies = jnp.broadcast_to(shard[None], (batches, own, width))
+    own_w = lax.all_to_all(copies, "batch", 0, 0)
     own_w = own_w.reshape(batches * own, width)
     other_w = swap(own_w)
+    given = jnp.stack([start, targets[0], following])
 
     has_next = (place < lax.axis_size(SEG) - 1).astype(jnp.int32)
     info = jnp.stack([counts[0], core, has_next])
-    ends, bar, bias, left, right = integrate(
-        info, start, targets[0], following, b_in[None], own_w, other_w
-    )
+    ends, bar, bias, left, right = integrate(info, given, b_in[None], own_w, other_w)
     previous = shift_seg(ends, 1)
     has_prev = (place > 0).astype(f32)
     grad_starts = (bar - penalty * ((previous - start) * has_prev))[None]
 
-    received = swap(contract_rows(left[0], right[0]))
-    keep = contract_rows(left[1], right[1])
+    received, keep = [], []
+    for half in range(2):
+        sent = contract_rows(left[0], right[0, half])
+        received.append(swap(sent))
+    for half in range(2):
+        keep.append(contract_rows(left[1], right[1, half]))
     message = code(keep, received, bias, halves, batches)
     message = lax.all_to_all(message.reshape((halves * batches,) + message.shape[2:]), GROUP, 0, 0)
     mine = decode(message, width)
-    four = lax.all_to_all(jnp.broadcast_to(mine[None], (4,) + mine.shape), SEG, 0, 0)
-    piece = mine.shape[0] - 8
-    four = four * (1.0 / math.sqrt(rows * batches))
-    grad_in = jnp.concatenate([four[0, :piece], four[2, :piece]], axis=0)
-    grad_out = jnp.concatenate([four[1, :piece], four[3, :piece]], axis=0)
-    bias_rows = four[0, piece, :LANES] + four[1, piece, :LANES]
+    quarters = [mine] + [
+        lax.ppermute(mine, SEG, [(i, i ^ flip) for i in range(4)]) for flip in (1, 2, 3)
+    ]
     offset = lax.axis_index("batch") % (LANES // own) * own
-    grad_bias = lax.dynamic_slice(bias_rows, (offset,), (own,))
-    return (grad_starts, grad_in, grad_out, grad_bias)
+    places = jnp.stack([core, lax.axis_index("zlo"), offset])
+    scale = 1.0 / math.sqrt(rows * batches)
+    grad_in, grad_out, grad_bias = lay_out(scale, places, *quarters)
+    return (grad_starts, grad_in, grad_out, grad_bias[0, :own])
 
 
 def solution(mesh):

time: 146 us -> 135 us (0.925); the launches traced: 149 us -> 135 us
  Pallas kernels: 28.2 us -> 15.6 us
  starting transfers between devices: 17.7 us -> 26.8 us
  waiting for transfers between devices: 44.5 us -> 39.3 us
  local copies, waits for them, and re-layouts: 4.54 us -> 0.78 us
  matrix products: 9.38 us -> 7.28 us
    pallas_call x1, Pallas kernels: 23.3 us -> 9.86 us  [integrate(): pl.pallas_call(integrate_kernel, out_shape=(states, states, jax.ShapeDtyp...]
    ppermute x2 -> x3, starting transfers between devices: 2.55 us -> 7.79 us  [swap(): return lax.ppermute(block, 'core', [(0, 1), (1, 0)])]
    all_to_all x1, starting transfers between devices: 4.71 us -> 9.82 us  [body(): lax.all_to_all(message.reshape((halves * batches,) + message.shape[2:]),...]
    all_to_all x1 -> x0, starting transfers between devices: 4.98 us -> none  [body(): lax.all_to_all(jnp.broadcast_to(mine[None], (4,) + mine.shape), SEG, 0, 0)]
    all_to_all x1 -> x0, waiting for transfers between devices: 4.51 us -> none  [body(): lax.all_to_all(jnp.broadcast_to(mine[None], (4,) + mine.shape), SEG, 0, 0)]
    ppermute x0 -> x3, starting transfers between devices: none -> 3.46 us  [body(): lax.ppermute(mine, SEG, [(i, i ^ flip) for i in range(4)])]
    unnamed x14 -> x8, local copies, waits for them, and re-layouts: 2.9 us -> 0.02 us
    all_to_all x1, waiting for transfers between devices: 28.6 us -> 26.4 us  [body(): lax.all_to_all(message.reshape((halves * batches,) + message.shape[2:]),...]
  transfers between devices with their start and end apart: 6 -> 9, of which waited for: 4 -> 4; matrix products, arithmetic and copies ran while one was open for 4% -> 5% of each run, Pallas kernels for 1% -> 1%
where the time goes in v3:
time: 135 us
  blocking collectives  39.3 us (29%)
  waiting for transfers between devices  39.3 us (29%)
  starting transfers between devices  26.8 us (20%)
  Pallas kernels  15.6 us (12%)
  matrix products  7.28 us (5%)
  other arithmetic  4.11 us (3%)
  between operations  1.44 us (1%)
    all_to_all x1, blocking collectives, body(): own_w = lax.all_to_all(copies, 'batch', 0, 0)  39.3 us
    all_to_all x1, waiting for transfers between devices, body(): lax.all_to_all(message.reshape((halves * batches,) + message.shape[2:]),...  26.4 us
    pallas_call x1, Pallas kernels, integrate(): pl.pallas_call(integrate_kernel, out_shape=(states, states, jax.ShapeDtyp...  9.86 us
    all_to_all x1, starting transfers between devices, body(): lax.all_to_all(message.reshape((halves * batches,) + message.shape[2:]),...  9.82 us
    ppermute x2, waiting for transfers between devices, shift_seg(): return lax.ppermute(block, SEG, route)  7.94 us
    ppermute x3, starting transfers between devices, swap(): return lax.ppermute(block, 'core', [(0, 1), (1, 0)])  7.79 us
    dot_general x4, matrix products, contract_rows(): lax.dot_general(left, right, (((0,), (0,)), ((), ())), preferred_element_...  7.28 us
    ppermute x2, starting transfers between devices, shift_seg(): return lax.ppermute(block, SEG, route)  5.75 us
  transfers between devices with their start and end apart: 9, of which 4 were waited for; matrix products, arithmetic and copies ran while one was open for 5% of the time, Pallas kernels for 1%

profile of v3, /device:TPU:1, one launch (start us, length us, event | category | flops | bytes accessed | tf_op | source)
XLA Modules:
  0.0 134.7 jit_solution(14139033239575557085)
XLA Ops:
  0.6 0.9 broadcast_select_fusion
  1.5 0.2 broadcast_in_dim.13
  1.8 0.0 copy-start.1
  1.8 0.0 copy-start.3
  1.8 39.3 %all_to_all.10 = bf16[32,32,1024]{2,1,0:T(8,128)(2,1)S(1)} all-to-all(bf16[32,32,1024]{2,1,0:T(8,128)(2,1)S(1)} %broadcast_in_dim.13), channel_id=1, replica_groups=mesh['zlo'=2,'core'=2,'batch'=32] {'batch'}, dimensions={0} | all-to-all | bytes 4194304 | tf_op jit(solution)/shard_map/all_to_all | solution.py:321
  41.1 2.3 %collective-permute-start.1 = (bf16[1024,1024]{1,0:T(8,128)(2,1)S(1)}, bf16[1024,1024]{1,0:T(8,128)(2,1)}, u32[]{:S(2)}, u32[]{:S(2)}) collective-permute-start(bf16[1024,1024]{1,0:T(8,128)(2,1)S(1)} %bitcast.36), channel_id=1, source_target_pairs={{0,32},{32,0},{1,33},{33,1},{2,34},{34,2},{3,35},{35,3},{4,36},{36... | collective-permute-start | bytes 6291464 | tf_op jit(solution)/shard_map/ppermute | solution.py:306
  43.4 1.9 %collective-permute-start = (f32[128,1024]{1,0:T(8,128)S(1)}, f32[128,1024]{1,0:T(8,128)}, u32[]{:S(2)}, u32[]{:S(2)}) collective-permute-start(f32[128,1024]{1,0:T(8,128)S(1)} %bitcast.39), channel_id=1, source_target_pairs={{32,0},{64,32},{96,64},{33,1},{65,33},{97,65},{34,2},{66,34},{98,6... | collective-permute-start | bytes 1572872 | tf_op jit(solution)/shard_map/ppermute | solution.py:302
  46.0 0.1 pad_add_fusion.info
  46.0 7.9 %collective-permute-done = f32[128,1024]{1,0:T(8,128)} collective-permute-done((f32[128,1024]{1,0:T(8,128)S(1)}, f32[128,1024]{1,0:T(8,128)}, u32[]{:S(2)}, u32[]{:S(2)}) %collective-permute-start) | collective-permute-done | bytes 524320 | tf_op jit(solution)/shard_map/ppermute | solution.py:302
  54.0 1.2 pad_maximum_fusion.given
  55.2 9.9 %integrate.1 = (f32[128,1024]{1,0:T(8,128)S(1)}, f32[128,1024]{1,0:T(8,128)S(1)}, f32[1,1024]{1,0:T(1,128)S(1)}, bf16[2,1536,1024]{2,1,0:T(8,128)(2,1)S(1)}, bf16[2,2,1536,512]{3,2,1,0:T(8,128)(2,1)S(1)}) custom-call(s32[3]{0:T(128)S(1)} %pad_add_fusion.info, f32[3,128,1024]{2,1,0:T(8,128)S(1)} %pad_maximum_fusion.given, f32[1,1024]{1,0:T(1,128)S(1)} %bitcast.38, ...), custom_call_target="tpu_custom_call" | custom-call | tf_op jit(solution)/shard_map/integrate/pallas_call | solution.py:128
  65.0 1.8 %fusion = f32[1024,512]{1,0:T(8,128)S(1)} fusion(bf16[2,1536,1024]{2,1,0:T(8,128)(2,1)S(1)} %get-tuple-element.14, bf16[2,2,1536,512]{3,2,1,0:T(8,128)(2,1)S(1)} %get-tuple-element.15), kind=kOutput, calls=%fused_computation | convolution fusion | flops 1610612736 | bytes 6815744 | tf_op jit(solution)/shard_map/dot_general | solution.py:296
  66.9 1.8 %fusion.2 = f32[1024,512]{1,0:T(8,128)S(1)} fusion(bf16[2,1536,1024]{2,1,0:T(8,128)(2,1)S(1)} %get-tuple-element.14, bf16[2,2,1536,512]{3,2,1,0:T(8,128)(2,1)S(1)} %get-tuple-element.15), kind=kOutput, calls=%fused_computation.2 | convolution fusion | flops 1610612736 | bytes 6815744 | tf_op jit(solution)/shard_map/dot_general | solution.py:296
  68.7 5.2 %collective-permute-start.3 = (f32[1024,512]{1,0:T(8,128)S(1)}, f32[1024,512]{1,0:T(8,128)S(1)}, u32[]{:S(2)}, u32[]{:S(2)}) collective-permute-start(f32[1024,512]{1,0:T(8,128)S(1)} %fusion.2), channel_id=1, source_target_pairs={{0,32},{32,0},{1,33},{33,1},{2,34},{34,2},{3,35},{35,3},{4,36},{36... | collective-permute-start | bytes 6291464 | tf_op jit(solution)/shard_map/ppermute | solution.py:306
  73.9 0.3 collective-permute-start.4
  74.2 1.8 %fusion.4.keep_high = f32[1024,512]{1,0:T(8,128)S(1)} fusion(bf16[2,1536,1024]{2,1,0:T(8,128)(2,1)S(1)} %get-tuple-element.14, bf16[2,2,1536,512]{3,2,1,0:T(8,128)(2,1)S(1)} %get-tuple-element.15), kind=kOutput, calls=%fused_computation.4 | convolution fusion | flops 1610612736 | bytes 6815744 | tf_op jit(solution)/shard_map/dot_general | solution.py:296
  76.0 1.8 %fusion.6.keep_low = f32[1024,512]{1,0:T(8,128)S(1)} fusion(bf16[2,1536,1024]{2,1,0:T(8,128)(2,1)S(1)} %get-tuple-element.14, bf16[2,2,1536,512]{3,2,1,0:T(8,128)(2,1)S(1)} %get-tuple-element.15), kind=kOutput, calls=%fused_computation.6 | convolution fusion | flops 1610612736 | bytes 6815744 | tf_op jit(solution)/shard_map/dot_general | solution.py:296
  77.9 2.9 %collective-permute-done.4.received_high = f32[1024,512]{1,0:T(8,128)S(1)} collective-permute-done((f32[1024,512]{1,0:T(8,128)S(1)}, f32[1024,512]{1,0:T(8,128)S(1)}, u32[]{:S(2)}, u32[]{:S(2)}) %collective-permute-start.4) | collective-permute-done | bytes 2097184 | tf_op jit(solution)/shard_map/ppermute | solution.py:306
  80.7 3.7 %code.1 = s16[2,32,136,128]{3,2,1,0:T(8,128)(2,1)} custom-call(f32[1024,512]{1,0:T(8,128)S(1)} %fusion.6.keep_low, f32[1024,512]{1,0:T(8,128)S(1)} %fusion.4.keep_high, f32[1024,512]{1,0:T(8,128)S(1)} %collective-permute-done.3.received_low, f32[1024,512]{1,0:T(8,128)S(1)} %collective-permute-done.4.received_high, f32[1,1024]{1,0:T(1,128)S(1)} %get-tuple-element.16.bias), custom_call_target="tpu_custom_call" | custom-call | tf_op jit(solution)/shard_map/code/pallas_call | solution.py:204
  84.4 9.8 %all-to-all-start.1 = ((s16[64,136,128]{2,1,0:T(8,128)(2,1)}), s16[64,136,128]{2,1,0:T(8,128)(2,1)S(1)}, u32[]{:S(2)}, u32[]{:S(2)}) async-start(s16[64,136,128]{2,1,0:T(8,128)(2,1)} %bitcast.15), calls=%async_computation.1 | async-start | bytes 4456448 | tf_op jit(solution)/shard_map/all_to_all | solution.py:340
  94.2 3.8 %collective-permute-start.2 = (f32[128,1024]{1,0:T(8,128)S(1)}, f32[128,1024]{1,0:T(8,128)}, u32[]{:S(2)}, u32[]{:S(2)}) collective-permute-start(f32[128,1024]{1,0:T(8,128)S(1)} %get-tuple-element.13), channel_id=1, source_target_pairs={{0,32},{32,64},{64,96},{1,33},{33,65},{65,97},{2,34},{34,66},{66,9... | collective-permute-start | bytes 1572872 | tf_op jit(solution)/shard_map/ppermute | solution.py:302
  98.1 0.1 pad_add_fusion.1.info
  98.2 26.4 %all-to-all-done.1.message = s16[64,136,128]{2,1,0:T(8,128)(2,1)S(1)} async-done(((s16[64,136,128]{2,1,0:T(8,128)(2,1)}), s16[64,136,128]{2,1,0:T(8,128)(2,1)S(1)}, u32[]{:S(2)}, u32[]{:S(2)}) %all-to-all-start.1) | async-done | bytes 2228256 | tf_op jit(solution)/shard_map/all_to_all | solution.py:340
  124.5 0.8 decode.1.mine
  125.3 1.7 %collective-permute-start.7 = (f32[24,1024]{1,0:T(8,128)S(1)}, f32[24,1024]{1,0:T(8,128)S(1)}, u32[]{:S(2)}, u32[]{:S(2)}) collective-permute-start(f32[24,1024]{1,0:T(8,128)S(1)} %decode.1.mine), channel_id=1, source_target_pairs={{0,96},{32,64},{64,32},{96,0},{1,97},{33,65},{65,33},{97,1},{2,98}... | collective-permute-start | bytes 294920 | tf_op jit(solution)/shard_map/ppermute | solution.py:343
  127.1 1.7 %collective-permute-start.6 = (f32[24,1024]{1,0:T(8,128)S(1)}, f32[24,1024]{1,0:T(8,128)S(1)}, u32[]{:S(2)}, u32[]{:S(2)}) collective-permute-start(f32[24,1024]{1,0:T(8,128)S(1)} %decode.1.mine), channel_id=1, source_target_pairs={{0,64},{32,96},{64,0},{96,32},{1,65},{33,97},{65,1},{97,33},{2,66}... | collective-permute-start | bytes 294920 | tf_op jit(solution)/shard_map/ppermute | solution.py:343
  128.8 0.0 collective-permute-done.2
  128.8 1.9 %subtract_bitcast_fusion = f32[1,128,1024]{2,1,0:T(8,128)} fusion(f32[128,1024]{1,0:T(8,128)S(1)} %get-tuple-element.12, f32[128,1024]{1,0:T(8,128)} %collective-permute-done.2, f32[]{:T(128)S(6)} %convert_element_type.4, f32[1,128,1024]{2,1,0:T(8,128)S(1)} %copy-done.2), kind=kLoop, calls=%fused_computation.21 | loop fusion | flops 393216 | bytes 2097156 | tf_op jit(solution)/shard_map/broadcast_in_dim | solution.py:331
  130.8 2.2 %collective-permute-done.6.by_zlo = f32[24,1024]{1,0:T(8,128)S(1)} collective-permute-done((f32[24,1024]{1,0:T(8,128)S(1)}, f32[24,1024]{1,0:T(8,128)S(1)}, u32[]{:S(2)}, u32[]{:S(2)}) %collective-permute-start.6) | collective-permute-done | bytes 98336 | tf_op jit(solution)/shard_map/ppermute | solution.py:343
  132.9 0.0 collective-permute-done.5.by_core
  132.9 1.3 lay_out.1
  134.2 0.5 slice_bitcast_fusion
  (10 shorter events, 0.0 us)
Async XLA Ops:
  1.8 41.6 %copy-start.1 = (f32[1,128,1024]{2,1,0:T(8,128)S(1)}, f32[1,128,1024]{2,1,0:T(8,128)}, u32[]{:S(2)}) copy-start(f32[1,128,1024]{2,1,0:T(8,128)} %param.6) | copy-start | bytes 1572868
  1.8 52.2 %copy-start.3 = (f32[1,128,1024]{2,1,0:T(8,128)S(1)}, f32[1,128,1024]{2,1,0:T(8,128)}, u32[]{:S(2)}) copy-start(f32[1,128,1024]{2,1,0:T(8,128)} %param.7) | copy-start | bytes 1572868
  41.1 14.1 %copy-start = (f32[1024]{0:T(1024)S(1)}, f32[1024]{0:T(1024)}, u32[]{:S(2)}) copy-start(f32[1024]{0:T(1024)} %param.10) | copy-start | bytes 12292
  41.1 14.1 %collective-permute-start.1 = (bf16[1024,1024]{1,0:T(8,128)(2,1)S(1)}, bf16[1024,1024]{1,0:T(8,128)(2,1)}, u32[]{:S(2)}, u32[]{:S(2)}) collective-permute-start(bf16[1024,1024]{1,0:T(8,128)(2,1)S(1)} %bitcast.36), channel_id=1, source_target_pairs={{0,32},{32,0},{1,33},{33,1},{2,34},{34,2},{3,35},{35,3},{4,36},{36... | collective-permute-start | bytes 6291464 | tf_op jit(solution)/shard_map/ppermute | solution.py:306
  43.4 10.6 %collective-permute-start = (f32[128,1024]{1,0:T(8,128)S(1)}, f32[128,1024]{1,0:T(8,128)}, u32[]{:S(2)}, u32[]{:S(2)}) collective-permute-start(f32[128,1024]{1,0:T(8,128)S(1)} %bitcast.39), channel_id=1, source_target_pairs={{32,0},{64,32},{96,64},{33,1},{65,33},{97,65},{34,2},{66,34},{98,6... | collective-permute-start | bytes 1572872 | tf_op jit(solution)/shard_map/ppermute | solution.py:302
  68.7 9.2 %collective-permute-start.3 = (f32[1024,512]{1,0:T(8,128)S(1)}, f32[1024,512]{1,0:T(8,128)S(1)}, u32[]{:S(2)}, u32[]{:S(2)}) collective-permute-start(f32[1024,512]{1,0:T(8,128)S(1)} %fusion.2), channel_id=1, source_target_pairs={{0,32},{32,0},{1,33},{33,1},{2,34},{34,2},{3,35},{35,3},{4,36},{36... | collective-permute-start | bytes 6291464 | tf_op jit(solution)/shard_map/ppermute | solution.py:306
  73.9 6.8 %collective-permute-start.4 = (f32[1024,512]{1,0:T(8,128)S(1)}, f32[1024,512]{1,0:T(8,128)S(1)}, u32[]{:S(2)}, u32[]{:S(2)}) collective-permute-start(f32[1024,512]{1,0:T(8,128)S(1)} %fusion), channel_id=1, source_target_pairs={{0,32},{32,0},{1,33},{33,1},{2,34},{34,2},{3,35},{35,3},{4,36},{36... | collective-permute-start | bytes 6291464 | tf_op jit(solution)/shard_map/ppermute | solution.py:306
  84.4 40.1 %all-to-all-start.1 = ((s16[64,136,128]{2,1,0:T(8,128)(2,1)}), s16[64,136,128]{2,1,0:T(8,128)(2,1)S(1)}, u32[]{:S(2)}, u32[]{:S(2)}) async-start(s16[64,136,128]{2,1,0:T(8,128)(2,1)} %bitcast.15), calls=%async_computation.1 | async-start | bytes 4456448 | tf_op jit(solution)/shard_map/all_to_all | solution.py:340
  94.2 34.6 %collective-permute-start.2 = (f32[128,1024]{1,0:T(8,128)S(1)}, f32[128,1024]{1,0:T(8,128)}, u32[]{:S(2)}, u32[]{:S(2)}) collective-permute-start(f32[128,1024]{1,0:T(8,128)S(1)} %get-tuple-element.13), channel_id=1, source_target_pairs={{0,32},{32,64},{64,96},{1,33},{33,65},{65,97},{2,34},{34,66},{66,9... | collective-permute-start | bytes 1572872 | tf_op jit(solution)/shard_map/ppermute | solution.py:302
  124.5 4.3 %copy-start.2 = (f32[1,128,1024]{2,1,0:T(8,128)S(1)}, f32[1,128,1024]{2,1,0:T(8,128)}, u32[]{:S(2)}) copy-start(f32[1,128,1024]{2,1,0:T(8,128)} %param.6) | copy-start | bytes 1572868
  125.3 5.4 %collective-permute-start.7 = (f32[24,1024]{1,0:T(8,128)S(1)}, f32[24,1024]{1,0:T(8,128)S(1)}, u32[]{:S(2)}, u32[]{:S(2)}) collective-permute-start(f32[24,1024]{1,0:T(8,128)S(1)} %decode.1.mine), channel_id=1, source_target_pairs={{0,96},{32,64},{64,32},{96,0},{1,97},{33,65},{65,33},{97,1},{2,98}... | collective-permute-start | bytes 294920 | tf_op jit(solution)/shard_map/ppermute | solution.py:343
  127.1 5.8 %collective-permute-start.6 = (f32[24,1024]{1,0:T(8,128)S(1)}, f32[24,1024]{1,0:T(8,128)S(1)}, u32[]{:S(2)}, u32[]{:S(2)}) collective-permute-start(f32[24,1024]{1,0:T(8,128)S(1)} %decode.1.mine), channel_id=1, source_target_pairs={{0,64},{32,96},{64,0},{96,32},{1,65},{33,97},{65,1},{97,33},{2,66}... | collective-permute-start | bytes 294920 | tf_op jit(solution)/shard_map/ppermute | solution.py:343
  128.8 4.1 %collective-permute-start.5 = (f32[24,1024]{1,0:T(8,128)S(1)}, f32[24,1024]{1,0:T(8,128)S(1)}, u32[]{:S(2)}, u32[]{:S(2)}) collective-permute-start(f32[24,1024]{1,0:T(8,128)S(1)} %decode.1.mine), channel_id=1, source_target_pairs={{0,32},{32,0},{64,96},{96,64},{1,33},{33,1},{65,97},{97,65},{2,34}... | collective-permute-start | bytes 294920 | tf_op jit(solution)/shard_map/ppermute | solution.py:343

commit v4 on v3

--- a/solution.py
+++ b/solution.py
@@ -14,7 +14,6 @@
 step_size = 0.25
 penalty = 1.0
 SEG = ("zlo", "core")
-GROUP = ("zlo", "batch")
 f32 = jnp.float32
 bf16 = jnp.bfloat16
 LANES = 128
@@ -159,113 +158,156 @@
     return jnp.round(values).astype(jnp.int32).astype(jnp.int16)
 
 
-def code_kernel(keep_low, keep_high, received_low, received_high, bias, message):
-    halves, owners, _, _ = message.shape
-    piece = keep_low.shape[0] // (halves * owners)
-    shared = keep_low.shape[1] // LANES
-    blocks = 2 * shared
+def head_of(bias):
+    level = level_of(jnp.abs(bias))
+    steps = bias * steps_of(level)
+    high = jnp.round(steps)
+    return level, high, (steps - high) * TOP
+
+
+def code_piece(low, high, head, store, store_head):
+    shared = len(low)
     row = lax.broadcasted_iota(jnp.int32, (HEAD, LANES), 0)
-    bias_now = bias[...]
-    bias_level = level_of(jnp.abs(bias_now))
-    bias_steps = bias_now * steps_of(bias_level)
-    bias_high = jnp.round(bias_steps)
-    bias_low = (bias_steps - bias_high) * TOP
-    head = jnp.where(row == shared, bias_level, 0.0)
-    head = jnp.where(row == shared + 1, bias_high, head)
-    head = jnp.where(row == shared + 2, bias_low, head)
+    tile = jnp.zeros((HEAD, LANES), f32)
+    for at, values in enumerate(head):
+        tile = jnp.where(row == shared + at, values, tile)
     for block in range(shared):
-        columns = pl.ds(block * LANES, LANES)
-        pair = (
-            keep_low[:, columns] + received_low[:, columns],
-            keep_high[:, columns] + received_high[:, columns],
-        )
+        pair = (low[block](), high[block]())
         peak = jnp.maximum(jnp.abs(pair[0]), jnp.abs(pair[1]))
         level = level_of(jnp.max(peak, axis=0, keepdims=True))
         steps = steps_of(level)
-        head = jnp.where(row == block, level, head)
-        for part, values in zip((block, block + shared), pair):
-            numbers = whole(values * steps)
+        tile = jnp.where(row == block, level, tile)
+        store(block, whole(pair[0] * steps))
+        store(block + shared, whole(pair[1] * steps))
+    store_head(whole(tile))
+
+
+def code_kernel(batches, keep_low, keep_high, got_low, got_high, bias, message):
+    turns = bias.shape[1] // LANES
+    owners = batches // turns
+    depth = keep_low.shape[0] // turns
+    piece = depth // owners
+    shared = keep_low.shape[1] // LANES
+
+    def turn(i, carry):
+        rows = pl.ds(pl.multiple_of(i * depth, depth), depth)
+        stretch = bias[:, pl.ds(pl.multiple_of(i * LANES, LANES), LANES)]
+
+        def sums(kept, got):
+            return [
+                functools.partial(lambda c: kept[rows, c] + got[rows, c], pl.ds(at * LANES, LANES))
+                for at in range(shared)
+            ]
+
+        def store(block, numbers):
             for owner in range(owners):
-                for half in range(halves):
-                    at = (owner * halves + half) * piece
-                    message[half, owner, pl.ds(part * piece, piece), :] = numbers[at : at + piece]
-    numbers = whole(head)
-    for owner in range(owners):
-        for half in range(halves):
-            message[half, owner, pl.ds(blocks * piece, HEAD), :] = numbers
-
-
-def code(keep, received, bias, halves, batches):
-    depth, width = keep[0].shape[0], 2 * keep[0].shape[1]
-    steps = width // LANES
-    owners = batches // steps
-    piece = depth // (halves * batches)
-    height = piece * steps + HEAD
+                message[i * owners + owner, pl.ds(block * piece, piece), :] = numbers[
+                    owner * piece : (owner + 1) * piece
+                ]
+
+        def store_head(numbers):
+            for owner in range(owners):
+                message[i * owners + owner, pl.ds(2 * shared * piece, HEAD), :] = numbers
+
+        code_piece(
+            sums(keep_low, got_low), sums(keep_high, got_high), head_of(stretch), store, store_head
+        )
+        return carry
+
+    lax.fori_loop(0, turns, turn, 0)
+
+
+def code(keep, received, bias, batches):
+    depth, middle = keep[0].shape
+    height = depth // batches * (2 * middle // LANES) + HEAD
     return pl.pallas_call(
-        code_kernel,
-        grid=(steps,),
-        out_shape=jax.ShapeDtypeStruct((halves, batches, height, LANES), jnp.int16),
-        in_specs=[pl.BlockSpec((depth // steps, width // 2), lambda i: (i, 0))] * 4
-        + [pl.BlockSpec((1, LANES), lambda i: (0, i))],
-        out_specs=pl.BlockSpec((halves, owners, height, LANES), lambda i: (0, i, 0, 0)),
+        functools.partial(code_kernel, batches),
+        out_shape=jax.ShapeDtypeStruct((batches, height, LANES), jnp.int16),
+        in_specs=[VMEM] * 5,
+        out_specs=VMEM,
         compiler_params=pltpu.CompilerParams(vmem_limit_bytes=16 * 1024 * 1024),
         name="code",
     )(*keep, *received, bias)
 
 
-def decode_kernel(message, out):
+def read_piece(blocks, load):
+    piece = blocks[0][1]
+    shared = len(blocks) // 2
+    head = load(len(blocks) * piece, HEAD).astype(jnp.int32).astype(f32)
+    scale = scale_of(head)
+    high, low = head[shared + 1 : shared + 2], head[shared + 2 : shared + 3]
+    bias = (high + low * (1.0 / TOP)) * scale[shared : shared + 1]
+    values = []
+    for block, (at, rows) in enumerate(blocks):
+        share = block % shared
+        numbers = load(at, rows).astype(jnp.int32).astype(f32)
+        values.append(numbers * scale[share : share + 1])
+    return values, bias
+
+
+def blocks_of(height, count):
+    piece = (height - HEAD) // count
+    return [(block * piece, piece) for block in range(count)]
+
+
+def decode_kernel(count, message, out):
     senders, height, _ = message.shape
-    blocks = out.shape[1] // LANES
-    shared = blocks // 2
-    piece = (height - HEAD) // blocks
-
-    @pl.when(pl.program_id(0) == 0)
-    def _():
-        out[...] = jnp.zeros_like(out)
-
-    sums = [jnp.zeros((piece, LANES), f32) for _ in range(blocks)]
-    bias = jnp.zeros((1, LANES), f32)
-    for sender in range(senders):
-        head = message[sender, pl.ds(blocks * piece, HEAD), :].astype(jnp.int32).astype(f32)
-        scale = scale_of(head)
-        high, low = head[shared + 1 : shared + 2], head[shared + 2 : shared + 3]
-        bias += (high + low * (1.0 / TOP)) * scale[shared : shared + 1]
-        for block in range(blocks):
-            data = message[sender, pl.ds(block * piece, piece), :].astype(jnp.int32).astype(f32)
-            at = block % shared
-            sums[block] += data * scale[at : at + 1]
-    for block in range(blocks):
-        out[pl.ds(0, piece), pl.ds(block * LANES, LANES)] += sums[block]
-    out[pl.ds(piece, 8), pl.ds(0, LANES)] += jnp.broadcast_to(bias, (8, LANES))
-
-
-def decode(message, width):
-    senders, height, _ = message.shape
-    steps = 8
-    piece = (height - HEAD) * LANES // width
+    blocks = blocks_of(height, count)
+    group = 4
+
+    def turn(i, carry):
+        bias, *sums = carry
+        for j in range(group):
+            values, more = read_piece(
+                blocks, lambda at, rows: message[i * group + j, pl.ds(at, rows), :]
+            )
+            bias = bias + more
+            sums = [one + other for one, other in zip(sums, values)]
+        return (bias, *sums)
+
+    zeros = (jnp.zeros((1, LANES), f32),) + (jnp.zeros((blocks[0][1], LANES), f32),) * count
+    bias, *sums = lax.fori_loop(0, senders // group, turn, zeros)
+    ready = [functools.partial(lambda v: v, value) for value in sums]
+
+    def store(block, numbers):
+        at, rows = blocks[block]
+        out[pl.ds(at, rows), :] = numbers
+
+    def store_head(numbers):
+        out[pl.ds(height - HEAD, HEAD), :] = numbers
+
+    code_piece(ready[: count // 2], ready[count // 2 :], head_of(bias), store, store_head)
+
+
+def decode(message, count):
     return pl.pallas_call(
-        decode_kernel,
-        grid=(steps,),
-        out_shape=jax.ShapeDtypeStruct((piece + 8, width), f32),
-        in_specs=[pl.BlockSpec((senders // steps, height, LANES), lambda i: (i, 0, 0))],
-        out_specs=pl.BlockSpec((piece + 8, width), lambda i: (0, 0)),
-        compiler_params=pltpu.CompilerParams(vmem_limit_bytes=16 * 1024 * 1024),
+        functools.partial(decode_kernel, count),
+        out_shape=jax.ShapeDtypeStruct(message.shape[1:], jnp.int16),
+        in_specs=[VMEM],
+        out_specs=VMEM,
+        compiler_params=pltpu.CompilerParams(vmem_limit_bytes=8 * 1024 * 1024),
         name="decode",
     )(message)
 
 
 def lay_out_kernel(scale, info, mine, by_core, by_zlo, by_both, grad_in, grad_out, grad_bias):
-    core, zlo, offset = info[0], info[1], info[2]
-    piece = mine.shape[0] - 8
-    here = pl.ds(pl.multiple_of(zlo * piece, piece), piece)
-    there = pl.ds(pl.multiple_of((1 - zlo) * piece, piece), piece)
-    rows = pl.ds(0, piece)
+    core, offset = info[0], info[1]
+    count = grad_in.shape[1] // LANES
+    blocks = blocks_of(mine.shape[0], count)
+    parts = []
+    stretches = []
+    for ref in (mine, by_core, by_zlo, by_both):
+        values, bias = read_piece(
+            blocks, functools.partial(lambda r, at, rows: r[pl.ds(at, rows), :], ref)
+        )
+        parts.append(values)
+        stretches.append(bias)
 
     def fill(kept, other):
-        kept[here, :] = mine[rows, :] * scale
-        kept[there, :] = by_zlo[rows, :] * scale
-        other[here, :] = by_core[rows, :] * scale
-        other[there, :] = by_both[rows, :] * scale
+        for block in range(count):
+            columns = pl.ds(block * LANES, LANES)
+            kept[:, columns] = (parts[0][block] + parts[2][block]) * scale
+            other[:, columns] = (parts[1][block] + parts[3][block]) * scale
 
     @pl.when(core == 0)
     def _():
@@ -275,16 +317,16 @@
     def _():
         fill(grad_out, grad_in)
 
-    stretch = (mine[pl.ds(piece, 8), pl.ds(0, LANES)] + by_core[pl.ds(piece, 8), pl.ds(0, LANES)]) * scale
-    grad_bias[...] = pltpu.roll(stretch, LANES - offset, 1)
-
-
-def lay_out(scale, info, *quarters):
-    rows, width = quarters[0].shape
-    gradient = jax.ShapeDtypeStruct((2 * (rows - 8), width), f32)
+    stretch = ((stretches[0] + stretches[3]) + (stretches[1] + stretches[2])) * scale
+    turned = pltpu.roll(jnp.broadcast_to(stretch, (8, LANES)), LANES - offset, 1)
+    grad_bias[...] = turned[0:1, : grad_bias.shape[1]]
+
+
+def lay_out(scale, info, quarters, rows, width):
+    gradient = jax.ShapeDtypeStruct((rows, width), f32)
     return pl.pallas_call(
         functools.partial(lay_out_kernel, scale),
-        out_shape=(gradient, gradient, jax.ShapeDtypeStruct((8, LANES), f32)),
+        out_shape=(gradient, gradient, jax.ShapeDtypeStruct((1, rows), f32)),
         in_specs=[SMEM] + [VMEM] * 4,
         out_specs=(VMEM,) * 3,
         compiler_params=pltpu.CompilerParams(vmem_limit_bytes=8 * 1024 * 1024),
@@ -311,7 +353,6 @@
     core = lax.axis_index("core")
     place = lax.axis_index(SEG)
     batches = lax.axis_size("batch")
-    halves = lax.axis_size("zlo")
     rows, width = start.shape
     own = w_in.shape[0]
 
@@ -336,17 +377,16 @@
         received.append(swap(sent))
     for half in range(2):
         keep.append(contract_rows(left[1], right[1, half]))
-    message = code(keep, received, bias, halves, batches)
-    message = lax.all_to_all(message.reshape((halves * batches,) + message.shape[2:]), GROUP, 0, 0)
-    mine = decode(message, width)
+    message = code(keep, received, bias, batches)
+    message = lax.all_to_all(message, "batch", 0, 0)
+    mine = decode(message, width // LANES)
     quarters = [mine] + [
         lax.ppermute(mine, SEG, [(i, i ^ flip) for i in range(4)]) for flip in (1, 2, 3)
     ]
     offset = lax.axis_index("batch") % (LANES // own) * own
-    places = jnp.stack([core, lax.axis_index("zlo"), offset])
     scale = 1.0 / math.sqrt(rows * batches)
-    grad_in, grad_out, grad_bias = lay_out(scale, places, *quarters)
-    return (grad_starts, grad_in, grad_out, grad_bias[0, :own])
+    grad_in, grad_out, grad_bias = lay_out(scale, jnp.stack([core, offset]), quarters, own, width)
+    return (grad_starts, grad_in, grad_out, grad_bias[0])
 
 
 def solution(mesh):

time: 135 us -> 130 us (0.963)
  waiting for transfers between devices: 39.3 us -> 32.9 us
  starting transfers between devices: 26.8 us -> 29.4 us
    all_to_all x1, starting transfers between devices: 9.82 us -> 4.08 us  [body(): message = lax.all_to_all(message, 'batch', 0, 0)]
    all_to_all x1, waiting for transfers between devices: 26.4 us -> 21.1 us  [body(): message = lax.all_to_all(message, 'batch', 0, 0)]
    ppermute x3, starting transfers between devices: 3.46 us -> 7.73 us  [body(): lax.ppermute(mine, SEG, [(i, i ^ flip) for i in range(4)])]
    ppermute x2, starting transfers between devices: 5.75 us -> 9.77 us  [shift_seg(): return lax.ppermute(block, SEG, route)]
where the time goes in v4:
time: 130 us; the launch traced here: 129 us
  blocking collectives  39.3 us (30%)
  waiting for transfers between devices  32.9 us (25%)
  starting transfers between devices  29.4 us (23%)
  Pallas kernels  14.6 us (11%)
  matrix products  7.28 us (6%)
  other arithmetic  4.11 us (3%)
  between operations  1.43 us (1%)
    all_to_all x1, blocking collectives, body(): own_w = lax.all_to_all(copies, 'batch', 0, 0)  39.3 us
    all_to_all x1, waiting for transfers between devices, body(): message = lax.all_to_all(message, 'batch', 0, 0)  21.1 us
    pallas_call x1, Pallas kernels, integrate(): pl.pallas_call(integrate_kernel, out_shape=(states, states, jax.ShapeDtyp...  9.86 us
    ppermute x2, starting transfers between devices, shift_seg(): return lax.ppermute(block, SEG, route)  9.77 us
    ppermute x2, waiting for transfers between devices, shift_seg(): return lax.ppermute(block, SEG, route)  7.94 us
    ppermute x3, starting transfers between devices, swap(): return lax.ppermute(block, 'core', [(0, 1), (1, 0)])  7.79 us
    ppermute x3, starting transfers between devices, body(): lax.ppermute(mine, SEG, [(i, i ^ flip) for i in range(4)])  7.73 us
    dot_general x4, matrix products, contract_rows(): lax.dot_general(left, right, (((0,), (0,)), ((), ())), preferred_element_...  7.28 us
  transfers between devices with their start and end apart: 9, of which 4 were waited for; matrix products, arithmetic and copies ran while one was open for 5% of the time, Pallas kernels for 1%

profile of v4, /device:TPU:1, one launch (start us, length us, event | category | flops | bytes accessed | tf_op | source)
XLA Modules:
  0.0 129.3 jit_solution(11052440583945630013)
XLA Ops:
  0.6 0.9 broadcast_select_fusion
  1.5 0.2 broadcast_in_dim.13
  1.8 0.0 copy-start.1
  1.8 0.0 copy-start.3
  1.8 39.3 %all_to_all.10 = bf16[32,32,1024]{2,1,0:T(8,128)(2,1)S(1)} all-to-all(bf16[32,32,1024]{2,1,0:T(8,128)(2,1)S(1)} %broadcast_in_dim.13), channel_id=1, replica_groups=mesh['zlo'=2,'core'=2,'batch'=32] {'batch'}, dimensions={0} | all-to-all | bytes 4194304 | tf_op jit(solution)/shard_map/all_to_all | solution.py:362
  41.1 2.3 %collective-permute-start.1 = (bf16[1024,1024]{1,0:T(8,128)(2,1)S(1)}, bf16[1024,1024]{1,0:T(8,128)(2,1)}, u32[]{:S(2)}, u32[]{:S(2)}) collective-permute-start(bf16[1024,1024]{1,0:T(8,128)(2,1)S(1)} %bitcast.33), channel_id=1, source_target_pairs={{0,32},{32,0},{1,33},{33,1},{2,34},{34,2},{3,35},{35,3},{4,36},{36... | collective-permute-start | bytes 6291464 | tf_op jit(solution)/shard_map/ppermute | solution.py:348
  43.4 1.9 %collective-permute-start = (f32[128,1024]{1,0:T(8,128)S(1)}, f32[128,1024]{1,0:T(8,128)}, u32[]{:S(2)}, u32[]{:S(2)}) collective-permute-start(f32[128,1024]{1,0:T(8,128)S(1)} %bitcast.36), channel_id=1, source_target_pairs={{32,0},{64,32},{96,64},{33,1},{65,33},{97,65},{34,2},{66,34},{98,6... | collective-permute-start | bytes 1572872 | tf_op jit(solution)/shard_map/ppermute | solution.py:344
  46.0 0.1 pad_add_fusion.info
  46.0 7.9 %collective-permute-done = f32[128,1024]{1,0:T(8,128)} collective-permute-done((f32[128,1024]{1,0:T(8,128)S(1)}, f32[128,1024]{1,0:T(8,128)}, u32[]{:S(2)}, u32[]{:S(2)}) %collective-permute-start) | collective-permute-done | bytes 524320 | tf_op jit(solution)/shard_map/ppermute | solution.py:344
  54.0 1.2 pad_maximum_fusion.given
  55.2 0.0 collective-permute-done.1.other_w
  55.2 9.9 %integrate.1 = (f32[128,1024]{1,0:T(8,128)S(1)}, f32[128,1024]{1,0:T(8,128)S(1)}, f32[1,1024]{1,0:T(1,128)S(1)}, bf16[2,1536,1024]{2,1,0:T(8,128)(2,1)S(1)}, bf16[2,2,1536,512]{3,2,1,0:T(8,128)(2,1)S(1)}) custom-call(s32[3]{0:T(128)S(1)} %pad_add_fusion.info, f32[3,128,1024]{2,1,0:T(8,128)S(1)} %pad_maximum_fusion.given, f32[1,1024]{1,0:T(1,128)S(1)} %bitcast.35, ...), custom_call_target="tpu_custom_call" | custom-call | tf_op jit(solution)/shard_map/integrate/pallas_call | solution.py:127
  65.0 1.8 %fusion = f32[1024,512]{1,0:T(8,128)S(1)} fusion(bf16[2,1536,1024]{2,1,0:T(8,128)(2,1)S(1)} %get-tuple-element.14, bf16[2,2,1536,512]{3,2,1,0:T(8,128)(2,1)S(1)} %get-tuple-element.15), kind=kOutput, calls=%fused_computation | convolution fusion | flops 1610612736 | bytes 6815744 | tf_op jit(solution)/shard_map/dot_general | solution.py:338
  66.9 1.8 %fusion.2 = f32[1024,512]{1,0:T(8,128)S(1)} fusion(bf16[2,1536,1024]{2,1,0:T(8,128)(2,1)S(1)} %get-tuple-element.14, bf16[2,2,1536,512]{3,2,1,0:T(8,128)(2,1)S(1)} %get-tuple-element.15), kind=kOutput, calls=%fused_computation.2 | convolution fusion | flops 1610612736 | bytes 6815744 | tf_op jit(solution)/shard_map/dot_general | solution.py:338
  68.7 5.2 %collective-permute-start.3 = (f32[1024,512]{1,0:T(8,128)S(1)}, f32[1024,512]{1,0:T(8,128)S(1)}, u32[]{:S(2)}, u32[]{:S(2)}) collective-permute-start(f32[1024,512]{1,0:T(8,128)S(1)} %fusion.2), channel_id=1, source_target_pairs={{0,32},{32,0},{1,33},{33,1},{2,34},{34,2},{3,35},{35,3},{4,36},{36... | collective-permute-start | bytes 6291464 | tf_op jit(solution)/shard_map/ppermute | solution.py:348
  73.9 0.3 collective-permute-start.4
  74.2 1.8 %fusion.4.keep_high = f32[1024,512]{1,0:T(8,128)S(1)} fusion(bf16[2,1536,1024]{2,1,0:T(8,128)(2,1)S(1)} %get-tuple-element.14, bf16[2,2,1536,512]{3,2,1,0:T(8,128)(2,1)S(1)} %get-tuple-element.15), kind=kOutput, calls=%fused_computation.4 | convolution fusion | flops 1610612736 | bytes 6815744 | tf_op jit(solution)/shard_map/dot_general | solution.py:338
  76.0 1.8 %fusion.6.keep_low = f32[1024,512]{1,0:T(8,128)S(1)} fusion(bf16[2,1536,1024]{2,1,0:T(8,128)(2,1)S(1)} %get-tuple-element.14, bf16[2,2,1536,512]{3,2,1,0:T(8,128)(2,1)S(1)} %get-tuple-element.15), kind=kOutput, calls=%fused_computation.6 | convolution fusion | flops 1610612736 | bytes 6815744 | tf_op jit(solution)/shard_map/dot_general | solution.py:338
  77.9 2.9 %collective-permute-done.4.got_high = f32[1024,512]{1,0:T(8,128)S(1)} collective-permute-done((f32[1024,512]{1,0:T(8,128)S(1)}, f32[1024,512]{1,0:T(8,128)S(1)}, u32[]{:S(2)}, u32[]{:S(2)}) %collective-permute-start.4) | collective-permute-done | bytes 2097184 | tf_op jit(solution)/shard_map/ppermute | solution.py:348
  80.7 2.6 %code.1 = s16[32,264,128]{2,1,0:T(8,128)(2,1)} custom-call(f32[1024,512]{1,0:T(8,128)S(1)} %fusion.6.keep_low, f32[1024,512]{1,0:T(8,128)S(1)} %fusion.4.keep_high, f32[1024,512]{1,0:T(8,128)S(1)} %collective-permute-done.3.got_low, f32[1024,512]{1,0:T(8,128)S(1)} %collective-permute-done.4.got_high, f32[1,1024]{1,0:T(1,128)S(1)} %get-tuple-element.16.bias), custom_call_target="tpu_custom_call" | custom-call | tf_op jit(solution)/shard_map/code/pallas_call | solution.py:223
  83.3 4.1 %all-to-all-start.1 = ((s16[32,264,128]{2,1,0:T(8,128)(2,1)}), s16[32,264,128]{2,1,0:T(8,128)(2,1)S(1)}, u32[]{:S(2)}, u32[]{:S(2)}) async-start(s16[32,264,128]{2,1,0:T(8,128)(2,1)} %code.1), calls=%async_computation.1 | async-start | bytes 4325376 | tf_op jit(solution)/shard_map/all_to_all | solution.py:381
  87.4 7.9 %collective-permute-start.2 = (f32[128,1024]{1,0:T(8,128)S(1)}, f32[128,1024]{1,0:T(8,128)}, u32[]{:S(2)}, u32[]{:S(2)}) collective-permute-start(f32[128,1024]{1,0:T(8,128)S(1)} %get-tuple-element.13), channel_id=1, source_target_pairs={{0,32},{32,64},{64,96},{1,33},{33,65},{65,97},{2,34},{34,66},{66,9... | collective-permute-start | bytes 1572872 | tf_op jit(solution)/shard_map/ppermute | solution.py:344
  95.3 0.1 pad_add_fusion.1.info
  95.4 21.1 %all-to-all-done.1.message = s16[32,264,128]{2,1,0:T(8,128)(2,1)S(1)} async-done(((s16[32,264,128]{2,1,0:T(8,128)(2,1)}), s16[32,264,128]{2,1,0:T(8,128)(2,1)S(1)}, u32[]{:S(2)}, u32[]{:S(2)}) %all-to-all-start.1) | async-done | bytes 2162720 | tf_op jit(solution)/shard_map/all_to_all | solution.py:381
  116.5 0.8 decode.1.mine
  117.3 7.2 %collective-permute-start.7 = (s16[264,128]{1,0:T(8,128)(2,1)S(1)}, s16[264,128]{1,0:T(8,128)(2,1)S(1)}, u32[]{:S(2)}, u32[]{:S(2)}) collective-permute-start(s16[264,128]{1,0:T(8,128)(2,1)S(1)} %decode.1.mine), channel_id=1, source_target_pairs={{0,96},{32,64},{64,32},{96,0},{1,97},{33,65},{65,33},{97,1},{2,98}... | collective-permute-start | bytes 202760 | tf_op jit(solution)/shard_map/ppermute | solution.py:384
  124.5 0.5 collective-permute-start.5
  125.0 1.9 %subtract_bitcast_fusion = f32[1,128,1024]{2,1,0:T(8,128)} fusion(f32[128,1024]{1,0:T(8,128)S(1)} %get-tuple-element.12, f32[128,1024]{1,0:T(8,128)} %collective-permute-done.2, f32[]{:T(128)S(6)} %convert_element_type.4, f32[1,128,1024]{2,1,0:T(8,128)S(1)} %copy-done.2), kind=kLoop, calls=%fused_computation.21 | loop fusion | flops 393216 | bytes 2097156 | tf_op jit(solution)/shard_map/broadcast_in_dim | solution.py:372
  126.9 0.0 collective-permute-done.7.by_both
  126.9 1.0 collective-permute-done.6.by_zlo
  127.9 0.0 collective-permute-done.5.by_core
  127.9 1.3 %lay_out.1 = (f32[32,1024]{1,0:T(8,128)}, f32[32,1024]{1,0:T(8,128)}, f32[1,32]{1,0:T(1,128)}) custom-call(s32[2]{0:T(128)S(1)} %pad_add_fusion.1.info, s16[264,128]{1,0:T(8,128)(2,1)S(1)} %decode.1.mine, s16[264,128]{1,0:T(8,128)(2,1)S(1)} %collective-permute-done.5.by_core, s16[264,128]{1,0:T(8,128)(2,1)S(1)} %collective-permute-done.6.by_zlo, ...), custom_call_target="tpu_custom_call" | custom-call | tf_op jit(solution)/shard_map/lay_out/pallas_call | solution.py:327
  (9 shorter events, 0.0 us)
Async XLA Ops:
  1.8 41.6 %copy-start.1 = (f32[1,128,1024]{2,1,0:T(8,128)S(1)}, f32[1,128,1024]{2,1,0:T(8,128)}, u32[]{:S(2)}) copy-start(f32[1,128,1024]{2,1,0:T(8,128)} %param.6) | copy-start | bytes 1572868
  1.8 52.2 %copy-start.3 = (f32[1,128,1024]{2,1,0:T(8,128)S(1)}, f32[1,128,1024]{2,1,0:T(8,128)}, u32[]{:S(2)}) copy-start(f32[1,128,1024]{2,1,0:T(8,128)} %param.7) | copy-start | bytes 1572868
  41.1 14.1 %copy-start = (f32[1024]{0:T(1024)S(1)}, f32[1024]{0:T(1024)}, u32[]{:S(2)}) copy-start(f32[1024]{0:T(1024)} %param.10) | copy-start | bytes 12292
  41.1 14.1 %collective-permute-start.1 = (bf16[1024,1024]{1,0:T(8,128)(2,1)S(1)}, bf16[1024,1024]{1,0:T(8,128)(2,1)}, u32[]{:S(2)}, u32[]{:S(2)}) collective-permute-start(bf16[1024,1024]{1,0:T(8,128)(2,1)S(1)} %bitcast.33), channel_id=1, source_target_pairs={{0,32},{32,0},{1,33},{33,1},{2,34},{34,2},{3,35},{35,3},{4,36},{36... | collective-permute-start | bytes 6291464 | tf_op jit(solution)/shard_map/ppermute | solution.py:348
  43.4 10.6 %collective-permute-start = (f32[128,1024]{1,0:T(8,128)S(1)}, f32[128,1024]{1,0:T(8,128)}, u32[]{:S(2)}, u32[]{:S(2)}) collective-permute-start(f32[128,1024]{1,0:T(8,128)S(1)} %bitcast.36), channel_id=1, source_target_pairs={{32,0},{64,32},{96,64},{33,1},{65,33},{97,65},{34,2},{66,34},{98,6... | collective-permute-start | bytes 1572872 | tf_op jit(solution)/shard_map/ppermute | solution.py:344
  68.7 9.2 %collective-permute-start.3 = (f32[1024,512]{1,0:T(8,128)S(1)}, f32[1024,512]{1,0:T(8,128)S(1)}, u32[]{:S(2)}, u32[]{:S(2)}) collective-permute-start(f32[1024,512]{1,0:T(8,128)S(1)} %fusion.2), channel_id=1, source_target_pairs={{0,32},{32,0},{1,33},{33,1},{2,34},{34,2},{3,35},{35,3},{4,36},{36... | collective-permute-start | bytes 6291464 | tf_op jit(solution)/shard_map/ppermute | solution.py:348
  73.9 6.8 %collective-permute-start.4 = (f32[1024,512]{1,0:T(8,128)S(1)}, f32[1024,512]{1,0:T(8,128)S(1)}, u32[]{:S(2)}, u32[]{:S(2)}) collective-permute-start(f32[1024,512]{1,0:T(8,128)S(1)} %fusion), channel_id=1, source_target_pairs={{0,32},{32,0},{1,33},{33,1},{2,34},{34,2},{3,35},{35,3},{4,36},{36... | collective-permute-start | bytes 6291464 | tf_op jit(solution)/shard_map/ppermute | solution.py:348
  83.3 33.1 %all-to-all-start.1 = ((s16[32,264,128]{2,1,0:T(8,128)(2,1)}), s16[32,264,128]{2,1,0:T(8,128)(2,1)S(1)}, u32[]{:S(2)}, u32[]{:S(2)}) async-start(s16[32,264,128]{2,1,0:T(8,128)(2,1)} %code.1), calls=%async_computation.1 | async-start | bytes 4325376 | tf_op jit(solution)/shard_map/all_to_all | solution.py:381
  87.4 37.6 %collective-permute-start.2 = (f32[128,1024]{1,0:T(8,128)S(1)}, f32[128,1024]{1,0:T(8,128)}, u32[]{:S(2)}, u32[]{:S(2)}) collective-permute-start(f32[128,1024]{1,0:T(8,128)S(1)} %get-tuple-element.13), channel_id=1, source_target_pairs={{0,32},{32,64},{64,96},{1,33},{33,65},{65,97},{2,34},{34,66},{66,9... | collective-permute-start | bytes 1572872 | tf_op jit(solution)/shard_map/ppermute | solution.py:344
  116.5 8.5 %copy-start.2 = (f32[1,128,1024]{2,1,0:T(8,128)S(1)}, f32[1,128,1024]{2,1,0:T(8,128)}, u32[]{:S(2)}) copy-start(f32[1,128,1024]{2,1,0:T(8,128)} %param.6) | copy-start | bytes 1572868
  117.3 9.7 %collective-permute-start.7 = (s16[264,128]{1,0:T(8,128)(2,1)S(1)}, s16[264,128]{1,0:T(8,128)(2,1)S(1)}, u32[]{:S(2)}, u32[]{:S(2)}) collective-permute-start(s16[264,128]{1,0:T(8,128)(2,1)S(1)} %decode.1.mine), channel_id=1, source_target_pairs={{0,96},{32,64},{64,32},{96,0},{1,97},{33,65},{65,33},{97,1},{2,98}... | collective-permute-start | bytes 202760 | tf_op jit(solution)/shard_map/ppermute | solution.py:384
  124.5 3.4 %collective-permute-start.6 = (s16[264,128]{1,0:T(8,128)(2,1)S(1)}, s16[264,128]{1,0:T(8,128)(2,1)S(1)}, u32[]{:S(2)}, u32[]{:S(2)}) collective-permute-start(s16[264,128]{1,0:T(8,128)(2,1)S(1)} %decode.1.mine), channel_id=1, source_target_pairs={{0,64},{32,96},{64,0},{96,32},{1,65},{33,97},{65,1},{97,33},{2,66}... | collective-permute-start | bytes 202760 | tf_op jit(solution)/shard_map/ppermute | solution.py:384
  124.5 3.4 %collective-permute-start.5 = (s16[264,128]{1,0:T(8,128)(2,1)S(1)}, s16[264,128]{1,0:T(8,128)(2,1)S(1)}, u32[]{:S(2)}, u32[]{:S(2)}) collective-permute-start(s16[264,128]{1,0:T(8,128)(2,1)S(1)} %decode.1.mine), channel_id=1, source_target_pairs={{0,32},{32,0},{64,96},{96,64},{1,33},{33,1},{65,97},{97,65},{2,34}... | collective-permute-start | bytes 202760 | tf_op jit(solution)/shard_map/ppermute | solution.py:384

commit v5 on v4

--- a/solution.py
+++ b/solution.py
@@ -47,8 +47,6 @@
     offset = bias_in[...]
     first.wait()
     second.wait()
-    w_turned[0] = w[0].T
-    w_turned[1] = w[1].T
 
     def place(at):
         return pl.ds(pl.multiple_of(at * rows, rows), rows)
@@ -74,19 +72,30 @@
         right[slot_in, 1, place(at), :] = low[:, middle:]
         return product(low, w_turned[0])
 
-    def forward(s, carry):
+    def turn(part):
+        quarter = w.shape[1] // STAGES
+        for which in range(2):
+            rows_now = pl.ds(part * quarter, quarter)
+            w_turned[which, :, rows_now] = w[which, rows_now, :].T
+
+    def forward(s, carry, beside=lambda part: None):
         at = STAGES * s
+        beside(0)
         k = field(state[...], at)
         total[...] = k
+        beside(1)
         k = field(state[...] + 0.5 * step_size * k, at + 1)
         total[...] += 2.0 * k
+        beside(2)
         k = field(state[...] + 0.5 * step_size * k, at + 2)
         total[...] += 2.0 * k
+        beside(3)
         k = field(state[...] + step_size * k, at + 3)
         state[...] = state[...] + step_size / 6.0 * (total[...] + k)
         return carry
 
-    lax.fori_loop(0, count, forward, 0)
+    forward(0, 0, turn)
+    lax.fori_loop(1, count, forward, 0)
     end = state[...]
     ends[...] = end
     state[...] = (end - given[1]) + penalty * ((end - given[2]) * has_next)

time: 130 us -> 129 us (level)
  no operation moved by 1% of the time
where the time goes in v5:
time: 129 us; the launch traced here: 128 us
  blocking collectives  39.3 us (30%)
  waiting for transfers between devices  33.1 us (26%)
  starting transfers between devices  29.2 us (23%)
  Pallas kernels  13.7 us (11%)
  matrix products  7.29 us (6%)
  other arithmetic  4.11 us (3%)
  between operations  1.42 us (1%)
    all_to_all x1, blocking collectives, body(): own_w = lax.all_to_all(copies, 'batch', 0, 0)  39.3 us
    all_to_all x1, waiting for transfers between devices, body(): message = lax.all_to_all(message, 'batch', 0, 0)  21.1 us
    ppermute x2, starting transfers between devices, shift_seg(): return lax.ppermute(block, SEG, route)  9.77 us
    pallas_call x1, Pallas kernels, integrate(): pl.pallas_call(integrate_kernel, out_shape=(states, states, jax.ShapeDtyp...  9.01 us
    ppermute x2, waiting for transfers between devices, shift_seg(): return lax.ppermute(block, SEG, route)  7.94 us
    ppermute x3, starting transfers between devices, body(): lax.ppermute(mine, SEG, [(i, i ^ flip) for i in range(4)])  7.72 us
    ppermute x3, starting transfers between devices, swap(): return lax.ppermute(block, 'core', [(0, 1), (1, 0)])  7.65 us
    dot_general x4, matrix products, contract_rows(): lax.dot_general(left, right, (((0,), (0,)), ((), ())), preferred_element_...  7.29 us
  transfers between devices with their start and end apart: 9, of which 4 were waited for; matrix products, arithmetic and copies ran while one was open for 5% of the time, Pallas kernels for 1%

profile of v5, /device:TPU:1, one launch (start us, length us, event | category | flops | bytes accessed | tf_op | source)
XLA Modules:
  0.0 128.4 jit_solution(1364360033480296294)
XLA Ops:
  0.6 0.9 broadcast_select_fusion
  1.5 0.2 broadcast_in_dim.13
  1.8 0.0 copy-start.1
  1.8 0.0 copy-start.3
  1.8 39.3 %all_to_all.10 = bf16[32,32,1024]{2,1,0:T(8,128)(2,1)S(1)} all-to-all(bf16[32,32,1024]{2,1,0:T(8,128)(2,1)S(1)} %broadcast_in_dim.13), channel_id=1, replica_groups=mesh['zlo'=2,'core'=2,'batch'=32] {'batch'}, dimensions={0} | all-to-all | bytes 4194304 | tf_op jit(solution)/shard_map/all_to_all | solution.py:371
  41.1 2.3 %collective-permute-start.1 = (bf16[1024,1024]{1,0:T(8,128)(2,1)S(1)}, bf16[1024,1024]{1,0:T(8,128)(2,1)}, u32[]{:S(2)}, u32[]{:S(2)}) collective-permute-start(bf16[1024,1024]{1,0:T(8,128)(2,1)S(1)} %bitcast.33), channel_id=1, source_target_pairs={{0,32},{32,0},{1,33},{33,1},{2,34},{34,2},{3,35},{35,3},{4,36},{36... | collective-permute-start | bytes 6291464 | tf_op jit(solution)/shard_map/ppermute | solution.py:357
  43.4 1.9 %collective-permute-start = (f32[128,1024]{1,0:T(8,128)S(1)}, f32[128,1024]{1,0:T(8,128)}, u32[]{:S(2)}, u32[]{:S(2)}) collective-permute-start(f32[128,1024]{1,0:T(8,128)S(1)} %bitcast.36), channel_id=1, source_target_pairs={{32,0},{64,32},{96,64},{33,1},{65,33},{97,65},{34,2},{66,34},{98,6... | collective-permute-start | bytes 1572872 | tf_op jit(solution)/shard_map/ppermute | solution.py:353
  46.0 0.1 pad_add_fusion.info
  46.0 7.9 %collective-permute-done = f32[128,1024]{1,0:T(8,128)} collective-permute-done((f32[128,1024]{1,0:T(8,128)S(1)}, f32[128,1024]{1,0:T(8,128)}, u32[]{:S(2)}, u32[]{:S(2)}) %collective-permute-start) | collective-permute-done | bytes 524320 | tf_op jit(solution)/shard_map/ppermute | solution.py:353
  54.0 1.2 pad_maximum_fusion.given
  55.2 9.0 %integrate.1 = (f32[128,1024]{1,0:T(8,128)S(1)}, f32[128,1024]{1,0:T(8,128)S(1)}, f32[1,1024]{1,0:T(1,128)S(1)}, bf16[2,1536,1024]{2,1,0:T(8,128)(2,1)S(1)}, bf16[2,2,1536,512]{3,2,1,0:T(8,128)(2,1)S(1)}) custom-call(s32[3]{0:T(128)S(1)} %pad_add_fusion.info, f32[3,128,1024]{2,1,0:T(8,128)S(1)} %pad_maximum_fusion.given, f32[1,1024]{1,0:T(1,128)S(1)} %bitcast.35, ...), custom_call_target="tpu_custom_call" | custom-call | tf_op jit(solution)/shard_map/integrate/pallas_call | solution.py:136
  64.2 1.8 %fusion = f32[1024,512]{1,0:T(8,128)S(1)} fusion(bf16[2,1536,1024]{2,1,0:T(8,128)(2,1)S(1)} %get-tuple-element.14, bf16[2,2,1536,512]{3,2,1,0:T(8,128)(2,1)S(1)} %get-tuple-element.15), kind=kOutput, calls=%fused_computation | convolution fusion | flops 1610612736 | bytes 6815744 | tf_op jit(solution)/shard_map/dot_general | solution.py:347
  66.0 1.8 %fusion.2 = f32[1024,512]{1,0:T(8,128)S(1)} fusion(bf16[2,1536,1024]{2,1,0:T(8,128)(2,1)S(1)} %get-tuple-element.14, bf16[2,2,1536,512]{3,2,1,0:T(8,128)(2,1)S(1)} %get-tuple-element.15), kind=kOutput, calls=%fused_computation.2 | convolution fusion | flops 1610612736 | bytes 6815744 | tf_op jit(solution)/shard_map/dot_general | solution.py:347
  67.9 5.3 %collective-permute-start.3 = (f32[1024,512]{1,0:T(8,128)S(1)}, f32[1024,512]{1,0:T(8,128)S(1)}, u32[]{:S(2)}, u32[]{:S(2)}) collective-permute-start(f32[1024,512]{1,0:T(8,128)S(1)} %fusion.2), channel_id=1, source_target_pairs={{0,32},{32,0},{1,33},{33,1},{2,34},{34,2},{3,35},{35,3},{4,36},{36... | collective-permute-start | bytes 6291464 | tf_op jit(solution)/shard_map/ppermute | solution.py:357
  73.1 0.1 collective-permute-start.4
  73.2 1.8 %fusion.4.keep_high = f32[1024,512]{1,0:T(8,128)S(1)} fusion(bf16[2,1536,1024]{2,1,0:T(8,128)(2,1)S(1)} %get-tuple-element.14, bf16[2,2,1536,512]{3,2,1,0:T(8,128)(2,1)S(1)} %get-tuple-element.15), kind=kOutput, calls=%fused_computation.4 | convolution fusion | flops 1610612736 | bytes 6815744 | tf_op jit(solution)/shard_map/dot_general | solution.py:347
  75.0 1.8 %fusion.6.keep_low = f32[1024,512]{1,0:T(8,128)S(1)} fusion(bf16[2,1536,1024]{2,1,0:T(8,128)(2,1)S(1)} %get-tuple-element.14, bf16[2,2,1536,512]{3,2,1,0:T(8,128)(2,1)S(1)} %get-tuple-element.15), kind=kOutput, calls=%fused_computation.6 | convolution fusion | flops 1610612736 | bytes 6815744 | tf_op jit(solution)/shard_map/dot_general | solution.py:347
  76.9 0.0 collective-permute-done.3.got_low
  76.9 3.0 %collective-permute-done.4.got_high = f32[1024,512]{1,0:T(8,128)S(1)} collective-permute-done((f32[1024,512]{1,0:T(8,128)S(1)}, f32[1024,512]{1,0:T(8,128)S(1)}, u32[]{:S(2)}, u32[]{:S(2)}) %collective-permute-start.4) | collective-permute-done | bytes 2097184 | tf_op jit(solution)/shard_map/ppermute | solution.py:357
  79.9 2.6 %code.1 = s16[32,264,128]{2,1,0:T(8,128)(2,1)} custom-call(f32[1024,512]{1,0:T(8,128)S(1)} %fusion.6.keep_low, f32[1024,512]{1,0:T(8,128)S(1)} %fusion.4.keep_high, f32[1024,512]{1,0:T(8,128)S(1)} %collective-permute-done.3.got_low, f32[1024,512]{1,0:T(8,128)S(1)} %collective-permute-done.4.got_high, f32[1,1024]{1,0:T(1,128)S(1)} %get-tuple-element.16.bias), custom_call_target="tpu_custom_call" | custom-call | tf_op jit(solution)/shard_map/code/pallas_call | solution.py:232
  82.5 4.1 %all-to-all-start.1 = ((s16[32,264,128]{2,1,0:T(8,128)(2,1)}), s16[32,264,128]{2,1,0:T(8,128)(2,1)S(1)}, u32[]{:S(2)}, u32[]{:S(2)}) async-start(s16[32,264,128]{2,1,0:T(8,128)(2,1)} %code.1), calls=%async_computation.1 | async-start | bytes 4325376 | tf_op jit(solution)/shard_map/all_to_all | solution.py:390
  86.6 7.9 %collective-permute-start.2 = (f32[128,1024]{1,0:T(8,128)S(1)}, f32[128,1024]{1,0:T(8,128)}, u32[]{:S(2)}, u32[]{:S(2)}) collective-permute-start(f32[128,1024]{1,0:T(8,128)S(1)} %get-tuple-element.13), channel_id=1, source_target_pairs={{0,32},{32,64},{64,96},{1,33},{33,65},{65,97},{2,34},{34,66},{66,9... | collective-permute-start | bytes 1572872 | tf_op jit(solution)/shard_map/ppermute | solution.py:353
  94.5 0.1 pad_add_fusion.1.info
  94.6 21.1 %all-to-all-done.1.message = s16[32,264,128]{2,1,0:T(8,128)(2,1)S(1)} async-done(((s16[32,264,128]{2,1,0:T(8,128)(2,1)}), s16[32,264,128]{2,1,0:T(8,128)(2,1)S(1)}, u32[]{:S(2)}, u32[]{:S(2)}) %all-to-all-start.1) | async-done | bytes 2162720 | tf_op jit(solution)/shard_map/all_to_all | solution.py:390
  115.7 0.8 decode.1.mine
  116.5 7.2 %collective-permute-start.7 = (s16[264,128]{1,0:T(8,128)(2,1)S(1)}, s16[264,128]{1,0:T(8,128)(2,1)S(1)}, u32[]{:S(2)}, u32[]{:S(2)}) collective-permute-start(s16[264,128]{1,0:T(8,128)(2,1)S(1)} %decode.1.mine), channel_id=1, source_target_pairs={{0,96},{32,64},{64,32},{96,0},{1,97},{33,65},{65,33},{97,1},{2,98}... | collective-permute-start | bytes 202760 | tf_op jit(solution)/shard_map/ppermute | solution.py:393
  123.7 0.5 collective-permute-start.5
  124.2 1.9 %subtract_bitcast_fusion = f32[1,128,1024]{2,1,0:T(8,128)} fusion(f32[128,1024]{1,0:T(8,128)S(1)} %get-tuple-element.12, f32[128,1024]{1,0:T(8,128)} %collective-permute-done.2, f32[]{:T(128)S(6)} %convert_element_type.4, f32[1,128,1024]{2,1,0:T(8,128)S(1)} %copy-done.2), kind=kLoop, calls=%fused_computation.21 | loop fusion | flops 393216 | bytes 2097156 | tf_op jit(solution)/shard_map/broadcast_in_dim | solution.py:381
  126.1 0.0 collective-permute-done.7.by_both
  126.1 1.0 collective-permute-done.6.by_zlo
  127.1 0.0 collective-permute-done.5.by_core
  127.1 1.3 %lay_out.1 = (f32[32,1024]{1,0:T(8,128)}, f32[32,1024]{1,0:T(8,128)}, f32[1,32]{1,0:T(1,128)}) custom-call(s32[2]{0:T(128)S(1)} %pad_add_fusion.1.info, s16[264,128]{1,0:T(8,128)(2,1)S(1)} %decode.1.mine, s16[264,128]{1,0:T(8,128)(2,1)S(1)} %collective-permute-done.5.by_core, s16[264,128]{1,0:T(8,128)(2,1)S(1)} %collective-permute-done.6.by_zlo, ...), custom_call_target="tpu_custom_call" | custom-call | tf_op jit(solution)/shard_map/lay_out/pallas_call | solution.py:336
  (9 shorter events, 0.0 us)
Async XLA Ops:
  1.8 41.6 %copy-start.1 = (f32[1,128,1024]{2,1,0:T(8,128)S(1)}, f32[1,128,1024]{2,1,0:T(8,128)}, u32[]{:S(2)}) copy-start(f32[1,128,1024]{2,1,0:T(8,128)} %param.6) | copy-start | bytes 1572868
  1.8 52.2 %copy-start.3 = (f32[1,128,1024]{2,1,0:T(8,128)S(1)}, f32[1,128,1024]{2,1,0:T(8,128)}, u32[]{:S(2)}) copy-start(f32[1,128,1024]{2,1,0:T(8,128)} %param.7) | copy-start | bytes 1572868
  41.1 14.1 %copy-start = (f32[1024]{0:T(1024)S(1)}, f32[1024]{0:T(1024)}, u32[]{:S(2)}) copy-start(f32[1024]{0:T(1024)} %param.10) | copy-start | bytes 12292
  41.1 14.1 %collective-permute-start.1 = (bf16[1024,1024]{1,0:T(8,128)(2,1)S(1)}, bf16[1024,1024]{1,0:T(8,128)(2,1)}, u32[]{:S(2)}, u32[]{:S(2)}) collective-permute-start(bf16[1024,1024]{1,0:T(8,128)(2,1)S(1)} %bitcast.33), channel_id=1, source_target_pairs={{0,32},{32,0},{1,33},{33,1},{2,34},{34,2},{3,35},{35,3},{4,36},{36... | collective-permute-start | bytes 6291464 | tf_op jit(solution)/shard_map/ppermute | solution.py:357
  43.4 10.6 %collective-permute-start = (f32[128,1024]{1,0:T(8,128)S(1)}, f32[128,1024]{1,0:T(8,128)}, u32[]{:S(2)}, u32[]{:S(2)}) collective-permute-start(f32[128,1024]{1,0:T(8,128)S(1)} %bitcast.36), channel_id=1, source_target_pairs={{32,0},{64,32},{96,64},{33,1},{65,33},{97,65},{34,2},{66,34},{98,6... | collective-permute-start | bytes 1572872 | tf_op jit(solution)/shard_map/ppermute | solution.py:353
  67.9 9.1 %collective-permute-start.3 = (f32[1024,512]{1,0:T(8,128)S(1)}, f32[1024,512]{1,0:T(8,128)S(1)}, u32[]{:S(2)}, u32[]{:S(2)}) collective-permute-start(f32[1024,512]{1,0:T(8,128)S(1)} %fusion.2), channel_id=1, source_target_pairs={{0,32},{32,0},{1,33},{33,1},{2,34},{34,2},{3,35},{35,3},{4,36},{36... | collective-permute-start | bytes 6291464 | tf_op jit(solution)/shard_map/ppermute | solution.py:357
  73.1 6.8 %collective-permute-start.4 = (f32[1024,512]{1,0:T(8,128)S(1)}, f32[1024,512]{1,0:T(8,128)S(1)}, u32[]{:S(2)}, u32[]{:S(2)}) collective-permute-start(f32[1024,512]{1,0:T(8,128)S(1)} %fusion), channel_id=1, source_target_pairs={{0,32},{32,0},{1,33},{33,1},{2,34},{34,2},{3,35},{35,3},{4,36},{36... | collective-permute-start | bytes 6291464 | tf_op jit(solution)/shard_map/ppermute | solution.py:357
  82.5 33.1 %all-to-all-start.1 = ((s16[32,264,128]{2,1,0:T(8,128)(2,1)}), s16[32,264,128]{2,1,0:T(8,128)(2,1)S(1)}, u32[]{:S(2)}, u32[]{:S(2)}) async-start(s16[32,264,128]{2,1,0:T(8,128)(2,1)} %code.1), calls=%async_computation.1 | async-start | bytes 4325376 | tf_op jit(solution)/shard_map/all_to_all | solution.py:390
  86.6 37.6 %collective-permute-start.2 = (f32[128,1024]{1,0:T(8,128)S(1)}, f32[128,1024]{1,0:T(8,128)}, u32[]{:S(2)}, u32[]{:S(2)}) collective-permute-start(f32[128,1024]{1,0:T(8,128)S(1)} %get-tuple-element.13), channel_id=1, source_target_pairs={{0,32},{32,64},{64,96},{1,33},{33,65},{65,97},{2,34},{34,66},{66,9... | collective-permute-start | bytes 1572872 | tf_op jit(solution)/shard_map/ppermute | solution.py:353
  115.7 8.5 %copy-start.2 = (f32[1,128,1024]{2,1,0:T(8,128)S(1)}, f32[1,128,1024]{2,1,0:T(8,128)}, u32[]{:S(2)}) copy-start(f32[1,128,1024]{2,1,0:T(8,128)} %param.6) | copy-start | bytes 1572868
  116.5 9.7 %collective-permute-start.7 = (s16[264,128]{1,0:T(8,128)(2,1)S(1)}, s16[264,128]{1,0:T(8,128)(2,1)S(1)}, u32[]{:S(2)}, u32[]{:S(2)}) collective-permute-start(s16[264,128]{1,0:T(8,128)(2,1)S(1)} %decode.1.mine), channel_id=1, source_target_pairs={{0,96},{32,64},{64,32},{96,0},{1,97},{33,65},{65,33},{97,1},{2,98}... | collective-permute-start | bytes 202760 | tf_op jit(solution)/shard_map/ppermute | solution.py:393
  123.7 3.4 %collective-permute-start.6 = (s16[264,128]{1,0:T(8,128)(2,1)S(1)}, s16[264,128]{1,0:T(8,128)(2,1)S(1)}, u32[]{:S(2)}, u32[]{:S(2)}) collective-permute-start(s16[264,128]{1,0:T(8,128)(2,1)S(1)} %decode.1.mine), channel_id=1, source_target_pairs={{0,64},{32,96},{64,0},{96,32},{1,65},{33,97},{65,1},{97,33},{2,66}... | collective-permute-start | bytes 202760 | tf_op jit(solution)/shard_map/ppermute | solution.py:393
  123.7 3.4 %collective-permute-start.5 = (s16[264,128]{1,0:T(8,128)(2,1)S(1)}, s16[264,128]{1,0:T(8,128)(2,1)S(1)}, u32[]{:S(2)}, u32[]{:S(2)}) collective-permute-start(s16[264,128]{1,0:T(8,128)(2,1)S(1)} %decode.1.mine), channel_id=1, source_target_pairs={{0,32},{32,0},{64,96},{96,64},{1,33},{33,1},{65,97},{97,65},{2,34}... | collective-permute-start | bytes 202760 | tf_op jit(solution)/shard_map/ppermute | solution.py:393

commit v6 on v5

--- a/solution.py
+++ b/solution.py
@@ -28,22 +28,20 @@
     return jnp.dot(left, right, preferred_element_type=f32)
 
 
-def integrate_kernel(
+def forward_kernel(
     info, given, bias_in, own_w, other_w,
-    ends, bar, bias, left, right,
-    w, w_turned, state, tanhs, total, sems,
+    ends, left, w_turned, tanhs,
+    w, state, total, sems,
 ):
-    count, core, has_next = info[0], info[1], info[2].astype(f32)
+    count, core = info[0], info[1]
     slot_in = 1 - core
     slot_out = core
     rows = state.shape[0]
-    middle = right.shape[3]
     first = pltpu.make_async_copy(own_w, w.at[core], sems.at[0])
     second = pltpu.make_async_copy(other_w, w.at[1 - core], sems.at[1])
     first.start()
     second.start()
     state[...] = given[0]
-    bias[...] = jnp.zeros_like(bias)
     offset = bias_in[...]
     first.wait()
     second.wait()
@@ -60,25 +58,13 @@
         left[slot_out, place(at), :] = low
         return product(low, w[1])
 
-    def field_back(q, at):
-        outer = q.astype(bf16)
-        right[slot_out, 0, place(at), :] = outer[:, :middle]
-        right[slot_out, 1, place(at), :] = outer[:, middle:]
-        hidden = tanhs[at]
-        inner = product(outer, w_turned[1]) * (1.0 - hidden * hidden)
-        bias[...] += jnp.sum(inner, axis=0, keepdims=True)
-        low = inner.astype(bf16)
-        right[slot_in, 0, place(at), :] = low[:, :middle]
-        right[slot_in, 1, place(at), :] = low[:, middle:]
-        return product(low, w_turned[0])
-
     def turn(part):
         quarter = w.shape[1] // STAGES
         for which in range(2):
             rows_now = pl.ds(part * quarter, quarter)
             w_turned[which, :, rows_now] = w[which, rows_now, :].T
 
-    def forward(s, carry, beside=lambda part: None):
+    def step(s, carry, beside=lambda part: None):
         at = STAGES * s
         beside(0)
         k = field(state[...], at)
@@ -94,13 +80,50 @@
         state[...] = state[...] + step_size / 6.0 * (total[...] + k)
         return carry
 
-    forward(0, 0, turn)
-    lax.fori_loop(1, count, forward, 0)
-    end = state[...]
-    ends[...] = end
-    state[...] = (end - given[1]) + penalty * ((end - given[2]) * has_next)
-
-    def backward(turn, carry):
+    step(0, 0, turn)
+    lax.fori_loop(1, count, step, 0)
+    ends[...] = state[...]
+
+    def clear(s, carry):
+        block = pl.ds(pl.multiple_of(s * STAGES * rows, STAGES * rows), STAGES * rows)
+        for slot in range(2):
+            left[slot, block, :] = jnp.zeros((STAGES * rows, left.shape[2]), bf16)
+        return carry
+
+    lax.fori_loop(count, MAXSTEP, clear, 0)
+
+
+def backward_kernel(
+    info, given, following, ends, w_turned, tanhs, bar, bias, right, state, total, after, sem
+):
+    count, core, has_next = info[0], info[1], info[2].astype(f32)
+    slot_in = 1 - core
+    slot_out = core
+    rows = state.shape[0]
+    middle = right.shape[3]
+    arrive = pltpu.make_async_copy(following, after, sem)
+    arrive.start()
+    bias[...] = jnp.zeros_like(bias)
+    end = ends[...]
+    arrive.wait()
+    state[...] = (end - given[1]) + penalty * ((end - after[...]) * has_next)
+
+    def place(at):
+        return pl.ds(pl.multiple_of(at * rows, rows), rows)
+
+    def field_back(q, at):
+        outer = q.astype(bf16)
+        right[slot_out, 0, place(at), :] = outer[:, :middle]
+        right[slot_out, 1, place(at), :] = outer[:, middle:]
+        hidden = tanhs[at]
+        inner = product(outer, w_turned[1]) * (1.0 - hidden * hidden)
+        bias[...] += jnp.sum(inner, axis=0, keepdims=True)
+        low = inner.astype(bf16)
+        right[slot_in, 0, place(at), :] = low[:, :middle]
+        right[slot_in, 1, place(at), :] = low[:, middle:]
+        return product(low, w_turned[0])
+
+    def step(turn, carry):
         at = STAGES * (count - 1 - turn)
         g = field_back(step_size / 6.0 * state[...], at + 3)
         total[...] = state[...] + g
@@ -112,13 +135,12 @@
         state[...] = total[...] + g
         return carry
 
-    lax.fori_loop(0, count, backward, 0)
+    lax.fori_loop(0, count, step, 0)
     bar[...] = state[...]
 
     def clear(s, carry):
         block = pl.ds(pl.multiple_of(s * STAGES * rows, STAGES * rows), STAGES * rows)
         for slot in range(2):
-            left[slot, block, :] = jnp.zeros((STAGES * rows, left.shape[2]), bf16)
             for half in range(2):
                 right[slot, half, block, :] = jnp.zeros((STAGES * rows, middle), bf16)
         return carry
@@ -126,29 +148,47 @@
     lax.fori_loop(count, MAXSTEP, clear, 0)
 
 
-def integrate(info, given, bias_in, own_w, other_w):
+def forward(info, given, bias_in, own_w, other_w):
     _, rows, width = given.shape
     depth = own_w.shape[1]
     terms = MAXSTEP * STAGES * rows
-    lefts = jax.ShapeDtypeStruct((2, terms, width), bf16)
-    rights = jax.ShapeDtypeStruct((2, 2, terms, width // 2), bf16)
-    states = jax.ShapeDtypeStruct((rows, width), f32)
     return pl.pallas_call(
-        integrate_kernel,
-        out_shape=(states, states, jax.ShapeDtypeStruct((1, depth), f32), lefts, rights),
+        forward_kernel,
+        out_shape=(
+            jax.ShapeDtypeStruct((rows, width), f32),
+            jax.ShapeDtypeStruct((2, terms, width), bf16),
+            jax.ShapeDtypeStruct((2, depth, width), bf16),
+            jax.ShapeDtypeStruct((MAXSTEP * STAGES, rows, depth), f32),
+        ),
         in_specs=[SMEM] + [VMEM] * 2 + [ANY] * 2,
-        out_specs=(VMEM,) * 5,
+        out_specs=(VMEM,) * 4,
         scratch_shapes=[
             pltpu.VMEM((2, width, depth), bf16),
-            pltpu.VMEM((2, depth, width), bf16),
             pltpu.VMEM((rows, width), f32),
-            pltpu.VMEM((MAXSTEP * STAGES, rows, depth), f32),
             pltpu.VMEM((rows, width), f32),
             pltpu.SemaphoreType.DMA((2,)),
         ],
-        compiler_params=pltpu.CompilerParams(vmem_limit_bytes=32 * 1024 * 1024),
-        name="integrate",
+        compiler_params=pltpu.CompilerParams(vmem_limit_bytes=26 * 1024 * 1024),
+        name="forward",
     )(info, given, bias_in, own_w, other_w)
+
+
+def backward(info, given, following, ends, w_turned, tanhs):
+    rows, width = ends.shape
+    depth = w_turned.shape[1]
+    return pl.pallas_call(
+        backward_kernel,
+        out_shape=(
+            jax.ShapeDtypeStruct((rows, width), f32),
+            jax.ShapeDtypeStruct((1, depth), f32),
+            jax.ShapeDtypeStruct((2, 2, MAXSTEP * STAGES * rows, width // 2), bf16),
+        ),
+        in_specs=[SMEM, VMEM, ANY] + [VMEM] * 3,
+        out_specs=(VMEM,) * 3,
+        scratch_shapes=[pltpu.VMEM((rows, width), f32)] * 3 + [pltpu.SemaphoreType.DMA],
+        compiler_params=pltpu.CompilerParams(vmem_limit_bytes=22 * 1024 * 1024),
+        name="backward",
+    )(info, given, following, ends, w_turned, tanhs)
 
 
 def level_of(peak):
@@ -371,11 +411,12 @@
     own_w = lax.all_to_all(copies, "batch", 0, 0)
     own_w = own_w.reshape(batches * own, width)
     other_w = swap(own_w)
-    given = jnp.stack([start, targets[0], following])
+    given = jnp.stack([start, targets[0]])
 
     has_next = (place < lax.axis_size(SEG) - 1).astype(jnp.int32)
     info = jnp.stack([counts[0], core, has_next])
-    ends, bar, bias, left, right = integrate(info, given, b_in[None], own_w, other_w)
+    ends, left, w_turned, tanhs = forward(info, given, b_in[None], own_w, other_w)
+    bar, bias, right = backward(info, given, pltpu.with_memory_space_constraint(following, pltpu.HBM), ends, w_turned, tanhs)
     previous = shift_seg(ends, 1)
     has_prev = (place > 0).astype(f32)
     grad_starts = (bar - penalty * ((previous - start) * has_prev))[None]

time: 129 us -> 126 us (0.977)
  starting transfers between devices: 29.2 us -> 25.2 us
  Pallas kernels: 13.7 us -> 15.3 us
    ppermute x2, waiting for transfers between devices: 7.94 us -> 1.1 us  [shift_seg(): return lax.ppermute(block, SEG, route)]
    ppermute x3, starting transfers between devices: 7.65 us -> 12.7 us  [swap(): return lax.ppermute(block, 'core', [(0, 1), (1, 0)])]
    ppermute x2, starting transfers between devices: 9.77 us -> 5.11 us  [shift_seg(): return lax.ppermute(block, SEG, route)]
    all_to_all x1, waiting for transfers between devices: 21.1 us -> 25.8 us  [body(): message = lax.all_to_all(message, 'batch', 0, 0)]
    ppermute x3, starting transfers between devices: 7.72 us -> 3.3 us  [body(): lax.ppermute(mine, SEG, [(i, i ^ flip) for i in range(4)])]
    pallas_call x1 -> x2, Pallas kernels: 9.01 us -> 10.7 us  [the longest x1 5.57 us: forward(): pl.pallas_call(forward_kernel, out_shape=(jax.ShapeDtypeStruct((rows, wid...]
  transfers between devices with their start and end apart: 9 -> 9, of which waited for: 4 -> 5; matrix products, arithmetic and copies ran while one was open for 5% -> 5% of each run, Pallas kernels for 1% -> 5%
where the time goes in v6:
time: 126 us; the launch traced here: 124 us
  blocking collectives  39.3 us (31%)
  waiting for transfers between devices  32.4 us (26%)
  starting transfers between devices  25.2 us (20%)
  Pallas kernels  15.3 us (12%)
  matrix products  7.36 us (6%)
  other arithmetic  3.11 us (2%)
  between operations  1.44 us (1%)
    all_to_all x1, blocking collectives, body(): own_w = lax.all_to_all(copies, 'batch', 0, 0)  39.3 us
    all_to_all x1, waiting for transfers between devices, body(): message = lax.all_to_all(message, 'batch', 0, 0)  25.8 us
    ppermute x3, starting transfers between devices, swap(): return lax.ppermute(block, 'core', [(0, 1), (1, 0)])  12.7 us
    dot_general x4, matrix products, contract_rows(): lax.dot_general(left, right, (((0,), (0,)), ((), ())), preferred_element_...  7.36 us
    pallas_call x1, Pallas kernels, forward(): pl.pallas_call(forward_kernel, out_shape=(jax.ShapeDtypeStruct((rows, wid...  5.57 us
    pallas_call x1, Pallas kernels, backward(): pl.pallas_call(backward_kernel, out_shape=(jax.ShapeDtypeStruct((rows, wi...  5.17 us
    ppermute x2, starting transfers between devices, shift_seg(): return lax.ppermute(block, SEG, route)  5.11 us
    ppermute x3, waiting for transfers between devices, swap(): return lax.ppermute(block, 'core', [(0, 1), (1, 0)])  4.18 us
  transfers between devices with their start and end apart: 9, of which 5 were waited for; matrix products, arithmetic and copies ran while one was open for 5% of the time, Pallas kernels for 5%

profile of v6, /device:TPU:1, one launch (start us, length us, event | category | flops | bytes accessed | tf_op | source)
XLA Modules:
  0.0 124.4 jit_solution(14430735955363161255)
XLA Ops:
  0.6 0.9 broadcast_select_fusion
  1.5 0.0 copy-start.1
  1.5 0.2 broadcast_in_dim.13
  1.8 0.0 copy-start.2
  1.8 0.0 copy-start
  1.8 39.3 %all_to_all.10 = bf16[32,32,1024]{2,1,0:T(8,128)(2,1)S(1)} all-to-all(bf16[32,32,1024]{2,1,0:T(8,128)(2,1)S(1)} %broadcast_in_dim.13), channel_id=1, replica_groups=mesh['zlo'=2,'core'=2,'batch'=32] {'batch'}, dimensions={0} | all-to-all | bytes 4194304 | tf_op jit(solution)/shard_map/all_to_all | solution.py:411
  41.1 2.3 %collective-permute-start.1 = (bf16[1024,1024]{1,0:T(8,128)(2,1)S(1)}, bf16[1024,1024]{1,0:T(8,128)(2,1)}, u32[]{:S(2)}, u32[]{:S(2)}) collective-permute-start(bf16[1024,1024]{1,0:T(8,128)(2,1)S(1)} %bitcast.32), channel_id=1, source_target_pairs={{0,32},{32,0},{1,33},{33,1},{2,34},{34,2},{3,35},{35,3},{4,36},{36... | collective-permute-start | bytes 6291464 | tf_op jit(solution)/shard_map/ppermute | solution.py:397
  43.4 1.9 %collective-permute-start = (f32[128,1024]{1,0:T(8,128)S(1)}, f32[128,1024]{1,0:T(8,128)}, u32[]{:S(2)}, u32[]{:S(2)}) collective-permute-start(f32[128,1024]{1,0:T(8,128)S(1)} %bitcast.35), channel_id=1, source_target_pairs={{32,0},{64,32},{96,64},{33,1},{65,33},{97,65},{34,2},{66,34},{98,6... | collective-permute-start | bytes 1572872 | tf_op jit(solution)/shard_map/ppermute | solution.py:393
  46.0 0.1 pad_add_fusion.info
  46.1 1.2 collective-permute-done.1.other_w
  47.3 5.6 %forward.1 = (f32[128,1024]{1,0:T(8,128)S(1)}, bf16[2,1536,1024]{2,1,0:T(8,128)(2,1)S(1)}, bf16[2,1024,1024]{2,1,0:T(8,128)(2,1)S(1)}, f32[12,128,1024]{2,1,0:T(8,128)S(1)}) custom-call(s32[3]{0:T(128)S(1)} %pad_add_fusion.info, f32[2,128,1024]{2,1,0:T(8,128)S(1)} %constant_dynamic-update-slice_fusion.given, f32[1,1024]{1,0:T(1,128)S(1)} %bitcast.34, ...), custom_call_target="tpu_custom_call" | custom-call | tf_op jit(solution)/shard_map/forward/pallas_call | solution.py:155
  52.9 1.1 collective-permute-done.following
  54.0 5.2 %backward.1 = (f32[128,1024]{1,0:T(8,128)S(1)}, f32[1,1024]{1,0:T(1,128)S(1)}, bf16[2,2,1536,512]{3,2,1,0:T(8,128)(2,1)S(1)}) custom-call(s32[3]{0:T(128)S(1)} %pad_add_fusion.info, f32[2,128,1024]{2,1,0:T(8,128)S(1)} %constant_dynamic-update-slice_fusion.given, f32[128,1024]{1,0:T(8,128)} %collective-permute-done.following, ...), custom_call_target="tpu_custom_call" | custom-call | tf_op jit(solution)/shard_map/backward/pallas_call | solution.py:179
  59.2 1.8 %fusion = f32[1024,512]{1,0:T(8,128)S(1)} fusion(bf16[2,1536,1024]{2,1,0:T(8,128)(2,1)S(1)} %get-tuple-element.18, bf16[2,2,1536,512]{3,2,1,0:T(8,128)(2,1)S(1)} %get-tuple-element.19), kind=kOutput, calls=%fused_computation | convolution fusion | flops 1610612736 | bytes 6815744 | tf_op jit(solution)/shard_map/dot_general | solution.py:387
  61.0 1.8 %fusion.2 = f32[1024,512]{1,0:T(8,128)S(1)} fusion(bf16[2,1536,1024]{2,1,0:T(8,128)(2,1)S(1)} %get-tuple-element.18, bf16[2,2,1536,512]{3,2,1,0:T(8,128)(2,1)S(1)} %get-tuple-element.19), kind=kOutput, calls=%fused_computation.2 | convolution fusion | flops 1610612736 | bytes 6815744 | tf_op jit(solution)/shard_map/dot_general | solution.py:387
  62.9 10.3 %collective-permute-start.3 = (f32[1024,512]{1,0:T(8,128)S(1)}, f32[1024,512]{1,0:T(8,128)S(1)}, u32[]{:S(2)}, u32[]{:S(2)}) collective-permute-start(f32[1024,512]{1,0:T(8,128)S(1)} %fusion.2), channel_id=1, source_target_pairs={{0,32},{32,0},{1,33},{33,1},{2,34},{34,2},{3,35},{35,3},{4,36},{36... | collective-permute-start | bytes 6291464 | tf_op jit(solution)/shard_map/ppermute | solution.py:397
  73.2 0.1 collective-permute-start.4
  73.3 1.8 %fusion.4.keep_high = f32[1024,512]{1,0:T(8,128)S(1)} fusion(bf16[2,1536,1024]{2,1,0:T(8,128)(2,1)S(1)} %get-tuple-element.18, bf16[2,2,1536,512]{3,2,1,0:T(8,128)(2,1)S(1)} %get-tuple-element.19), kind=kOutput, calls=%fused_computation.4 | convolution fusion | flops 1610612736 | bytes 6815744 | tf_op jit(solution)/shard_map/dot_general | solution.py:387
  75.1 1.8 %fusion.6.keep_low = f32[1024,512]{1,0:T(8,128)S(1)} fusion(bf16[2,1536,1024]{2,1,0:T(8,128)(2,1)S(1)} %get-tuple-element.18, bf16[2,2,1536,512]{3,2,1,0:T(8,128)(2,1)S(1)} %get-tuple-element.19), kind=kOutput, calls=%fused_computation.6 | convolution fusion | flops 1610612736 | bytes 6815744 | tf_op jit(solution)/shard_map/dot_general | solution.py:387
  77.0 0.0 collective-permute-done.3.got_low
  77.0 3.0 %collective-permute-done.4.got_high = f32[1024,512]{1,0:T(8,128)S(1)} collective-permute-done((f32[1024,512]{1,0:T(8,128)S(1)}, f32[1024,512]{1,0:T(8,128)S(1)}, u32[]{:S(2)}, u32[]{:S(2)}) %collective-permute-start.4) | collective-permute-done | bytes 2097184 | tf_op jit(solution)/shard_map/ppermute | solution.py:397
  80.0 2.4 %code.1 = s16[32,264,128]{2,1,0:T(8,128)(2,1)} custom-call(f32[1024,512]{1,0:T(8,128)S(1)} %fusion.6.keep_low, f32[1024,512]{1,0:T(8,128)S(1)} %fusion.4.keep_high, f32[1024,512]{1,0:T(8,128)S(1)} %collective-permute-done.3.got_low, f32[1024,512]{1,0:T(8,128)S(1)} %collective-permute-done.4.got_high, f32[1,1024]{1,0:T(1,128)S(1)} %get-tuple-element.20.bias), custom_call_target="tpu_custom_call" | custom-call | tf_op jit(solution)/shard_map/code/pallas_call | solution.py:272
  82.4 4.1 %all-to-all-start.1 = ((s16[32,264,128]{2,1,0:T(8,128)(2,1)}), s16[32,264,128]{2,1,0:T(8,128)(2,1)S(1)}, u32[]{:S(2)}, u32[]{:S(2)}) async-start(s16[32,264,128]{2,1,0:T(8,128)(2,1)} %code.1), calls=%async_computation.1 | async-start | bytes 4325376 | tf_op jit(solution)/shard_map/all_to_all | solution.py:431
  86.5 3.2 %collective-permute-start.2 = (f32[128,1024]{1,0:T(8,128)S(1)}, f32[128,1024]{1,0:T(8,128)}, u32[]{:S(2)}, u32[]{:S(2)}) collective-permute-start(f32[128,1024]{1,0:T(8,128)S(1)} %get-tuple-element.14.ends), channel_id=1, source_target_pairs={{0,32},{32,64},{64,96},{1,33},{33,65},{65,97},{2,34},{34,66},{66,9... | collective-permute-start | bytes 1572872 | tf_op jit(solution)/shard_map/ppermute | solution.py:393
  89.7 0.1 pad_add_fusion.1.info
  89.8 25.8 %all-to-all-done.1.message = s16[32,264,128]{2,1,0:T(8,128)(2,1)S(1)} async-done(((s16[32,264,128]{2,1,0:T(8,128)(2,1)}), s16[32,264,128]{2,1,0:T(8,128)(2,1)S(1)}, u32[]{:S(2)}, u32[]{:S(2)}) %all-to-all-start.1) | async-done | bytes 2162720 | tf_op jit(solution)/shard_map/all_to_all | solution.py:431
  115.5 0.8 decode.1.mine
  116.3 2.6 %collective-permute-start.7 = (s16[264,128]{1,0:T(8,128)(2,1)S(1)}, s16[264,128]{1,0:T(8,128)(2,1)S(1)}, u32[]{:S(2)}, u32[]{:S(2)}) collective-permute-start(s16[264,128]{1,0:T(8,128)(2,1)S(1)} %decode.1.mine), channel_id=1, source_target_pairs={{0,96},{32,64},{64,32},{96,0},{1,97},{33,65},{65,33},{97,1},{2,98}... | collective-permute-start | bytes 202760 | tf_op jit(solution)/shard_map/ppermute | solution.py:434
  118.9 0.7 collective-permute-start.6
  119.6 2.1 %subtract_bitcast_fusion = f32[1,128,1024]{2,1,0:T(8,128)} fusion(f32[128,1024]{1,0:T(8,128)S(1)} %get-tuple-element.17, f32[128,1024]{1,0:T(8,128)} %collective-permute-done.2, f32[]{:T(128)S(6)} %convert_element_type.4, f32[1,128,1024]{2,1,0:T(8,128)} %param.6), kind=kLoop, calls=%fused_computation.20 | loop fusion | flops 393216 | bytes 2097156 | tf_op jit(solution)/shard_map/broadcast_in_dim | solution.py:422
  121.7 1.3 %collective-permute-done.6.by_zlo = s16[264,128]{1,0:T(8,128)(2,1)S(1)} collective-permute-done((s16[264,128]{1,0:T(8,128)(2,1)S(1)}, s16[264,128]{1,0:T(8,128)(2,1)S(1)}, u32[]{:S(2)}, u32[]{:S(2)}) %collective-permute-start.6) | collective-permute-done | bytes 67616 | tf_op jit(solution)/shard_map/ppermute | solution.py:434
  123.0 1.3 %lay_out.1 = (f32[32,1024]{1,0:T(8,128)}, f32[32,1024]{1,0:T(8,128)}, f32[1,32]{1,0:T(1,128)}) custom-call(s32[2]{0:T(128)S(1)} %pad_add_fusion.1.info, s16[264,128]{1,0:T(8,128)(2,1)S(1)} %decode.1.mine, s16[264,128]{1,0:T(8,128)(2,1)S(1)} %collective-permute-done.5.by_core, s16[264,128]{1,0:T(8,128)(2,1)S(1)} %collective-permute-done.6.by_zlo, ...), custom_call_target="tpu_custom_call" | custom-call | tf_op jit(solution)/shard_map/lay_out/pallas_call | solution.py:376
  (9 shorter events, 0.1 us)
Async XLA Ops:
  1.5 41.9 %copy-start.1 = (f32[1,128,1024]{2,1,0:T(8,128)S(1)}, f32[1,128,1024]{2,1,0:T(8,128)}, u32[]{:S(2)}) copy-start(f32[1,128,1024]{2,1,0:T(8,128)} %param.6) | copy-start | bytes 1572868
  1.8 44.3 %copy-start.2 = (f32[1,128,1024]{2,1,0:T(8,128)S(1)}, f32[1,128,1024]{2,1,0:T(8,128)}, u32[]{:S(2)}) copy-start(f32[1,128,1024]{2,1,0:T(8,128)} %param.7) | copy-start | bytes 1572868
  1.8 45.5 %copy-start = (f32[1024]{0:T(1024)S(1)}, f32[1024]{0:T(1024)}, u32[]{:S(2)}) copy-start(f32[1024]{0:T(1024)} %param.10) | copy-start | bytes 12292
  41.1 6.2 %collective-permute-start.1 = (bf16[1024,1024]{1,0:T(8,128)(2,1)S(1)}, bf16[1024,1024]{1,0:T(8,128)(2,1)}, u32[]{:S(2)}, u32[]{:S(2)}) collective-permute-start(bf16[1024,1024]{1,0:T(8,128)(2,1)S(1)} %bitcast.32), channel_id=1, source_target_pairs={{0,32},{32,0},{1,33},{33,1},{2,34},{34,2},{3,35},{35,3},{4,36},{36... | collective-permute-start | bytes 6291464 | tf_op jit(solution)/shard_map/ppermute | solution.py:397
  43.4 10.6 %collective-permute-start = (f32[128,1024]{1,0:T(8,128)S(1)}, f32[128,1024]{1,0:T(8,128)}, u32[]{:S(2)}, u32[]{:S(2)}) collective-permute-start(f32[128,1024]{1,0:T(8,128)S(1)} %bitcast.35), channel_id=1, source_target_pairs={{32,0},{64,32},{96,64},{33,1},{65,33},{97,65},{34,2},{66,34},{98,6... | collective-permute-start | bytes 1572872 | tf_op jit(solution)/shard_map/ppermute | solution.py:393
  62.9 14.1 %collective-permute-start.3 = (f32[1024,512]{1,0:T(8,128)S(1)}, f32[1024,512]{1,0:T(8,128)S(1)}, u32[]{:S(2)}, u32[]{:S(2)}) collective-permute-start(f32[1024,512]{1,0:T(8,128)S(1)} %fusion.2), channel_id=1, source_target_pairs={{0,32},{32,0},{1,33},{33,1},{2,34},{34,2},{3,35},{35,3},{4,36},{36... | collective-permute-start | bytes 6291464 | tf_op jit(solution)/shard_map/ppermute | solution.py:397
  73.2 6.8 %collective-permute-start.4 = (f32[1024,512]{1,0:T(8,128)S(1)}, f32[1024,512]{1,0:T(8,128)S(1)}, u32[]{:S(2)}, u32[]{:S(2)}) collective-permute-start(f32[1024,512]{1,0:T(8,128)S(1)} %fusion), channel_id=1, source_target_pairs={{0,32},{32,0},{1,33},{33,1},{2,34},{34,2},{3,35},{35,3},{4,36},{36... | collective-permute-start | bytes 6291464 | tf_op jit(solution)/shard_map/ppermute | solution.py:397
  82.4 33.1 %all-to-all-start.1 = ((s16[32,264,128]{2,1,0:T(8,128)(2,1)}), s16[32,264,128]{2,1,0:T(8,128)(2,1)S(1)}, u32[]{:S(2)}, u32[]{:S(2)}) async-start(s16[32,264,128]{2,1,0:T(8,128)(2,1)} %code.1), calls=%async_computation.1 | async-start | bytes 4325376 | tf_op jit(solution)/shard_map/all_to_all | solution.py:431
  86.5 33.1 %collective-permute-start.2 = (f32[128,1024]{1,0:T(8,128)S(1)}, f32[128,1024]{1,0:T(8,128)}, u32[]{:S(2)}, u32[]{:S(2)}) collective-permute-start(f32[128,1024]{1,0:T(8,128)S(1)} %get-tuple-element.14.ends), channel_id=1, source_target_pairs={{0,32},{32,64},{64,96},{1,33},{33,65},{65,97},{2,34},{34,66},{66,9... | collective-permute-start | bytes 1572872 | tf_op jit(solution)/shard_map/ppermute | solution.py:393
  116.3 5.4 %collective-permute-start.7 = (s16[264,128]{1,0:T(8,128)(2,1)S(1)}, s16[264,128]{1,0:T(8,128)(2,1)S(1)}, u32[]{:S(2)}, u32[]{:S(2)}) collective-permute-start(s16[264,128]{1,0:T(8,128)(2,1)S(1)} %decode.1.mine), channel_id=1, source_target_pairs={{0,96},{32,64},{64,32},{96,0},{1,97},{33,65},{65,33},{97,1},{2,98}... | collective-permute-start | bytes 202760 | tf_op jit(solution)/shard_map/ppermute | solution.py:434
  118.9 4.1 %collective-permute-start.6 = (s16[264,128]{1,0:T(8,128)(2,1)S(1)}, s16[264,128]{1,0:T(8,128)(2,1)S(1)}, u32[]{:S(2)}, u32[]{:S(2)}) collective-permute-start(s16[264,128]{1,0:T(8,128)(2,1)S(1)} %decode.1.mine), channel_id=1, source_target_pairs={{0,64},{32,96},{64,0},{96,32},{1,65},{33,97},{65,1},{97,33},{2,66}... | collective-permute-start | bytes 202760 | tf_op jit(solution)/shard_map/ppermute | solution.py:434
  119.6 3.4 %collective-permute-start.5 = (s16[264,128]{1,0:T(8,128)(2,1)S(1)}, s16[264,128]{1,0:T(8,128)(2,1)S(1)}, u32[]{:S(2)}, u32[]{:S(2)}) collective-permute-start(s16[264,128]{1,0:T(8,128)(2,1)S(1)} %decode.1.mine), channel_id=1, source_target_pairs={{0,32},{32,0},{64,96},{96,64},{1,33},{33,1},{65,97},{97,65},{2,34}... | collective-permute-start | bytes 202760 | tf_op jit(solution)/shard_map/ppermute | solution.py:434

commit v7 on v6

--- a/solution.py
+++ b/solution.py
@@ -22,6 +22,10 @@
 VMEM = pl.BlockSpec(memory_space=pltpu.VMEM)
 ANY = pl.BlockSpec(memory_space=pl.ANY)
 SMEM = pl.BlockSpec(memory_space=pltpu.SMEM)
+
+
+def packed_options(mebibytes):
+    return pltpu.CompilerParams(vmem_limit_bytes=mebibytes * 1024 * 1024)
 
 
 def product(left, right):
@@ -168,7 +172,7 @@
             pltpu.VMEM((rows, width), f32),
             pltpu.SemaphoreType.DMA((2,)),
         ],
-        compiler_params=pltpu.CompilerParams(vmem_limit_bytes=26 * 1024 * 1024),
+        compiler_params=packed_options(26),
         name="forward",
     )(info, given, bias_in, own_w, other_w)
 
@@ -186,7 +190,7 @@
         in_specs=[SMEM, VMEM, ANY] + [VMEM] * 3,
         out_specs=(VMEM,) * 3,
         scratch_shapes=[pltpu.VMEM((rows, width), f32)] * 3 + [pltpu.SemaphoreType.DMA],
-        compiler_params=pltpu.CompilerParams(vmem_limit_bytes=22 * 1024 * 1024),
+        compiler_params=packed_options(22),
         name="backward",
     )(info, given, following, ends, w_turned, tanhs)
 

time: 126 us -> 126 us (level)
  no operation moved by 1% of the time
where the time goes in v7:
time: 126 us; the launch traced here: 124 us
  blocking collectives  39.3 us (31%)
  waiting for transfers between devices  32.4 us (26%)
  starting transfers between devices  25.2 us (20%)
  Pallas kernels  15.3 us (12%)
  matrix products  7.36 us (6%)
  other arithmetic  3.11 us (2%)
  between operations  1.44 us (1%)
    all_to_all x1, blocking collectives, body(): own_w = lax.all_to_all(copies, 'batch', 0, 0)  39.3 us
    all_to_all x1, waiting for transfers between devices, body(): message = lax.all_to_all(message, 'batch', 0, 0)  25.8 us
    ppermute x3, starting transfers between devices, swap(): return lax.ppermute(block, 'core', [(0, 1), (1, 0)])  12.7 us
    dot_general x4, matrix products, contract_rows(): lax.dot_general(left, right, (((0,), (0,)), ((), ())), preferred_element_...  7.36 us
    pallas_call x1, Pallas kernels, forward(): pl.pallas_call(forward_kernel, out_shape=(jax.ShapeDtypeStruct((rows, wid...  5.57 us
    pallas_call x1, Pallas kernels, backward(): pl.pallas_call(backward_kernel, out_shape=(jax.ShapeDtypeStruct((rows, wi...  5.17 us
    ppermute x2, starting transfers between devices, shift_seg(): return lax.ppermute(block, SEG, route)  5.11 us
    ppermute x3, waiting for transfers between devices, swap(): return lax.ppermute(block, 'core', [(0, 1), (1, 0)])  4.18 us
  transfers between devices with their start and end apart: 9, of which 5 were waited for; matrix products, arithmetic and copies ran while one was open for 5% of the time, Pallas kernels for 5%

profile of v7, /device:TPU:1, one launch (start us, length us, event | category | flops | bytes accessed | tf_op | source)
XLA Modules:
  0.0 124.4 jit_solution(14430735955363161255)
XLA Ops:
  0.6 0.9 broadcast_select_fusion
  1.5 0.0 copy-start.1
  1.5 0.2 broadcast_in_dim.13
  1.8 0.0 copy-start.2
  1.8 0.0 copy-start
  1.8 39.3 %all_to_all.10 = bf16[32,32,1024]{2,1,0:T(8,128)(2,1)S(1)} all-to-all(bf16[32,32,1024]{2,1,0:T(8,128)(2,1)S(1)} %broadcast_in_dim.13), channel_id=1, replica_groups=mesh['zlo'=2,'core'=2,'batch'=32] {'batch'}, dimensions={0} | all-to-all | bytes 4194304 | tf_op jit(solution)/shard_map/all_to_all | solution.py:415
  41.1 2.3 %collective-permute-start.1 = (bf16[1024,1024]{1,0:T(8,128)(2,1)S(1)}, bf16[1024,1024]{1,0:T(8,128)(2,1)}, u32[]{:S(2)}, u32[]{:S(2)}) collective-permute-start(bf16[1024,1024]{1,0:T(8,128)(2,1)S(1)} %bitcast.32), channel_id=1, source_target_pairs={{0,32},{32,0},{1,33},{33,1},{2,34},{34,2},{3,35},{35,3},{4,36},{36... | collective-permute-start | bytes 6291464 | tf_op jit(solution)/shard_map/ppermute | solution.py:401
  43.4 1.9 %collective-permute-start = (f32[128,1024]{1,0:T(8,128)S(1)}, f32[128,1024]{1,0:T(8,128)}, u32[]{:S(2)}, u32[]{:S(2)}) collective-permute-start(f32[128,1024]{1,0:T(8,128)S(1)} %bitcast.35), channel_id=1, source_target_pairs={{32,0},{64,32},{96,64},{33,1},{65,33},{97,65},{34,2},{66,34},{98,6... | collective-permute-start | bytes 1572872 | tf_op jit(solution)/shard_map/ppermute | solution.py:397
  46.0 0.1 pad_add_fusion.info
  46.1 1.2 collective-permute-done.1.other_w
  47.3 5.6 %forward.1 = (f32[128,1024]{1,0:T(8,128)S(1)}, bf16[2,1536,1024]{2,1,0:T(8,128)(2,1)S(1)}, bf16[2,1024,1024]{2,1,0:T(8,128)(2,1)S(1)}, f32[12,128,1024]{2,1,0:T(8,128)S(1)}) custom-call(s32[3]{0:T(128)S(1)} %pad_add_fusion.info, f32[2,128,1024]{2,1,0:T(8,128)S(1)} %constant_dynamic-update-slice_fusion.given, f32[1,1024]{1,0:T(1,128)S(1)} %bitcast.34, ...), custom_call_target="tpu_custom_call" | custom-call | tf_op jit(solution)/shard_map/forward/pallas_call | solution.py:159
  52.9 1.1 collective-permute-done.following
  54.0 5.2 %backward.1 = (f32[128,1024]{1,0:T(8,128)S(1)}, f32[1,1024]{1,0:T(1,128)S(1)}, bf16[2,2,1536,512]{3,2,1,0:T(8,128)(2,1)S(1)}) custom-call(s32[3]{0:T(128)S(1)} %pad_add_fusion.info, f32[2,128,1024]{2,1,0:T(8,128)S(1)} %constant_dynamic-update-slice_fusion.given, f32[128,1024]{1,0:T(8,128)} %collective-permute-done.following, ...), custom_call_target="tpu_custom_call" | custom-call | tf_op jit(solution)/shard_map/backward/pallas_call | solution.py:183
  59.2 1.8 %fusion = f32[1024,512]{1,0:T(8,128)S(1)} fusion(bf16[2,1536,1024]{2,1,0:T(8,128)(2,1)S(1)} %get-tuple-element.18, bf16[2,2,1536,512]{3,2,1,0:T(8,128)(2,1)S(1)} %get-tuple-element.19), kind=kOutput, calls=%fused_computation | convolution fusion | flops 1610612736 | bytes 6815744 | tf_op jit(solution)/shard_map/dot_general | solution.py:391
  61.0 1.8 %fusion.2 = f32[1024,512]{1,0:T(8,128)S(1)} fusion(bf16[2,1536,1024]{2,1,0:T(8,128)(2,1)S(1)} %get-tuple-element.18, bf16[2,2,1536,512]{3,2,1,0:T(8,128)(2,1)S(1)} %get-tuple-element.19), kind=kOutput, calls=%fused_computation.2 | convolution fusion | flops 1610612736 | bytes 6815744 | tf_op jit(solution)/shard_map/dot_general | solution.py:391
  62.9 10.3 %collective-permute-start.3 = (f32[1024,512]{1,0:T(8,128)S(1)}, f32[1024,512]{1,0:T(8,128)S(1)}, u32[]{:S(2)}, u32[]{:S(2)}) collective-permute-start(f32[1024,512]{1,0:T(8,128)S(1)} %fusion.2), channel_id=1, source_target_pairs={{0,32},{32,0},{1,33},{33,1},{2,34},{34,2},{3,35},{35,3},{4,36},{36... | collective-permute-start | bytes 6291464 | tf_op jit(solution)/shard_map/ppermute | solution.py:401
  73.2 0.1 collective-permute-start.4
  73.3 1.8 %fusion.4.keep_high = f32[1024,512]{1,0:T(8,128)S(1)} fusion(bf16[2,1536,1024]{2,1,0:T(8,128)(2,1)S(1)} %get-tuple-element.18, bf16[2,2,1536,512]{3,2,1,0:T(8,128)(2,1)S(1)} %get-tuple-element.19), kind=kOutput, calls=%fused_computation.4 | convolution fusion | flops 1610612736 | bytes 6815744 | tf_op jit(solution)/shard_map/dot_general | solution.py:391
  75.1 1.8 %fusion.6.keep_low = f32[1024,512]{1,0:T(8,128)S(1)} fusion(bf16[2,1536,1024]{2,1,0:T(8,128)(2,1)S(1)} %get-tuple-element.18, bf16[2,2,1536,512]{3,2,1,0:T(8,128)(2,1)S(1)} %get-tuple-element.19), kind=kOutput, calls=%fused_computation.6 | convolution fusion | flops 1610612736 | bytes 6815744 | tf_op jit(solution)/shard_map/dot_general | solution.py:391
  77.0 0.0 collective-permute-done.3.got_low
  77.0 3.0 %collective-permute-done.4.got_high = f32[1024,512]{1,0:T(8,128)S(1)} collective-permute-done((f32[1024,512]{1,0:T(8,128)S(1)}, f32[1024,512]{1,0:T(8,128)S(1)}, u32[]{:S(2)}, u32[]{:S(2)}) %collective-permute-start.4) | collective-permute-done | bytes 2097184 | tf_op jit(solution)/shard_map/ppermute | solution.py:401
  80.0 2.4 %code.1 = s16[32,264,128]{2,1,0:T(8,128)(2,1)} custom-call(f32[1024,512]{1,0:T(8,128)S(1)} %fusion.6.keep_low, f32[1024,512]{1,0:T(8,128)S(1)} %fusion.4.keep_high, f32[1024,512]{1,0:T(8,128)S(1)} %collective-permute-done.3.got_low, f32[1024,512]{1,0:T(8,128)S(1)} %collective-permute-done.4.got_high, f32[1,1024]{1,0:T(1,128)S(1)} %get-tuple-element.20.bias), custom_call_target="tpu_custom_call" | custom-call | tf_op jit(solution)/shard_map/code/pallas_call | solution.py:276
  82.4 4.1 %all-to-all-start.1 = ((s16[32,264,128]{2,1,0:T(8,128)(2,1)}), s16[32,264,128]{2,1,0:T(8,128)(2,1)S(1)}, u32[]{:S(2)}, u32[]{:S(2)}) async-start(s16[32,264,128]{2,1,0:T(8,128)(2,1)} %code.1), calls=%async_computation.1 | async-start | bytes 4325376 | tf_op jit(solution)/shard_map/all_to_all | solution.py:435
  86.5 3.2 %collective-permute-start.2 = (f32[128,1024]{1,0:T(8,128)S(1)}, f32[128,1024]{1,0:T(8,128)}, u32[]{:S(2)}, u32[]{:S(2)}) collective-permute-start(f32[128,1024]{1,0:T(8,128)S(1)} %get-tuple-element.14.ends), channel_id=1, source_target_pairs={{0,32},{32,64},{64,96},{1,33},{33,65},{65,97},{2,34},{34,66},{66,9... | collective-permute-start | bytes 1572872 | tf_op jit(solution)/shard_map/ppermute | solution.py:397
  89.7 0.1 pad_add_fusion.1.info
  89.8 25.8 %all-to-all-done.1.message = s16[32,264,128]{2,1,0:T(8,128)(2,1)S(1)} async-done(((s16[32,264,128]{2,1,0:T(8,128)(2,1)}), s16[32,264,128]{2,1,0:T(8,128)(2,1)S(1)}, u32[]{:S(2)}, u32[]{:S(2)}) %all-to-all-start.1) | async-done | bytes 2162720 | tf_op jit(solution)/shard_map/all_to_all | solution.py:435
  115.5 0.8 decode.1.mine
  116.3 2.6 %collective-permute-start.7 = (s16[264,128]{1,0:T(8,128)(2,1)S(1)}, s16[264,128]{1,0:T(8,128)(2,1)S(1)}, u32[]{:S(2)}, u32[]{:S(2)}) collective-permute-start(s16[264,128]{1,0:T(8,128)(2,1)S(1)} %decode.1.mine), channel_id=1, source_target_pairs={{0,96},{32,64},{64,32},{96,0},{1,97},{33,65},{65,33},{97,1},{2,98}... | collective-permute-start | bytes 202760 | tf_op jit(solution)/shard_map/ppermute | solution.py:438
  118.9 0.7 collective-permute-start.6
  119.6 2.1 %subtract_bitcast_fusion = f32[1,128,1024]{2,1,0:T(8,128)} fusion(f32[128,1024]{1,0:T(8,128)S(1)} %get-tuple-element.17, f32[128,1024]{1,0:T(8,128)} %collective-permute-done.2, f32[]{:T(128)S(6)} %convert_element_type.4, f32[1,128,1024]{2,1,0:T(8,128)} %param.6), kind=kLoop, calls=%fused_computation.20 | loop fusion | flops 393216 | bytes 2097156 | tf_op jit(solution)/shard_map/broadcast_in_dim | solution.py:426
  121.7 1.3 %collective-permute-done.6.by_zlo = s16[264,128]{1,0:T(8,128)(2,1)S(1)} collective-permute-done((s16[264,128]{1,0:T(8,128)(2,1)S(1)}, s16[264,128]{1,0:T(8,128)(2,1)S(1)}, u32[]{:S(2)}, u32[]{:S(2)}) %collective-permute-start.6) | collective-permute-done | bytes 67616 | tf_op jit(solution)/shard_map/ppermute | solution.py:438
  123.0 1.3 %lay_out.1 = (f32[32,1024]{1,0:T(8,128)}, f32[32,1024]{1,0:T(8,128)}, f32[1,32]{1,0:T(1,128)}) custom-call(s32[2]{0:T(128)S(1)} %pad_add_fusion.1.info, s16[264,128]{1,0:T(8,128)(2,1)S(1)} %decode.1.mine, s16[264,128]{1,0:T(8,128)(2,1)S(1)} %collective-permute-done.5.by_core, s16[264,128]{1,0:T(8,128)(2,1)S(1)} %collective-permute-done.6.by_zlo, ...), custom_call_target="tpu_custom_call" | custom-call | tf_op jit(solution)/shard_map/lay_out/pallas_call | solution.py:380
  (9 shorter events, 0.1 us)
Async XLA Ops:
  1.5 41.9 %copy-start.1 = (f32[1,128,1024]{2,1,0:T(8,128)S(1)}, f32[1,128,1024]{2,1,0:T(8,128)}, u32[]{:S(2)}) copy-start(f32[1,128,1024]{2,1,0:T(8,128)} %param.6) | copy-start | bytes 1572868
  1.8 44.3 %copy-start.2 = (f32[1,128,1024]{2,1,0:T(8,128)S(1)}, f32[1,128,1024]{2,1,0:T(8,128)}, u32[]{:S(2)}) copy-start(f32[1,128,1024]{2,1,0:T(8,128)} %param.7) | copy-start | bytes 1572868
  1.8 45.5 %copy-start = (f32[1024]{0:T(1024)S(1)}, f32[1024]{0:T(1024)}, u32[]{:S(2)}) copy-start(f32[1024]{0:T(1024)} %param.10) | copy-start | bytes 12292
  41.1 6.2 %collective-permute-start.1 = (bf16[1024,1024]{1,0:T(8,128)(2,1)S(1)}, bf16[1024,1024]{1,0:T(8,128)(2,1)}, u32[]{:S(2)}, u32[]{:S(2)}) collective-permute-start(bf16[1024,1024]{1,0:T(8,128)(2,1)S(1)} %bitcast.32), channel_id=1, source_target_pairs={{0,32},{32,0},{1,33},{33,1},{2,34},{34,2},{3,35},{35,3},{4,36},{36... | collective-permute-start | bytes 6291464 | tf_op jit(solution)/shard_map/ppermute | solution.py:401
  43.4 10.6 %collective-permute-start = (f32[128,1024]{1,0:T(8,128)S(1)}, f32[128,1024]{1,0:T(8,128)}, u32[]{:S(2)}, u32[]{:S(2)}) collective-permute-start(f32[128,1024]{1,0:T(8,128)S(1)} %bitcast.35), channel_id=1, source_target_pairs={{32,0},{64,32},{96,64},{33,1},{65,33},{97,65},{34,2},{66,34},{98,6... | collective-permute-start | bytes 1572872 | tf_op jit(solution)/shard_map/ppermute | solution.py:397
  62.9 14.1 %collective-permute-start.3 = (f32[1024,512]{1,0:T(8,128)S(1)}, f32[1024,512]{1,0:T(8,128)S(1)}, u32[]{:S(2)}, u32[]{:S(2)}) collective-permute-start(f32[1024,512]{1,0:T(8,128)S(1)} %fusion.2), channel_id=1, source_target_pairs={{0,32},{32,0},{1,33},{33,1},{2,34},{34,2},{3,35},{35,3},{4,36},{36... | collective-permute-start | bytes 6291464 | tf_op jit(solution)/shard_map/ppermute | solution.py:401
  73.2 6.8 %collective-permute-start.4 = (f32[1024,512]{1,0:T(8,128)S(1)}, f32[1024,512]{1,0:T(8,128)S(1)}, u32[]{:S(2)}, u32[]{:S(2)}) collective-permute-start(f32[1024,512]{1,0:T(8,128)S(1)} %fusion), channel_id=1, source_target_pairs={{0,32},{32,0},{1,33},{33,1},{2,34},{34,2},{3,35},{35,3},{4,36},{36... | collective-permute-start | bytes 6291464 | tf_op jit(solution)/shard_map/ppermute | solution.py:401
  82.4 33.1 %all-to-all-start.1 = ((s16[32,264,128]{2,1,0:T(8,128)(2,1)}), s16[32,264,128]{2,1,0:T(8,128)(2,1)S(1)}, u32[]{:S(2)}, u32[]{:S(2)}) async-start(s16[32,264,128]{2,1,0:T(8,128)(2,1)} %code.1), calls=%async_computation.1 | async-start | bytes 4325376 | tf_op jit(solution)/shard_map/all_to_all | solution.py:435
  86.5 33.1 %collective-permute-start.2 = (f32[128,1024]{1,0:T(8,128)S(1)}, f32[128,1024]{1,0:T(8,128)}, u32[]{:S(2)}, u32[]{:S(2)}) collective-permute-start(f32[128,1024]{1,0:T(8,128)S(1)} %get-tuple-element.14.ends), channel_id=1, source_target_pairs={{0,32},{32,64},{64,96},{1,33},{33,65},{65,97},{2,34},{34,66},{66,9... | collective-permute-start | bytes 1572872 | tf_op jit(solution)/shard_map/ppermute | solution.py:397
  116.3 5.4 %collective-permute-start.7 = (s16[264,128]{1,0:T(8,128)(2,1)S(1)}, s16[264,128]{1,0:T(8,128)(2,1)S(1)}, u32[]{:S(2)}, u32[]{:S(2)}) collective-permute-start(s16[264,128]{1,0:T(8,128)(2,1)S(1)} %decode.1.mine), channel_id=1, source_target_pairs={{0,96},{32,64},{64,32},{96,0},{1,97},{33,65},{65,33},{97,1},{2,98}... | collective-permute-start | bytes 202760 | tf_op jit(solution)/shard_map/ppermute | solution.py:438
  118.9 4.1 %collective-permute-start.6 = (s16[264,128]{1,0:T(8,128)(2,1)S(1)}, s16[264,128]{1,0:T(8,128)(2,1)S(1)}, u32[]{:S(2)}, u32[]{:S(2)}) collective-permute-start(s16[264,128]{1,0:T(8,128)(2,1)S(1)} %decode.1.mine), channel_id=1, source_target_pairs={{0,64},{32,96},{64,0},{96,32},{1,65},{33,97},{65,1},{97,33},{2,66}... | collective-permute-start | bytes 202760 | tf_op jit(solution)/shard_map/ppermute | solution.py:438
  119.6 3.4 %collective-permute-start.5 = (s16[264,128]{1,0:T(8,128)(2,1)S(1)}, s16[264,128]{1,0:T(8,128)(2,1)S(1)}, u32[]{:S(2)}, u32[]{:S(2)}) collective-permute-start(s16[264,128]{1,0:T(8,128)(2,1)S(1)} %decode.1.mine), channel_id=1, source_target_pairs={{0,32},{32,0},{64,96},{96,64},{1,33},{33,1},{65,97},{97,65},{2,34}... | collective-permute-start | bytes 202760 | tf_op jit(solution)/shard_map/ppermute | solution.py:438

commit v8 on v7

--- a/solution.py
+++ b/solution.py
@@ -387,6 +387,54 @@
     )(info, *quarters)
 
 
+def shrink_kernel(values, out):
+    rows, width = values.shape
+    columns = [pl.ds(at, LANES) for at in range(0, width, LANES)]
+    loads = [functools.partial(lambda c: values[:, c], c) for c in columns]
+    middle = len(loads) // 2
+
+    def store(block, numbers):
+        out[pl.ds(block * rows, rows), :] = numbers
+
+    def store_head(numbers):
+        out[pl.ds(2 * middle * rows, HEAD), :] = numbers
+
+    code_piece(loads[:middle], loads[middle:], (), store, store_head)
+
+
+def shrink(values):
+    rows, width = values.shape
+    return pl.pallas_call(
+        shrink_kernel,
+        out_shape=jax.ShapeDtypeStruct((rows * width // LANES + HEAD, LANES), jnp.int16),
+        in_specs=[VMEM],
+        out_specs=VMEM,
+        compiler_params=pltpu.CompilerParams(vmem_limit_bytes=8 * 1024 * 1024),
+        name="shrink",
+    )(values)
+
+
+def finish_kernel(info, bar, message, start, out):
+    has_prev = info[0].astype(f32)
+    blocks = blocks_of(message.shape[0], out.shape[1] // LANES)
+    values, _ = read_piece(blocks, lambda at, rows: message[pl.ds(at, rows), :])
+    for block, previous in enumerate(values):
+        columns = pl.ds(block * LANES, LANES)
+        gap = (previous - start[:, columns]) * has_prev
+        out[:, columns] = bar[:, columns] - penalty * gap
+
+
+def finish(info, bar, message, start):
+    return pl.pallas_call(
+        finish_kernel,
+        out_shape=jax.ShapeDtypeStruct(bar.shape, f32),
+        in_specs=[SMEM] + [VMEM] * 3,
+        out_specs=VMEM,
+        compiler_params=pltpu.CompilerParams(vmem_limit_bytes=8 * 1024 * 1024),
+        name="finish",
+    )(info, bar, message, start)
+
+
 def contract_rows(left, right):
     return lax.dot_general(left, right, (((0,), (0,)), ((), ())), preferred_element_type=f32)
 
@@ -421,9 +469,10 @@
     info = jnp.stack([counts[0], core, has_next])
     ends, left, w_turned, tanhs = forward(info, given, b_in[None], own_w, other_w)
     bar, bias, right = backward(info, given, pltpu.with_memory_space_constraint(following, pltpu.HBM), ends, w_turned, tanhs)
-    previous = shift_seg(ends, 1)
-    has_prev = (place > 0).astype(f32)
-    grad_starts = (bar - penalty * ((previous - start) * has_prev))[None]
+    small = shrink(ends)
+    previous = shift_seg(small, 1)
+    has_prev = (place > 0).astype(jnp.int32)
+    grad_starts = finish(has_prev[None], bar, previous, start)[None]
 
     received, keep = [], []
     for half in range(2):

time: 126 us -> 126 us (level)
  other arithmetic: 3.11 us -> 1.01 us
    broadcast_in_dim x1 -> x0, other arithmetic: 2.09 us -> none  [body(): grad_starts = (bar - penalty * ((previous - start) * has_prev))[None]]
  transfers between devices with their start and end apart: 9 -> 9, of which waited for: 5 -> 5; matrix products, arithmetic and copies ran while one was open for 5% -> 3% of each run, Pallas kernels for 5% -> 6%
where the time goes in v8:
time: 126 us; the launch traced here: 124 us
  blocking collectives  39.3 us (31%)
  waiting for transfers between devices  32.4 us (26%)
  starting transfers between devices  25.2 us (20%)
  Pallas kernels  16.4 us (13%)
  matrix products  7.36 us (6%)
  between operations  1.46 us (1%)
  local copies, waits for them, and re-layouts  1.39 us (1%)
    all_to_all x1, blocking collectives, body(): own_w = lax.all_to_all(copies, 'batch', 0, 0)  39.3 us
    all_to_all x1, waiting for transfers between devices, body(): message = lax.all_to_all(message, 'batch', 0, 0)  25.7 us
    ppermute x3, starting transfers between devices, swap(): return lax.ppermute(block, 'core', [(0, 1), (1, 0)])  12.7 us
    dot_general x4, matrix products, contract_rows(): lax.dot_general(left, right, (((0,), (0,)), ((), ())), preferred_element_...  7.36 us
    pallas_call x1, Pallas kernels, forward(): pl.pallas_call(forward_kernel, out_shape=(jax.ShapeDtypeStruct((rows, wid...  5.59 us
    pallas_call x1, Pallas kernels, backward(): pl.pallas_call(backward_kernel, out_shape=(jax.ShapeDtypeStruct((rows, wi...  5.12 us
    ppermute x2, starting transfers between devices, shift_seg(): return lax.ppermute(block, SEG, route)  5.1 us
    ppermute x3, waiting for transfers between devices, swap(): return lax.ppermute(block, 'core', [(0, 1), (1, 0)])  4.18 us
  transfers between devices with their start and end apart: 9, of which 5 were waited for; matrix products, arithmetic and copies ran while one was open for 3% of the time, Pallas kernels for 6%

profile of v8, /device:TPU:1, one launch (start us, length us, event | category | flops | bytes accessed | tf_op | source)
XLA Modules:
  0.0 124.5 jit_solution(3920196849191431216)
XLA Ops:
  0.6 0.9 broadcast_select_fusion
  1.5 0.0 copy-start
  1.5 0.2 broadcast_in_dim.20
  1.8 39.3 %all_to_all.10 = bf16[32,32,1024]{2,1,0:T(8,128)(2,1)S(1)} all-to-all(bf16[32,32,1024]{2,1,0:T(8,128)(2,1)S(1)} %broadcast_in_dim.20), channel_id=1, replica_groups=mesh['zlo'=2,'core'=2,'batch'=32] {'batch'}, dimensions={0} | all-to-all | bytes 4194304 | tf_op jit(solution)/shard_map/all_to_all | solution.py:463
  41.1 2.3 %collective-permute-start.1 = (bf16[1024,1024]{1,0:T(8,128)(2,1)S(1)}, bf16[1024,1024]{1,0:T(8,128)(2,1)}, u32[]{:S(2)}, u32[]{:S(2)}) collective-permute-start(bf16[1024,1024]{1,0:T(8,128)(2,1)S(1)} %bitcast.31), channel_id=1, source_target_pairs={{0,32},{32,0},{1,33},{33,1},{2,34},{34,2},{3,35},{35,3},{4,36},{36... | collective-permute-start | bytes 6291464 | tf_op jit(solution)/shard_map/ppermute | solution.py:449
  43.4 1.9 %collective-permute-start = (f32[128,1024]{1,0:T(8,128)S(1)}, f32[128,1024]{1,0:T(8,128)}, u32[]{:S(2)}, u32[]{:S(2)}) collective-permute-start(f32[128,1024]{1,0:T(8,128)S(1)} %bitcast.33), channel_id=1, source_target_pairs={{32,0},{64,32},{96,64},{33,1},{65,33},{97,65},{34,2},{66,34},{98,6... | collective-permute-start | bytes 1572872 | tf_op jit(solution)/shard_map/ppermute | solution.py:445
  46.0 0.1 pad_add_fusion.info
  46.1 1.2 collective-permute-done.1.other_w
  47.3 5.6 %forward.1 = (f32[128,1024]{1,0:T(8,128)S(1)}, bf16[2,1536,1024]{2,1,0:T(8,128)(2,1)S(1)}, bf16[2,1024,1024]{2,1,0:T(8,128)(2,1)S(1)}, f32[12,128,1024]{2,1,0:T(8,128)S(1)}) custom-call(s32[3]{0:T(128)S(1)} %pad_add_fusion.info, f32[2,128,1024]{2,1,0:T(8,128)S(1)} %constant_dynamic-update-slice_fusion.given, f32[1,1024]{1,0:T(1,128)S(1)} %bitcast.35, ...), custom_call_target="tpu_custom_call" | custom-call | tf_op jit(solution)/shard_map/forward/pallas_call | solution.py:159
  52.9 1.1 collective-permute-done.following
  54.0 5.1 %backward.1 = (f32[128,1024]{1,0:T(8,128)S(1)}, f32[1,1024]{1,0:T(1,128)S(1)}, bf16[2,2,1536,512]{3,2,1,0:T(8,128)(2,1)S(1)}) custom-call(s32[3]{0:T(128)S(1)} %pad_add_fusion.info, f32[2,128,1024]{2,1,0:T(8,128)S(1)} %constant_dynamic-update-slice_fusion.given, f32[128,1024]{1,0:T(8,128)} %collective-permute-done.following, ...), custom_call_target="tpu_custom_call" | custom-call | tf_op jit(solution)/shard_map/backward/pallas_call | solution.py:183
  59.1 1.8 %fusion = f32[1024,512]{1,0:T(8,128)S(1)} fusion(bf16[2,1536,1024]{2,1,0:T(8,128)(2,1)S(1)} %get-tuple-element.18, bf16[2,2,1536,512]{3,2,1,0:T(8,128)(2,1)S(1)} %get-tuple-element.19), kind=kOutput, calls=%fused_computation | convolution fusion | flops 1610612736 | bytes 6815744 | tf_op jit(solution)/shard_map/dot_general | solution.py:439
  61.0 1.8 %fusion.2 = f32[1024,512]{1,0:T(8,128)S(1)} fusion(bf16[2,1536,1024]{2,1,0:T(8,128)(2,1)S(1)} %get-tuple-element.18, bf16[2,2,1536,512]{3,2,1,0:T(8,128)(2,1)S(1)} %get-tuple-element.19), kind=kOutput, calls=%fused_computation.2 | convolution fusion | flops 1610612736 | bytes 6815744 | tf_op jit(solution)/shard_map/dot_general | solution.py:439
  62.8 10.3 %collective-permute-start.3 = (f32[1024,512]{1,0:T(8,128)S(1)}, f32[1024,512]{1,0:T(8,128)S(1)}, u32[]{:S(2)}, u32[]{:S(2)}) collective-permute-start(f32[1024,512]{1,0:T(8,128)S(1)} %fusion.2), channel_id=1, source_target_pairs={{0,32},{32,0},{1,33},{33,1},{2,34},{34,2},{3,35},{35,3},{4,36},{36... | collective-permute-start | bytes 6291464 | tf_op jit(solution)/shard_map/ppermute | solution.py:449
  73.1 0.1 collective-permute-start.4
  73.2 1.8 %fusion.4.keep_high = f32[1024,512]{1,0:T(8,128)S(1)} fusion(bf16[2,1536,1024]{2,1,0:T(8,128)(2,1)S(1)} %get-tuple-element.18, bf16[2,2,1536,512]{3,2,1,0:T(8,128)(2,1)S(1)} %get-tuple-element.19), kind=kOutput, calls=%fused_computation.4 | convolution fusion | flops 1610612736 | bytes 6815744 | tf_op jit(solution)/shard_map/dot_general | solution.py:439
  75.1 1.8 %fusion.6.keep_low = f32[1024,512]{1,0:T(8,128)S(1)} fusion(bf16[2,1536,1024]{2,1,0:T(8,128)(2,1)S(1)} %get-tuple-element.18, bf16[2,2,1536,512]{3,2,1,0:T(8,128)(2,1)S(1)} %get-tuple-element.19), kind=kOutput, calls=%fused_computation.6 | convolution fusion | flops 1610612736 | bytes 6815744 | tf_op jit(solution)/shard_map/dot_general | solution.py:439
  76.9 0.0 collective-permute-done.3.got_low
  76.9 3.0 %collective-permute-done.4.got_high = f32[1024,512]{1,0:T(8,128)S(1)} collective-permute-done((f32[1024,512]{1,0:T(8,128)S(1)}, f32[1024,512]{1,0:T(8,128)S(1)}, u32[]{:S(2)}, u32[]{:S(2)}) %collective-permute-start.4) | collective-permute-done | bytes 2097184 | tf_op jit(solution)/shard_map/ppermute | solution.py:449
  79.9 2.6 %code.1 = s16[32,264,128]{2,1,0:T(8,128)(2,1)} custom-call(f32[1024,512]{1,0:T(8,128)S(1)} %fusion.6.keep_low, f32[1024,512]{1,0:T(8,128)S(1)} %fusion.4.keep_high, f32[1024,512]{1,0:T(8,128)S(1)} %collective-permute-done.3.got_low, f32[1024,512]{1,0:T(8,128)S(1)} %collective-permute-done.4.got_high, f32[1,1024]{1,0:T(1,128)S(1)} %get-tuple-element.20.bias), custom_call_target="tpu_custom_call" | custom-call | tf_op jit(solution)/shard_map/code/pallas_call | solution.py:276
  82.5 4.1 %all-to-all-start.1 = ((s16[32,264,128]{2,1,0:T(8,128)(2,1)}), s16[32,264,128]{2,1,0:T(8,128)(2,1)S(1)}, u32[]{:S(2)}, u32[]{:S(2)}) async-start(s16[32,264,128]{2,1,0:T(8,128)(2,1)} %code.1), calls=%async_computation.1 | async-start | bytes 4325376 | tf_op jit(solution)/shard_map/all_to_all | solution.py:484
  86.6 0.1 shrink.1
  86.7 3.2 %collective-permute-start.2 = (s16[1032,128]{1,0:T(8,128)(2,1)S(1)}, s16[1032,128]{1,0:T(8,128)(2,1)S(1)}, u32[]{:S(2)}, u32[]{:S(2)}) collective-permute-start(s16[1032,128]{1,0:T(8,128)(2,1)S(1)} %shrink.1), channel_id=1, source_target_pairs={{0,32},{32,64},{64,96},{1,33},{33,65},{65,97},{2,34},{34,66},{66,9... | collective-permute-start | bytes 792584 | tf_op jit(solution)/shard_map/ppermute | solution.py:445
  89.9 25.7 %all-to-all-done.1.message = s16[32,264,128]{2,1,0:T(8,128)(2,1)S(1)} async-done(((s16[32,264,128]{2,1,0:T(8,128)(2,1)}), s16[32,264,128]{2,1,0:T(8,128)(2,1)S(1)}, u32[]{:S(2)}, u32[]{:S(2)}) %all-to-all-start.1) | async-done | bytes 2162720 | tf_op jit(solution)/shard_map/all_to_all | solution.py:484
  115.7 0.8 decode.1.mine
  116.4 2.6 %collective-permute-start.7 = (s16[264,128]{1,0:T(8,128)(2,1)S(1)}, s16[264,128]{1,0:T(8,128)(2,1)S(1)}, u32[]{:S(2)}, u32[]{:S(2)}) collective-permute-start(s16[264,128]{1,0:T(8,128)(2,1)S(1)} %decode.1.mine), channel_id=1, source_target_pairs={{0,96},{32,64},{64,32},{96,0},{1,97},{33,65},{65,33},{97,1},{2,98}... | collective-permute-start | bytes 202760 | tf_op jit(solution)/shard_map/ppermute | solution.py:487
  119.0 0.7 collective-permute-start.6
  119.8 0.1 pad_add_fusion.1.info
  119.8 1.0 copy-done.2
  120.9 0.9 finish.1
  121.8 1.4 %collective-permute-done.6.by_zlo = s16[264,128]{1,0:T(8,128)(2,1)S(1)} collective-permute-done((s16[264,128]{1,0:T(8,128)(2,1)S(1)}, s16[264,128]{1,0:T(8,128)(2,1)S(1)}, u32[]{:S(2)}, u32[]{:S(2)}) %collective-permute-start.6) | collective-permute-done | bytes 67616 | tf_op jit(solution)/shard_map/ppermute | solution.py:487
  123.2 1.3 %lay_out.1 = (f32[32,1024]{1,0:T(8,128)}, f32[32,1024]{1,0:T(8,128)}, f32[1,32]{1,0:T(1,128)}) custom-call(s32[2]{0:T(128)S(1)} %pad_add_fusion.1.info, s16[264,128]{1,0:T(8,128)(2,1)S(1)} %decode.1.mine, s16[264,128]{1,0:T(8,128)(2,1)S(1)} %collective-permute-done.5.by_core, s16[264,128]{1,0:T(8,128)(2,1)S(1)} %collective-permute-done.6.by_zlo, ...), custom_call_target="tpu_custom_call" | custom-call | tf_op jit(solution)/shard_map/lay_out/pallas_call | solution.py:380
  (14 shorter events, 0.1 us)
Async XLA Ops:
  1.5 41.9 %copy-start = (f32[1,128,1024]{2,1,0:T(8,128)S(1)}, f32[1,128,1024]{2,1,0:T(8,128)}, u32[]{:S(2)}) copy-start(f32[1,128,1024]{2,1,0:T(8,128)} %param.6) | copy-start | bytes 1572868
  1.8 44.3 %copy-start.4 = (f32[1,128,1024]{2,1,0:T(8,128)S(1)}, f32[1,128,1024]{2,1,0:T(8,128)}, u32[]{:S(2)}) copy-start(f32[1,128,1024]{2,1,0:T(8,128)} %param.7) | copy-start | bytes 1572868
  1.8 45.5 %copy-start.3 = (f32[1024]{0:T(1024)S(1)}, f32[1024]{0:T(1024)}, u32[]{:S(2)}) copy-start(f32[1024]{0:T(1024)} %param.10) | copy-start | bytes 12292
  41.1 6.2 %collective-permute-start.1 = (bf16[1024,1024]{1,0:T(8,128)(2,1)S(1)}, bf16[1024,1024]{1,0:T(8,128)(2,1)}, u32[]{:S(2)}, u32[]{:S(2)}) collective-permute-start(bf16[1024,1024]{1,0:T(8,128)(2,1)S(1)} %bitcast.31), channel_id=1, source_target_pairs={{0,32},{32,0},{1,33},{33,1},{2,34},{34,2},{3,35},{35,3},{4,36},{36... | collective-permute-start | bytes 6291464 | tf_op jit(solution)/shard_map/ppermute | solution.py:449
  43.4 10.6 %collective-permute-start = (f32[128,1024]{1,0:T(8,128)S(1)}, f32[128,1024]{1,0:T(8,128)}, u32[]{:S(2)}, u32[]{:S(2)}) collective-permute-start(f32[128,1024]{1,0:T(8,128)S(1)} %bitcast.33), channel_id=1, source_target_pairs={{32,0},{64,32},{96,64},{33,1},{65,33},{97,65},{34,2},{66,34},{98,6... | collective-permute-start | bytes 1572872 | tf_op jit(solution)/shard_map/ppermute | solution.py:445
  59.1 1.9 %copy-start.1 = (f32[128,1024]{1,0:T(8,128)}, f32[128,1024]{1,0:T(8,128)S(1)}, u32[]{:S(2)}) copy-start(f32[128,1024]{1,0:T(8,128)S(1)} %get-tuple-element.17.bar) | copy-start | bytes 1572868
  62.8 14.1 %collective-permute-start.3 = (f32[1024,512]{1,0:T(8,128)S(1)}, f32[1024,512]{1,0:T(8,128)S(1)}, u32[]{:S(2)}, u32[]{:S(2)}) collective-permute-start(f32[1024,512]{1,0:T(8,128)S(1)} %fusion.2), channel_id=1, source_target_pairs={{0,32},{32,0},{1,33},{33,1},{2,34},{34,2},{3,35},{35,3},{4,36},{36... | collective-permute-start | bytes 6291464 | tf_op jit(solution)/shard_map/ppermute | solution.py:449
  73.1 6.8 %collective-permute-start.4 = (f32[1024,512]{1,0:T(8,128)S(1)}, f32[1024,512]{1,0:T(8,128)S(1)}, u32[]{:S(2)}, u32[]{:S(2)}) collective-permute-start(f32[1024,512]{1,0:T(8,128)S(1)} %fusion), channel_id=1, source_target_pairs={{0,32},{32,0},{1,33},{33,1},{2,34},{34,2},{3,35},{35,3},{4,36},{36... | collective-permute-start | bytes 6291464 | tf_op jit(solution)/shard_map/ppermute | solution.py:449
  82.5 33.1 %all-to-all-start.1 = ((s16[32,264,128]{2,1,0:T(8,128)(2,1)}), s16[32,264,128]{2,1,0:T(8,128)(2,1)S(1)}, u32[]{:S(2)}, u32[]{:S(2)}) async-start(s16[32,264,128]{2,1,0:T(8,128)(2,1)} %code.1), calls=%async_computation.1 | async-start | bytes 4325376 | tf_op jit(solution)/shard_map/all_to_all | solution.py:484
  86.7 33.1 %collective-permute-start.2 = (s16[1032,128]{1,0:T(8,128)(2,1)S(1)}, s16[1032,128]{1,0:T(8,128)(2,1)S(1)}, u32[]{:S(2)}, u32[]{:S(2)}) collective-permute-start(s16[1032,128]{1,0:T(8,128)(2,1)S(1)} %shrink.1), channel_id=1, source_target_pairs={{0,32},{32,64},{64,96},{1,33},{33,65},{65,97},{2,34},{34,66},{66,9... | collective-permute-start | bytes 792584 | tf_op jit(solution)/shard_map/ppermute | solution.py:445
  116.4 5.3 %collective-permute-start.7 = (s16[264,128]{1,0:T(8,128)(2,1)S(1)}, s16[264,128]{1,0:T(8,128)(2,1)S(1)}, u32[]{:S(2)}, u32[]{:S(2)}) collective-permute-start(s16[264,128]{1,0:T(8,128)(2,1)S(1)} %decode.1.mine), channel_id=1, source_target_pairs={{0,96},{32,64},{64,32},{96,0},{1,97},{33,65},{65,33},{97,1},{2,98}... | collective-permute-start | bytes 202760 | tf_op jit(solution)/shard_map/ppermute | solution.py:487
  119.0 4.1 %collective-permute-start.6 = (s16[264,128]{1,0:T(8,128)(2,1)S(1)}, s16[264,128]{1,0:T(8,128)(2,1)S(1)}, u32[]{:S(2)}, u32[]{:S(2)}) collective-permute-start(s16[264,128]{1,0:T(8,128)(2,1)S(1)} %decode.1.mine), channel_id=1, source_target_pairs={{0,64},{32,96},{64,0},{96,32},{1,65},{33,97},{65,1},{97,33},{2,66}... | collective-permute-start | bytes 202760 | tf_op jit(solution)/shard_map/ppermute | solution.py:487
  119.7 3.4 %collective-permute-start.5 = (s16[264,128]{1,0:T(8,128)(2,1)S(1)}, s16[264,128]{1,0:T(8,128)(2,1)S(1)}, u32[]{:S(2)}, u32[]{:S(2)}) collective-permute-start(s16[264,128]{1,0:T(8,128)(2,1)S(1)} %decode.1.mine), channel_id=1, source_target_pairs={{0,32},{32,0},{64,96},{96,64},{1,33},{33,1},{65,97},{97,65},{2,34}... | collective-permute-start | bytes 202760 | tf_op jit(solution)/shard_map/ppermute | solution.py:487
  119.8 1.0 copy-start.2
